TPU v7x, 32 devices: a whole 2x2x4 slice. The times are simulated.
32 devices in a mesh: dp: 8 (over y, x, core), seq: 4 (over z).
Axes of the slice: x: 2, y: 2, z: 4, core: 2. Of those that a mesh axis runs over, the one named last changes fastest.
Arguments:
- hidden_in: bfloat16 [8, 2048, 2048], P('dp', 'seq'), may hold values from -6 to 6
- memory: bfloat16 [8, 2048, 2048], P('dp', 'seq'), may hold values from -6 to 6
- segments: int32 [8, 2048], P('dp'), may hold values from 0 to 3, never falling along the last dimension, each value on 1 to 1200 neighbouring positions
- gain_attn: bfloat16 [2048], P(('dp', 'seq')), may hold values from 0.25 to 1.75
- w_query: bfloat16 [2048, 2048], P(('dp', 'seq')), may hold values from -0.125 to 0.125
- w_key: bfloat16 [2048, 2048], P(('dp', 'seq')), may hold values from -0.125 to 0.125
- w_value: bfloat16 [2048, 2048], P(('dp', 'seq')), may hold values from -0.125 to 0.125
- w_out: bfloat16 [2048, 2048], P(('dp', 'seq')), may hold values from -0.75 to 0.75
- gain_ffn: bfloat16 [2048], P(('dp', 'seq')), may hold values from 0.25 to 1.75
- w_gate: bfloat16 [5504, 2048], P(('dp', 'seq')), may hold values from -0.125 to 0.125
- w_up: bfloat16 [5504, 2048], P(('dp', 'seq')), may hold values from -0.125 to 0.125
- w_down: bfloat16 [5504, 2048], P(('dp', 'seq')), may hold values from -0.078125 to 0.078125
- cotangent: bfloat16 [8, 2048, 2048], P('dp', 'seq'), may hold values from -6 to 6
Outputs:
- layer_out: bfloat16 [8, 2048, 2048], P('dp', 'seq')
- grad_hidden: float32 [8, 2048, 2048], P('dp', 'seq')
- grad_memory: float32 [8, 2048, 2048], P('dp', 'seq')
- grad_gain_attn: float32 [2048], P(('dp', 'seq'))
- grad_w_query: float32 [2048, 2048], P(('dp', 'seq'))
- grad_w_key: float32 [2048, 2048], P(('dp', 'seq'))
- grad_w_value: float32 [2048, 2048], P(('dp', 'seq'))
- grad_w_out: float32 [2048, 2048], P(('dp', 'seq'))
- grad_gain_ffn: float32 [2048], P(('dp', 'seq'))
- grad_w_gate: float32 [5504, 2048], P(('dp', 'seq'))
- grad_w_up: float32 [5504, 2048], P(('dp', 'seq'))
- grad_w_down: float32 [5504, 2048], P(('dp', 'seq'))
Inputs may be any that keep to these rules, and one draw needn't show every extreme that they name: `segments`: along each sequence the numbers never fall; each number is held by 1 to 1200 consecutive tokens, and in every draw some document has exactly 1200.
All inputs are finite; a program needn't handle non-finite values.
Results may differ from a plain program's by a relative error of at most 0.019.
Values may be sent and summed in bfloat16 or wider, within the bound.
A program may use at most 384 MiB of HBM per device.

v0:
```python
import jax
import jax.numpy as jnp
from jax import lax
from jax.sharding import PartitionSpec as P

HEAD_DIM = 128


EPSILON = 1e-06
MASKED = -1e30


def rms_scale(values):
    return lax.rsqrt(jnp.mean(values * values, axis=-1, keepdims=True) + EPSILON)


def norm_back(grad_normed, normed, rstd, gain):
    scaled = grad_normed * gain
    return rstd * (scaled - normed * jnp.mean(scaled * normed, axis=-1, keepdims=True))


def visible(segment_ids, start, rows):
    length = segment_ids.shape[0]
    query_pos = start + lax.broadcasted_iota(jnp.int32, (rows, length), 0)
    key_pos = lax.broadcasted_iota(jnp.int32, (rows, length), 1)
    query_segment = lax.dynamic_slice_in_dim(segment_ids, start, rows)
    return (key_pos <= query_pos) & (query_segment[:, None] == segment_ids[None, :])


def block_scores(query_block, keys, segment_ids, start):
    rows = query_block.shape[0]
    scale = query_block.shape[2] ** (-0.5)
    score = (
        jnp.einsum("qhd,khd->hqk", query_block, keys, preferred_element_type=jnp.float32) * scale
    )
    return jnp.where(visible(segment_ids, start, rows)[None], score, MASKED)


def attend_forward(query, key, value, segment_ids):
    length, heads, width = query.shape
    rows = min(512, length)

    def one_block(index):
        start = index * rows
        query_block = lax.dynamic_slice_in_dim(query, start, rows, 0)
        score = block_scores(query_block, key, segment_ids, start)
        top = jnp.max(score, axis=-1, keepdims=True)
        raised = jnp.exp(score - top)
        total = jnp.sum(raised, axis=-1, keepdims=True)
        prob_low = (raised / total).astype(jnp.bfloat16)
        context = jnp.einsum("hqk,khd->qhd", prob_low, value, preferred_element_type=jnp.float32)
        return (context.astype(jnp.bfloat16), (top + jnp.log(total))[..., 0])

    context, logsum = lax.map(one_block, jnp.arange(length // rows, dtype=jnp.int32))
    return (context.reshape(length, heads * width), logsum)


def attend_backward(query, key, value, segment_ids, logsum, grad_context):
    length, heads, width = query.shape
    rows = min(512, length)
    scale = width ** (-0.5)

    def one_block(carry, index):
        grad_key, grad_value = carry
        start = index * rows
        query_block = lax.dynamic_slice_in_dim(query, start, rows, 0)
        grad_block = lax.dynamic_slice_in_dim(grad_context, start, rows, 0)
        score = block_scores(query_block, key, segment_ids, start)
        prob = jnp.exp(score - logsum[index][..., None])
        grad_value = grad_value + jnp.einsum(
            "hqk,qhd->khd",
            prob.astype(jnp.bfloat16),
            grad_block,
            preferred_element_type=jnp.float32,
        )
        grad_prob = jnp.einsum(
            "qhd,khd->hqk", grad_block, value, preferred_element_type=jnp.float32
        )
        grad_score = (
            prob * (grad_prob - jnp.sum(prob * grad_prob, axis=-1, keepdims=True))
        ).astype(jnp.bfloat16)
        grad_query = (
            jnp.einsum("hqk,khd->qhd", grad_score, key, preferred_element_type=jnp.float32) * scale
        )
        grad_key = (
            grad_key
            + jnp.einsum(
                "hqk,qhd->khd", grad_score, query_block, preferred_element_type=jnp.float32
            )
            * scale
        )
        return ((grad_key, grad_value), grad_query.astype(jnp.bfloat16))

    zeros = jnp.zeros((length, heads, width), jnp.float32)
    (grad_key, grad_value), grad_query = lax.scan(
        one_block, (zeros, zeros), jnp.arange(length // rows, dtype=jnp.int32)
    )
    flat = (length, heads * width)
    return (
        grad_query.reshape(flat),
        grad_key.astype(jnp.bfloat16).reshape(flat),
        grad_value.astype(jnp.bfloat16).reshape(flat),
    )


def row_terms(left, right, blocks, share):
    term = jnp.einsum("tk,td->kd", left, right, preferred_element_type=jnp.float32)
    return term.reshape(blocks, share, right.shape[1])


def gain_terms(vector, blocks):
    return jnp.broadcast_to(vector[None, None, :], (blocks, 1, vector.shape[0]))


def shards(
    hidden_in,
    memory,
    segments,
    gain_attn,
    w_query,
    w_key,
    w_value,
    w_out,
    gain_ffn,
    w_gate,
    w_up,
    w_down,
    cotangent,
):
    seqs, piece, width = hidden_in.shape
    groups = lax.axis_size("seq")
    dp_count = lax.axis_size("dp")
    length = piece * groups
    heads_here = width // groups // HEAD_DIM
    count = seqs * piece
    share_d = w_query.shape[0]
    share_f = w_gate.shape[0]
    tokens = hidden_in.reshape(count, width)
    memory_flat = memory.reshape(count, width)
    grad_out = cotangent.reshape(count, width)
    hidden32 = tokens.astype(jnp.float32)
    rstd_in = rms_scale(hidden32)
    normed_in = hidden32 * rstd_in
    gain_piece = lax.all_gather(gain_attn, ("dp", "seq"), axis=0, tiled=True)
    query_rows = lax.all_gather(w_query, ("dp", "seq"), axis=0, tiled=True)
    key_rows = lax.all_gather(w_key, ("dp", "seq"), axis=0, tiled=True)
    value_rows = lax.all_gather(w_value, ("dp", "seq"), axis=0, tiled=True)
    gain32 = gain_piece.astype(jnp.float32)
    columns = (normed_in * gain32).astype(jnp.bfloat16)
    query = jnp.dot(columns, query_rows, preferred_element_type=jnp.float32)
    key = jnp.dot(memory_flat, key_rows, preferred_element_type=jnp.float32)
    value = jnp.dot(memory_flat, value_rows, preferred_element_type=jnp.float32)
    attn_in = columns
    query, key, value, attn_in, gain_attn_full = (query, key, value, attn_in, gain32)
    cube = (seqs, piece, width)
    query_heads, key_heads, value_heads = (
        lax.all_to_all(
            query.astype(jnp.bfloat16).reshape(cube), "seq", split_axis=2, concat_axis=1, tiled=True
        ),
        lax.all_to_all(
            key.astype(jnp.bfloat16).reshape(cube), "seq", split_axis=2, concat_axis=1, tiled=True
        ),
        lax.all_to_all(
            value.astype(jnp.bfloat16).reshape(cube), "seq", split_axis=2, concat_axis=1, tiled=True
        ),
    )
    head_shape = (length, heads_here, HEAD_DIM)

    def forward_one(item):
        query_seq, key_seq, value_seq, segment_ids = item
        return attend_forward(
            query_seq.reshape(head_shape),
            key_seq.reshape(head_shape),
            value_seq.reshape(head_shape),
            segment_ids,
        )

    context_heads, logsum = lax.map(forward_one, (query_heads, key_heads, value_heads, segments))
    context = lax.all_to_all(context_heads, "seq", split_axis=1, concat_axis=2, tiled=True).reshape(
        count, width
    )
    out_full, gain_ffn_full = (
        lax.all_gather(w_out, ("dp", "seq"), axis=0, tiled=True),
        lax.all_gather(gain_ffn, ("dp", "seq"), axis=0, tiled=True),
    )
    mid = hidden32 + jnp.dot(context, out_full, preferred_element_type=jnp.float32)
    rstd_mid = rms_scale(mid)
    normed_mid = mid * rstd_mid
    gain_ffn32 = gain_ffn_full.astype(jnp.float32)
    ffn_in = (normed_mid * gain_ffn32).astype(jnp.bfloat16)
    gate_rows, up_rows = lax.all_gather((w_gate, w_up), ("dp", "seq"), axis=0, tiled=True)
    gate_part = jnp.einsum("td,fd->tf", ffn_in, gate_rows, preferred_element_type=jnp.float32)
    up_part = jnp.einsum("td,fd->tf", ffn_in, up_rows, preferred_element_type=jnp.float32)
    both = jnp.stack((gate_part, up_part))
    gate = both[0]
    up = both[1]
    gate_sigmoid = jax.nn.sigmoid(gate)
    act = (gate * gate_sigmoid * up).astype(jnp.bfloat16)
    columns = act
    branch = jnp.dot(
        columns,
        lax.all_gather(w_down, ("dp", "seq"), axis=0, tiled=True),
        preferred_element_type=jnp.float32,
    )
    layer_out = (mid + branch).astype(jnp.bfloat16).reshape(cube)
    grad_act = jnp.einsum(
        "td,fd->tf",
        grad_out,
        lax.all_gather(w_down, ("dp", "seq"), axis=0, tiled=True),
        preferred_element_type=jnp.float32,
    )
    grad_gate = (grad_act * up * gate_sigmoid * (1.0 + gate * (1.0 - gate_sigmoid))).astype(
        jnp.bfloat16
    )
    grad_up = (grad_act * gate * gate_sigmoid).astype(jnp.bfloat16)
    gate_rows = lax.all_gather(w_gate, ("dp", "seq"), axis=0, tiled=True)
    up_rows = lax.all_gather(w_up, ("dp", "seq"), axis=0, tiled=True)
    total = jnp.dot(grad_gate, gate_rows, preferred_element_type=jnp.float32)
    grad_ffn_in = total + jnp.dot(grad_up, up_rows, preferred_element_type=jnp.float32)
    grad_gain_ffn_all = jnp.sum(normed_mid * grad_ffn_in, axis=0)
    grad_mid = grad_out.astype(jnp.float32) + norm_back(
        grad_ffn_in, normed_mid, rstd_mid, gain_ffn32
    )
    grad_branch = grad_mid.astype(jnp.bfloat16)
    grad_context = jnp.einsum(
        "td,ed->te", grad_branch, out_full, preferred_element_type=jnp.float32
    ).astype(jnp.bfloat16)
    grad_context_heads = lax.all_to_all(
        grad_context.reshape(cube), "seq", split_axis=2, concat_axis=1, tiled=True
    )

    def backward_one(item):
        query_seq, key_seq, value_seq, segment_ids, logsum_seq, grad_seq = item
        return attend_backward(
            query_seq.reshape(head_shape),
            key_seq.reshape(head_shape),
            value_seq.reshape(head_shape),
            segment_ids,
            logsum_seq,
            grad_seq.reshape(head_shape),
        )

    grad_query_heads, grad_key_heads, grad_value_heads = lax.map(
        backward_one, (query_heads, key_heads, value_heads, segments, logsum, grad_context_heads)
    )
    grad_query, grad_key, grad_value = (
        lax.all_to_all(grad_query_heads, "seq", split_axis=1, concat_axis=2, tiled=True),
        lax.all_to_all(grad_key_heads, "seq", split_axis=1, concat_axis=2, tiled=True),
        lax.all_to_all(grad_value_heads, "seq", split_axis=1, concat_axis=2, tiled=True),
    )
    grad_query = grad_query.reshape(count, width)
    grad_key = grad_key.reshape(count, width)
    grad_value = grad_value.reshape(count, width)
    query_rows, key_rows, value_rows = lax.all_gather(
        (w_query, w_key, w_value), ("dp", "seq"), axis=0, tiled=True
    )
    grad_in = jnp.einsum("te,de->td", grad_query, query_rows, preferred_element_type=jnp.float32)
    grad_memory_part = jnp.einsum(
        "te,de->td", grad_key, key_rows, preferred_element_type=jnp.float32
    )
    grad_memory_part = grad_memory_part + jnp.einsum(
        "te,de->td", grad_value, value_rows, preferred_element_type=jnp.float32
    )
    both_grads = jnp.stack((grad_in, grad_memory_part))
    grad_attn_in = both_grads[0]
    grad_memory = both_grads[1].reshape(cube)
    grad_gain_attn_all = jnp.sum(normed_in * grad_attn_in, axis=0)
    grad_hidden = (grad_mid + norm_back(grad_attn_in, normed_in, rstd_in, gain_attn_full)).reshape(
        cube
    )
    gain_attn_group, gain_ffn_group = lax.psum((grad_gain_attn_all, grad_gain_ffn_all), "seq")

    def regroup(values):
        return values.reshape(count, dp_count, groups, values.shape[1] // (dp_count * groups))

    left_parts = (
        lax.all_to_all(regroup(attn_in), "seq", split_axis=2, concat_axis=0, tiled=True),
        lax.all_to_all(regroup(memory_flat), "seq", split_axis=2, concat_axis=0, tiled=True),
        lax.all_to_all(regroup(context), "seq", split_axis=2, concat_axis=0, tiled=True),
        lax.all_to_all(regroup(grad_gate), "seq", split_axis=2, concat_axis=0, tiled=True),
        lax.all_to_all(regroup(grad_up), "seq", split_axis=2, concat_axis=0, tiled=True),
        lax.all_to_all(regroup(act), "seq", split_axis=2, concat_axis=0, tiled=True),
    )
    whole_count = count * groups
    attn_left, memory_left, context_left, gate_left, up_left, act_left = [
        part.reshape(whole_count, part.shape[1] * part.shape[3]) for part in left_parts
    ]
    query_right, key_right, value_right, branch_right, ffn_right, out_right = (
        lax.all_gather(grad_query, "seq", axis=0, tiled=True),
        lax.all_gather(grad_key, "seq", axis=0, tiled=True),
        lax.all_gather(grad_value, "seq", axis=0, tiled=True),
        lax.all_gather(grad_branch, "seq", axis=0, tiled=True),
        lax.all_gather(ffn_in, "seq", axis=0, tiled=True),
        lax.all_gather(grad_out, "seq", axis=0, tiled=True),
    )
    attn_block = 4 * share_d + 1
    ffn_block = 3 * share_f + 1
    whole_block = attn_block + ffn_block
    blocks = whole_block * lax.axis_size("dp") // whole_block
    all_grads = lax.psum_scatter(
        jnp.concatenate(
            [
                row_terms(attn_left, query_right, blocks, share_d),
                row_terms(memory_left, key_right, blocks, share_d),
                row_terms(memory_left, value_right, blocks, share_d),
                row_terms(context_left, branch_right, blocks, share_d),
                gain_terms(gain_attn_group, blocks),
            ]
            + [
                row_terms(gate_left, ffn_right, blocks, share_f),
                row_terms(up_left, ffn_right, blocks, share_f),
                row_terms(act_left, out_right, blocks, share_f),
                gain_terms(gain_ffn_group, blocks),
            ],
            axis=1,
        )
        .reshape(whole_block * lax.axis_size("dp"), width)
        .astype(jnp.bfloat16),
        "dp",
        scatter_dimension=0,
        tiled=True,
    ).astype(jnp.float32)
    attn_grads = all_grads[:attn_block]
    ffn_grads = all_grads[attn_block:]
    owner = lax.axis_index("dp") * groups + lax.axis_index("seq")
    grad_w_query = attn_grads[0:share_d]
    grad_w_key = attn_grads[share_d : 2 * share_d]
    grad_w_value = attn_grads[2 * share_d : 3 * share_d]
    grad_w_out = attn_grads[3 * share_d : 4 * share_d]
    grad_gain_attn = lax.dynamic_slice_in_dim(attn_grads[4 * share_d], owner * share_d, share_d)
    grad_w_gate = ffn_grads[0:share_f]
    grad_w_up = ffn_grads[share_f : 2 * share_f]
    grad_w_down = ffn_grads[2 * share_f : 3 * share_f]
    grad_gain_ffn = lax.dynamic_slice_in_dim(ffn_grads[3 * share_f], owner * share_d, share_d)
    return (
        layer_out,
        grad_hidden,
        grad_memory,
        grad_gain_attn,
        grad_w_query,
        grad_w_key,
        grad_w_value,
        grad_w_out,
        grad_gain_ffn,
        grad_w_gate,
        grad_w_up,
        grad_w_down,
    )


def solution(mesh):
    in_specs = (
        P("dp", "seq", None),
        P("dp", "seq", None),
        P("dp", None),
        P(("dp", "seq")),
        P(("dp", "seq"), None),
        P(("dp", "seq"), None),
        P(("dp", "seq"), None),
        P(("dp", "seq"), None),
        P(("dp", "seq")),
        P(("dp", "seq"), None),
        P(("dp", "seq"), None),
        P(("dp", "seq"), None),
        P("dp", "seq", None),
    )
    out_specs = (
        P("dp", "seq", None),
        P("dp", "seq", None),
        P("dp", "seq", None),
        P(("dp", "seq")),
        P(("dp", "seq"), None),
        P(("dp", "seq"), None),
        P(("dp", "seq"), None),
        P(("dp", "seq"), None),
        P(("dp", "seq")),
        P(("dp", "seq"), None),
        P(("dp", "seq"), None),
        P(("dp", "seq"), None),
    )
    return jax.shard_map(shards, mesh=mesh, in_specs=in_specs, out_specs=out_specs, check_vma=False)
```

profile of v0, /device:TPU:0, one launch (start us, length us, event | category | flops | bytes accessed | tf_op | source)
XLA Modules:
  0.0 3069.1 jit_solution(8761035630606516971)
XLA Ops:
  13.6 42.4 %all-reduce.5 = (bf16[2048]{0:T(1024)(128)(2,1)S(1)}, bf16[2048]{0:T(1024)(128)(2,1)}) all-reduce(bf16[2048]{0:T(1024)(128)(2,1)S(1)} %dynamic-update-slice, bf16[2048]{0:T(1024)(128)(2,1)S(1)} %dynamic-update-slice.1), channel_id=1, replica_groups=mesh['dp'=8,'seq'=4] {'dp','seq'}, use_global_device_ids=true, to_apply=%add | all-reduce | flops 4096 | bytes 16384
  57.1 34.2 %all-gather.18.cloned.1.call-done = bf16[2048,2048]{1,0:T(8,128)(2,1)} async-done(((bf16[64,2048]{1,0:T(8,128)(2,1)}), bf16[2048,2048]{1,0:T(8,128)(2,1)}) %all-gather.18.cloned.1.call-update) | async-done | bytes 8388624 | tf_op jit(solution)/shard_map/all_gather | solution.py:145
  132.4 63.3 %all-gather.20.cloned.1.call-done = bf16[2048,2048]{1,0:T(8,128)(2,1)} async-done(((bf16[64,2048]{1,0:T(8,128)(2,1)}), bf16[2048,2048]{1,0:T(8,128)(2,1)}) %all-gather.20.cloned.1.call-update) | async-done | bytes 8388624 | tf_op jit(solution)/shard_map/all_gather | solution.py:146
  245.4 63.2 %all-gather.22.cloned.1.call-done = bf16[2048,2048]{1,0:T(8,128)(2,1)} async-done(((bf16[64,2048]{1,0:T(8,128)(2,1)}), bf16[2048,2048]{1,0:T(8,128)(2,1)}) %all-gather.22.cloned.1.call-update) | async-done | bytes 8388624 | tf_op jit(solution)/shard_map/all_gather | solution.py:147
  385.5 42.8 %all-to-all-done.2 = bf16[4,2,131072]{2,1,0:T(2,128)(2,1)} async-done(((bf16[4,2,131072]{2,1,0:T(2,128)(2,1)}), bf16[4,2,131072]{2,1,0:T(2,128)(2,1)}, u32[]{:S(2)}, u32[]{:S(2)}) %all-to-all-start.2) | async-done | bytes 2097184 | tf_op jit(solution)/shard_map/all_to_all | solution.py:163
  450.9 74.5 %while.47 = (s32[]{:T(128)}, bf16[4,512,4,128]{3,2,1,0:T(4,128)(2,1)}, f32[4,4,512]{2,1,0:T(4,128)}, s32[4]{0:T(128)S(1)}, s32[2048]{0:T(1024)S(1)}, /*index=5*/...) while((s32[]{:T(128)}, ...), condition=%wide.region_4.5_spmd, body=%wide.region_1.4_spmd.sunk | while | flops 2201221632 | bytes 69291224 | solution.py:54
  562.3 65.8 %all-to-all-done.3 = bf16[4,2,131072]{2,1,0:T(2,128)(2,1)S(1)} async-done(((bf16[4,2,131072]{2,1,0:T(2,128)(2,1)}), bf16[4,2,131072]{2,1,0:T(2,128)(2,1)S(1)}, u32[]{:S(2)}, u32[]{:S(2)}) %all-to-all-start.3) | async-done | bytes 2097184 | tf_op jit(solution)/shard_map/all_to_all | solution.py:179
  663.9 22.7 reshape.356
  686.6 19.1 fusion.72
  705.7 70.9 %all-gather.40.cloned.1.call-done = bf16[32,172,2048]{2,1,0:T(8,128)(2,1)} async-done(((bf16[1,172,2048]{2,1,0:T(8,128)(2,1)}), bf16[32,172,2048]{2,1,0:T(8,128)(2,1)}) %all-gather.40.cloned.1.call-update) | async-done | bytes 22544400 | tf_op jit(solution)/shard_map/all_gather | solution.py:191
  776.6 22.2 reshape.358
  798.8 19.1 fusion.73
  817.9 104.3 %all-gather.42.cloned.1.call-done = bf16[32,172,2048]{2,1,0:T(8,128)(2,1)} async-done(((bf16[1,172,2048]{2,1,0:T(8,128)(2,1)}), bf16[32,172,2048]{2,1,0:T(8,128)(2,1)}) %all-gather.42.cloned.1.call-update) | async-done | bytes 22544400 | tf_op jit(solution)/shard_map/all_gather | solution.py:202
  922.2 22.4 reshape.360
  944.7 26.8 multiply_convert_fusion.1
  971.5 19.6 fusion.74
  991.1 21.8 multiply_reduce_fusion.1
  1062.0 88.2 %all-to-all-done.4 = bf16[4,2,131072]{2,1,0:T(2,128)(2,1)S(1)} async-done(((bf16[4,2,131072]{2,1,0:T(2,128)(2,1)}), bf16[4,2,131072]{2,1,0:T(2,128)(2,1)S(1)}, u32[]{:S(2)}, u32[]{:S(2)}) %all-to-all-start.4) | async-done | bytes 2097184 | tf_op jit(solution)/shard_map/all_to_all | solution.py:228
  1170.4 83.9 %all-to-all-done.9 = bf16[512,8,4,64]{0,3,1,2:T(8,128)(2,1)} async-done(((bf16[512,8,4,64]{0,3,1,2:T(8,128)(2,1)}), bf16[512,8,4,64]{0,3,1,2:T(8,128)(2,1)}, u32[]{:S(2)}, u32[]{:S(2)}) %all-to-all-start.9) | async-done | bytes 2097184 | tf_op jit(solution)/shard_map/all_to_all | solution.py:278
  1260.6 274.6 %while.48 = (s32[]{:T(128)}, f32[2048,4,128]{0,2,1:T(8,128)}, f32[2048,4,128]{0,2,1:T(8,128)}, bf16[4,512,4,128]{3,2,1,0:T(4,128)(2,1)}, s32[4]{0:T(128)S(1)}, /...) while((s32[]{:T(128)}, f32[2048,4,128]{0,2,1:T(8,128)}, ...), condition=%wide.region_9.10_spmd.clone, body=%wide.region_7.9_spmd.clone.sunk | while | flops 5440535040 | bytes 193538896 | solution.py:95
  1653.6 54.0 %all-to-all-done.5 = bf16[4,2,131072]{2,1,0:T(2,128)(2,1)} async-done(((bf16[4,2,131072]{2,1,0:T(2,128)(2,1)}), bf16[4,2,131072]{2,1,0:T(2,128)(2,1)}, u32[]{:S(2)}, u32[]{:S(2)}) %all-to-all-start.5) | async-done | bytes 2097184 | tf_op jit(solution)/shard_map/all_to_all | solution.py:247
  1711.6 29.0 reshape.365
  1755.2 56.0 %all-to-all-done.7 = bf16[4,2,131072]{2,1,0:T(2,128)(2,1)S(1)} async-done(((bf16[4,2,131072]{2,1,0:T(2,128)(2,1)}), bf16[4,2,131072]{2,1,0:T(2,128)(2,1)S(1)}, u32[]{:S(2)}, u32[]{:S(2)}) %all-to-all-start.7) | async-done | bytes 2097184 | tf_op jit(solution)/shard_map/all_to_all | solution.py:249
  1824.9 29.1 reshape.366
  1868.5 158.7 %all-to-all-done.11 = bf16[512,8,4,172]{0,1,3,2:T(8,128)(2,1)} async-done(((bf16[512,8,4,172]{0,1,3,2:T(8,128)(2,1)}), bf16[512,8,4,172]{0,1,3,2:T(8,128)(2,1)}, u32[]{:S(2)}, u32[]{:S(2)}) %all-to-all-start.11) | async-done | bytes 5636128 | tf_op jit(solution)/shard_map/all_to_all | solution.py:280
  2032.5 29.1 reshape.367
  2076.1 146.4 %all-to-all-done.12 = bf16[512,8,4,172]{0,1,3,2:T(8,128)(2,1)} async-done(((bf16[512,8,4,172]{0,1,3,2:T(8,128)(2,1)}), bf16[512,8,4,172]{0,1,3,2:T(8,128)(2,1)}, u32[]{:S(2)}, u32[]{:S(2)}) %all-to-all-start.12) | async-done | bytes 5636128 | tf_op jit(solution)/shard_map/all_to_all | solution.py:281
  2285.1 162.8 %all-reduce.4 = (bf16[2048]{0:T(1024)(128)(2,1)S(1)}, bf16[2048]{0:T(1024)(128)(2,1)S(1)}) all-reduce(f32[2048]{0:T(1024)S(1)} %get-tuple-element.284, f32[2048]{0:T(1024)S(1)} %copy-done.35), channel_id=1, replica_groups=mesh['dp'=8,'seq'=4] {'seq'}, use_global_device_ids=true, to_apply=%region_12.13 | all-reduce | flops 4096 | bytes 24576 | tf_op jit(solution)/shard_map/psum | solution.py:271
  2519.7 18.4 fusion.41
  2610.5 143.7 %concatenate.4 = bf16[8,774,2048]{2,1,0:T(8,128)(2,1)} concatenate(bf16[8,64,2048]{2,1,0:T(8,128)(2,1)} %fusion.51, bf16[8,64,2048]{2,1,0:T(8,128)(2,1)} %bitcast.343, bf16[8,64,2048]{2,1,0:T(8,128)(2,1)} %bitcast.344, bf16[8,64,2048]{2,1,0:T(8,128)(2,1)S(1)} %fusion.54, bf16[8,1,2048]{2,1,0:T(2,128)(2,1)S(1)} %broadcast_in_dim.83, bf16[8,172,2048]{2,1,0:T(8,128)(2,1)} %fusion.41, ...), dimensions={1} | concatenate | bytes 50724864 | tf_op jit(solution)/shard_map/concatenate | solution.py:301
  2754.2 25.0 convert_element_type.114
  2779.2 250.9 %fusion = bf16[784,2048]{1,0:T(8,128)(2,1)} fusion(bf16[6192,2048]{1,0:T(8,128)(2,1)} %convert_element_type.114), kind=kCustom, calls=%all-reduce-scatter | all-reduce-scatter fusion | flops 12845057 | bytes 28574208
  (375 shorter events, 1103.4 us)
Async XLA Ops:
  7.2 84.1 %all-gather.18.cloned.1.call-start = ((), (), s32[]{:S(2)}) async-start(), calls=%async_computation.14 | async-start | bytes 8650752 | tf_op jit(solution)/shard_map/all_gather | solution.py:145
  7.9 187.8 %all-gather.20.cloned.1.call-start = ((), (), s32[]{:S(2)}) async-start(), calls=%async_computation.15 | async-start | bytes 8650752 | tf_op jit(solution)/shard_map/all_gather | solution.py:146
  8.7 299.9 %all-gather.22.cloned.1.call-start = ((), (), s32[]{:S(2)}) async-start(), calls=%async_computation.16 | async-start | bytes 8650752 | tf_op jit(solution)/shard_map/all_gather | solution.py:147
  9.4 630.4 %all-gather.24.cloned.1.call-start = ((), (), s32[]{:S(2)}) async-start(), calls=%async_computation.17 | async-start | bytes 8650752 | tf_op jit(solution)/shard_map/all_gather | solution.py:183
  10.0 653.9 %all-gather.38.cloned.1.call-start = ((), (), s32[]{:S(2)}) async-start(), calls=%async_computation.24 | async-start | bytes 23789568 | tf_op jit(solution)/shard_map/all_gather | solution.py:191
  10.6 766.0 %all-gather.40.cloned.1.call-start = ((), (), s32[]{:S(2)}) async-start(), calls=%async_computation.25 | async-start | bytes 23789568 | tf_op jit(solution)/shard_map/all_gather | solution.py:191
  11.1 911.1 %all-gather.42.cloned.1.call-start = ((), (), s32[]{:S(2)}) async-start(), calls=%async_computation.26 | async-start | bytes 23789568 | tf_op jit(solution)/shard_map/all_gather | solution.py:202
  128.6 107.6 %all-to-all-start = ((bf16[4,2,131072]{2,1,0:T(2,128)(2,1)}), bf16[4,2,131072]{2,1,0:T(2,128)(2,1)S(1)}, u32[]{:S(2)}, u32[]{:S(2)}) async-start(bf16[4,2,131072]{2,1,0:T(2,128)(2,1)} %reshape.369), calls=%async_computation | async-start | bytes 4194304 | tf_op jit(solution)/shard_map/all_to_all | solution.py:157
  236.2 112.8 %all-to-all-start.1 = ((bf16[4,2,131072]{2,1,0:T(2,128)(2,1)}), bf16[4,2,131072]{2,1,0:T(2,128)(2,1)}, u32[]{:S(2)}, u32[]{:S(2)}) async-start(bf16[4,2,131072]{2,1,0:T(2,128)(2,1)} %reshape.371), calls=%async_computation.1 | async-start | bytes 4194304 | tf_op jit(solution)/shard_map/all_to_all | solution.py:160
  349.0 79.2 %all-to-all-start.2 = ((bf16[4,2,131072]{2,1,0:T(2,128)(2,1)}), bf16[4,2,131072]{2,1,0:T(2,128)(2,1)}, u32[]{:S(2)}, u32[]{:S(2)}) async-start(bf16[4,2,131072]{2,1,0:T(2,128)(2,1)} %reshape.373), calls=%async_computation.2 | async-start | bytes 4194304 | tf_op jit(solution)/shard_map/all_to_all | solution.py:163
  558.6 69.5 %all-to-all-start.3 = ((bf16[4,2,131072]{2,1,0:T(2,128)(2,1)}), bf16[4,2,131072]{2,1,0:T(2,128)(2,1)S(1)}, u32[]{:S(2)}, u32[]{:S(2)}) async-start(bf16[4,2,131072]{2,1,0:T(2,128)(2,1)} %reshape.375), calls=%async_computation.3 | async-start | bytes 4194304 | tf_op jit(solution)/shard_map/all_to_all | solution.py:179
  562.2 1957.4 %all-gather.34.cloned.1.call-start = ((), (), s32[]{:S(2)}) async-start(), calls=%async_computation.22 | async-start | bytes 10485760 | tf_op jit(solution)/shard_map/all_gather | solution.py:293
  658.7 392.7 %all-to-all-start.8 = ((bf16[512,8,4,64]{0,3,1,2:T(8,128)(2,1)}), bf16[512,8,4,64]{0,3,1,2:T(8,128)(2,1)}, u32[]{:S(2)}, u32[]{:S(2)}) async-start(bf16[512,8,4,64]{0,3,1,2:T(8,128)(2,1)} %copy.157), calls=%async_computation.8 | async-start | bytes 4194304 | tf_op jit(solution)/shard_map/all_to_all | solution.py:277
  663.1 1890.8 %all-gather.36.cloned.1.call-start = ((), (), s32[]{:S(2)}) async-start(), calls=%async_computation.23 | async-start | bytes 10485760 | tf_op jit(solution)/shard_map/all_gather | solution.py:294
  1051.3 98.9 %all-to-all-start.4 = ((bf16[4,2,131072]{2,1,0:T(2,128)(2,1)}), bf16[4,2,131072]{2,1,0:T(2,128)(2,1)S(1)}, u32[]{:S(2)}, u32[]{:S(2)}) async-start(bf16[4,2,131072]{2,1,0:T(2,128)(2,1)} %reshape.377), calls=%async_computation.4 | async-start | bytes 4194304 | tf_op jit(solution)/shard_map/all_to_all | solution.py:228
  1150.2 104.1 %all-to-all-start.9 = ((bf16[512,8,4,64]{0,3,1,2:T(8,128)(2,1)}), bf16[512,8,4,64]{0,3,1,2:T(8,128)(2,1)}, u32[]{:S(2)}, u32[]{:S(2)}) async-start(bf16[512,8,4,64]{0,3,1,2:T(8,128)(2,1)} %copy.160), calls=%async_computation.9 | async-start | bytes 4194304 | tf_op jit(solution)/shard_map/all_to_all | solution.py:278
  1154.7 1417.3 %all-gather.32.cloned.1.call-start = ((), (), s32[]{:S(2)}) async-start(), calls=%async_computation.21 | async-start | bytes 10485760 | tf_op jit(solution)/shard_map/all_gather | solution.py:292
  1254.3 307.9 %all-to-all-start.10 = ((bf16[512,8,4,64]{0,3,1,2:T(8,128)(2,1)}), bf16[512,8,4,64]{0,3,1,2:T(8,128)(2,1)}, u32[]{:S(2)}, u32[]{:S(2)}) async-start(bf16[512,8,4,64]{0,3,1,2:T(8,128)(2,1)} %copy.163), calls=%async_computation.10 | async-start | bytes 4194304 | tf_op jit(solution)/shard_map/all_to_all | solution.py:279
  1562.2 51.5 %all-to-all-start.6 = ((bf16[4,2,131072]{2,1,0:T(2,128)(2,1)}), bf16[4,2,131072]{2,1,0:T(2,128)(2,1)S(1)}, u32[]{:S(2)}, u32[]{:S(2)}) async-start(bf16[4,2,131072]{2,1,0:T(2,128)(2,1)} %reshape.381), calls=%async_computation.6 | async-start | bytes 4194304 | tf_op jit(solution)/shard_map/all_to_all | solution.py:248
  1613.7 94.0 %all-to-all-start.5 = ((bf16[4,2,131072]{2,1,0:T(2,128)(2,1)}), bf16[4,2,131072]{2,1,0:T(2,128)(2,1)}, u32[]{:S(2)}, u32[]{:S(2)}) async-start(bf16[4,2,131072]{2,1,0:T(2,128)(2,1)} %reshape.379), calls=%async_computation.5 | async-start | bytes 4194304 | tf_op jit(solution)/shard_map/all_to_all | solution.py:247
  1618.1 962.4 %all-gather.28.cloned.1.call-start = ((), (), s32[]{:S(2)}) async-start(), calls=%async_computation.19 | async-start | bytes 10485760 | tf_op jit(solution)/shard_map/all_gather | solution.py:290
  1707.6 103.6 %all-to-all-start.7 = ((bf16[4,2,131072]{2,1,0:T(2,128)(2,1)}), bf16[4,2,131072]{2,1,0:T(2,128)(2,1)S(1)}, u32[]{:S(2)}, u32[]{:S(2)}) async-start(bf16[4,2,131072]{2,1,0:T(2,128)(2,1)} %reshape.383), calls=%async_computation.7 | async-start | bytes 4194304 | tf_op jit(solution)/shard_map/all_to_all | solution.py:249
  1811.2 215.9 %all-to-all-start.11 = ((bf16[512,8,4,172]{0,1,3,2:T(8,128)(2,1)}), bf16[512,8,4,172]{0,1,3,2:T(8,128)(2,1)}, u32[]{:S(2)}, u32[]{:S(2)}) async-start(bf16[512,8,4,172]{0,1,3,2:T(8,128)(2,1)} %copy.166), calls=%async_computation.11 | async-start | bytes 11272192 | tf_op jit(solution)/shard_map/all_to_all | solution.py:280
  1816.4 774.1 %all-gather.30.cloned.1.call-start = ((), (), s32[]{:S(2)}) async-start(), calls=%async_computation.20 | async-start | bytes 10485760 | tf_op jit(solution)/shard_map/all_gather | solution.py:291
  2027.2 195.3 %all-to-all-start.12 = ((bf16[512,8,4,172]{0,1,3,2:T(8,128)(2,1)}), bf16[512,8,4,172]{0,1,3,2:T(8,128)(2,1)}, u32[]{:S(2)}, u32[]{:S(2)}) async-start(bf16[512,8,4,172]{0,1,3,2:T(8,128)(2,1)} %copy.169), calls=%async_computation.12 | async-start | bytes 11272192 | tf_op jit(solution)/shard_map/all_to_all | solution.py:281
  2222.5 279.4 %all-to-all-start.13 = ((bf16[512,8,4,172]{0,1,3,2:T(8,128)(2,1)}), bf16[512,8,4,172]{0,1,3,2:T(8,128)(2,1)}, u32[]{:S(2)}, u32[]{:S(2)}) async-start(bf16[512,8,4,172]{0,1,3,2:T(8,128)(2,1)} %copy.172), calls=%async_computation.13 | async-start | bytes 11272192 | tf_op jit(solution)/shard_map/all_to_all | solution.py:282
  2227.6 372.6 %all-gather.26.cloned.1.call-start = ((), (), s32[]{:S(2)}) async-start(), calls=%async_computation.18 | async-start | bytes 10485760 | tf_op jit(solution)/shard_map/all_gather | solution.py:289
  2779.2 254.0 %copy-start.19 = (f32[2048]{0:T(1024)S(1)}, f32[2048]{0:T(1024)}, u32[]{:S(2)}) copy-start(f32[2048]{0:T(1024)} %copy-done.17) | copy-start | bytes 24580
  2779.2 254.0 %copy-start.22 = (f32[512]{0:T(512)S(1)}, f32[512]{0:T(512)}, u32[]{:S(2)}) copy-start(f32[512]{0:T(512)} %copy-done.20) | copy-start | bytes 6148
  2779.2 254.0 %copy-start.25 = (f32[2048]{0:T(1024)S(1)}, f32[2048]{0:T(1024)}, u32[]{:S(2)}) copy-start(f32[2048]{0:T(1024)} %copy-done.23) | copy-start | bytes 24580
  2779.2 254.0 %copy-start.29 = (f32[512]{0:T(512)S(1)}, f32[512]{0:T(512)}, u32[]{:S(2)}) copy-start(f32[512]{0:T(512)} %copy-done.26) | copy-start | bytes 6148
  3031.1 9.9 collective-permute-start
  (46 other events, 1721.4 us)
Sparse Core Ops, SparseCore 0:
  11.0 80.3 all-gather.17
  94.2 101.4 all-gather.19
  198.7 109.8 all-gather.21
  311.3 108.5 all-gather.23
  422.7 161.4 all-gather.37
  586.9 189.6 all-gather.39
  779.4 142.7 all-gather.41
  923.8 165.6 all-gather.33
  1091.0 250.4 all-gather.35
  1343.0 147.7 all-gather.31
  1626.8 306.7 all-gather.27
  1935.0 272.3 all-gather.29
  2274.3 213.2 all-gather.25
where the time goes:
time: 3090 us; the launch traced here: 3070 us
  waiting for transfers between devices  1050 us (34%)
  local copies, waits for them, and re-layouts  720 us (23%)
  matrix products  509 us (16%)
  blocking collectives  456 us (15%)
  other arithmetic  231 us (7%)
  starting transfers between devices  72.7 us (2%)
    unnamed x2, blocking collectives  293 us
    unnamed x119, local copies, waits for them, and re-layouts  203 us
    psum x1, blocking collectives, shards(): lax.psum((grad_gain_attn_all, grad_gain_ffn_all), 'seq')  163 us
    all_to_all x1, waiting for transfers between devices, shards(): lax.all_to_all(regroup(grad_gate), 'seq', split_axis=2, concat_axis=0, ti...  159 us
    all_to_all x1, waiting for transfers between devices, shards(): lax.all_to_all(regroup(grad_up), 'seq', split_axis=2, concat_axis=0, tile...  146 us
    concatenate x1, local copies, waits for them, and re-layouts, shards(): jnp.concatenate([row_terms(attn_left, query_right, blocks, share_d), row_...  144 us
    reshape x6, local copies, waits for them, and re-layouts, regroup(): values.reshape(count, dp_count, groups, values.shape[1] // (dp_count * gr...  131 us
    unnamed x11, other arithmetic  118 us
  transfers between devices with their start and end apart: 28, of which 14 were waited for; matrix products, arithmetic and copies ran while one was open for 41% of the time, Pallas kernels for 0%

commit v1 on v0

v1 whole, which is shorter than its diff:
```python
import functools
import math

import jax
import jax.numpy as jnp
from jax import lax
from jax.experimental import pallas as pl
from jax.experimental.pallas import tpu as pltpu
from jax.sharding import PartitionSpec as P

HEAD_DIM = 128
EPSILON = 1e-06
MASKED = -1e30
ALL = ("dp", "seq")
F32 = jnp.float32
BF16 = jnp.bfloat16
EXP2_SCALE = HEAD_DIM ** (-0.5) * math.log2(math.e)
NT = (((1,), (1,)), ((), ()))
TN = (((0,), (0,)), ((), ()))
NN = (((1,), (0,)), ((), ()))


def mxu(left, right, dims):
    return lax.dot_general(left, right, dims, preferred_element_type=F32)


def rms_scale(values):
    return lax.rsqrt(jnp.mean(values * values, axis=-1, keepdims=True) + EPSILON)


def norm_back(grad_normed, normed, rstd, gain):
    scaled = grad_normed * gain
    return rstd * (scaled - normed * jnp.mean(scaled * normed, axis=-1, keepdims=True))


def forward_kernel(block, low_ref, start_ref, q_ref, k_ref, v_ref, out_ref, lse_ref):
    length = q_ref.shape[0]

    def one_query_block(qb, _):
        q0 = pl.multiple_of(qb * block, block)
        rows = pl.ds(q0, block)
        query = q_ref[rows, :]
        start = start_ref[:, rows]
        query_pos = q0 + lax.broadcasted_iota(jnp.int32, (block, block), 1)

        def one_key_block(kb, carry):
            top, total, acc = carry
            k0 = pl.multiple_of(kb * block, block)
            keys = pl.ds(k0, block)
            score = mxu(k_ref[keys, :], query, NT)
            key_pos = k0 + lax.broadcasted_iota(jnp.int32, (block, block), 0)
            score = jnp.where((key_pos >= start) & (key_pos <= query_pos), score, MASKED)
            new_top = jnp.maximum(top, jnp.max(score, axis=0, keepdims=True))
            shrink = jnp.exp2((top - new_top) * EXP2_SCALE)
            raised = jnp.exp2((score - new_top) * EXP2_SCALE)
            total = total * shrink + jnp.sum(raised, axis=0, keepdims=True)
            acc = acc * shrink + mxu(v_ref[keys, :], raised.astype(BF16), TN)
            return new_top, total, acc

        top, total, acc = lax.fori_loop(
            low_ref[qb],
            qb + 1,
            one_key_block,
            (
                jnp.full((1, block), MASKED, F32),
                jnp.zeros((1, block), F32),
                jnp.zeros((HEAD_DIM, block), F32),
            ),
        )
        out_ref[rows, :] = (acc / total).T.astype(BF16)
        lse_ref[0, :, rows] = top * EXP2_SCALE + jnp.log2(total)
        return 0

    lax.fori_loop(0, length // block, one_query_block, 0)


def backward_kernel(
    block, high_ref, start_ref, q_ref, k_ref, v_ref, ctx_ref, grad_ref, lse_ref,
    dq_ref, dk_ref, dv_ref, dq_acc, delta_acc,
):
    length = q_ref.shape[0]
    blocks = length // block
    scale = HEAD_DIM ** (-0.5)
    dq_acc[...] = jnp.zeros_like(dq_acc)

    def one_delta(qb, _):
        rows = pl.ds(pl.multiple_of(qb * block, block), block)
        both = ctx_ref[rows, :].astype(F32) * grad_ref[rows, :].astype(F32)
        delta_acc[:, rows] = jnp.sum(both.T, axis=0, keepdims=True)
        return 0

    lax.fori_loop(0, blocks, one_delta, 0)

    def one_key_block(kb, _):
        k0 = pl.multiple_of(kb * block, block)
        keys = pl.ds(k0, block)
        key = k_ref[keys, :]
        value = v_ref[keys, :]
        key_pos = k0 + lax.broadcasted_iota(jnp.int32, (block, block), 0)

        def one_query_block(qb, carry):
            dk, dv = carry
            q0 = pl.multiple_of(qb * block, block)
            rows = pl.ds(q0, block)
            query = q_ref[rows, :]
            grad = grad_ref[rows, :]
            start = start_ref[:, rows]
            query_pos = q0 + lax.broadcasted_iota(jnp.int32, (block, block), 1)
            score = mxu(key, query, NT)
            prob = jnp.exp2(score * EXP2_SCALE - lse_ref[0, :, rows])
            prob = jnp.where((key_pos >= start) & (key_pos <= query_pos), prob, 0.0)
            grad_prob = mxu(value, grad, NT)
            grad_score = (prob * (grad_prob - delta_acc[:, rows])).astype(BF16)
            dv = dv + mxu(prob.astype(BF16), grad, NN)
            dk = dk + mxu(grad_score, query, NN)
            dq_acc[rows, :] += mxu(grad_score, key, TN)
            return dk, dv

        zeros = jnp.zeros((block, HEAD_DIM), F32)
        dk, dv = lax.fori_loop(kb, high_ref[kb], one_query_block, (zeros, zeros))
        dk_ref[keys, :] = (dk * scale).astype(BF16)
        dv_ref[keys, :] = dv.astype(BF16)
        return 0

    lax.fori_loop(0, blocks, one_key_block, 0)
    dq_ref[...] = (dq_acc[...] * scale).astype(BF16)


def attention_calls(length, heads, block):
    column = pl.BlockSpec((length, HEAD_DIM), lambda h, *_: (0, h))
    row = pl.BlockSpec((1, length), lambda h, *_: (0, 0))
    stat = pl.BlockSpec((1, 1, length), lambda h, *_: (h, 0, 0))
    flat = jax.ShapeDtypeStruct((length, heads * HEAD_DIM), BF16)
    pairs = heads * length * length // 4
    forward = pl.pallas_call(
        functools.partial(forward_kernel, block),
        grid_spec=pltpu.PrefetchScalarGridSpec(
            num_scalar_prefetch=1,
            grid=(heads,),
            in_specs=[row, column, column, column],
            out_specs=[column, stat],
        ),
        out_shape=(flat, jax.ShapeDtypeStruct((heads, 1, length), F32)),
        cost_estimate=pl.CostEstimate(
            flops=16 * pairs * HEAD_DIM, transcendentals=pairs, bytes_accessed=8 * length * heads * HEAD_DIM
        ),
        name="attend_forward",
    )
    backward = pl.pallas_call(
        functools.partial(backward_kernel, block),
        grid_spec=pltpu.PrefetchScalarGridSpec(
            num_scalar_prefetch=1,
            grid=(heads,),
            in_specs=[row, column, column, column, column, column, stat],
            out_specs=[column, column, column],
            scratch_shapes=[pltpu.VMEM((length, HEAD_DIM), F32), pltpu.VMEM((1, length), F32)],
        ),
        out_shape=(flat, flat, flat),
        cost_estimate=pl.CostEstimate(
            flops=40 * pairs * HEAD_DIM, transcendentals=pairs, bytes_accessed=16 * length * heads * HEAD_DIM
        ),
        name="attend_backward",
    )
    return forward, backward


def document_bounds(segment_ids, block):
    length = segment_ids.shape[0]
    position = jnp.arange(length, dtype=jnp.int32)
    same = segment_ids[:, None] == segment_ids[None, :]
    first = jnp.min(jnp.where(same, position[None, :], length), axis=1)
    last = jnp.max(jnp.where(same, position[None, :], -1), axis=1)
    low = first[::block] // block
    high = last[block - 1 :: block] // block + 1
    return first[None, :], low, high


def shards(
    hidden_in, memory, segments, gain_attn, w_query, w_key, w_value, w_out, gain_ffn, w_gate, w_up, w_down, cotangent
):
    seqs, piece, width = hidden_in.shape
    groups = lax.axis_size("seq")
    assert seqs == 1
    length = piece * groups
    share = width // groups
    heads = share // HEAD_DIM
    block = min(512, length)
    tokens = hidden_in.reshape(piece, width)
    mem = memory.reshape(piece, width)
    grad_out = cotangent.reshape(piece, width)

    def gather_all(value):
        return lax.all_gather(value, ALL, axis=0, tiled=True)

    def gather_dp(value):
        return lax.all_gather(value, "dp", axis=0, tiled=True)

    def to_heads(value):
        return lax.all_to_all(value, "seq", split_axis=0, concat_axis=0, tiled=True)

    attend_forward, attend_backward = attention_calls(length, heads, block)
    start, low, high = document_bounds(segments[0], block)

    hidden32 = tokens.astype(F32)
    rstd_in = rms_scale(hidden32)
    normed_in = hidden32 * rstd_in
    gain_attn32 = gather_all(gain_attn).astype(F32)
    gain_ffn32 = gather_all(gain_ffn).astype(F32)
    attn_in = (normed_in * gain_attn32).astype(BF16)

    key_rows = gather_all(w_key)
    value_rows = gather_all(w_value)
    query_rows = gather_all(w_query)
    out_rows = gather_all(w_out)

    def project(left, rows):
        return jnp.einsum(
            "td,dge->gte", left, rows.reshape(width, groups, share), preferred_element_type=F32
        ).astype(BF16)

    flat = (length, share)
    split = (groups, piece, share)
    key = to_heads(project(mem, key_rows)).reshape(flat)
    value = to_heads(project(mem, value_rows)).reshape(flat)
    query = to_heads(project(attn_in, query_rows)).reshape(flat)
    context_heads, lse = attend_forward(low, start, query, key, value)
    context = to_heads(context_heads.reshape(split))

    out_split = out_rows.reshape(groups, share, width)
    mid = hidden32 + jnp.einsum("gte,ged->td", context, out_split, preferred_element_type=F32)
    rstd_mid = rms_scale(mid)
    normed_mid = mid * rstd_mid
    ffn_in = (normed_mid * gain_ffn32).astype(BF16)

    def gather_units(weight):
        return lax.all_gather(weight, "seq", axis=0, tiled=True)

    gate_rows, up_rows, down_rows = gather_units(w_gate), gather_units(w_up), gather_units(w_down)
    dy = gather_dp(grad_out)
    ffn_all = gather_dp(ffn_in)
    gate = mxu(ffn_all, gate_rows, NT)
    up = mxu(ffn_all, up_rows, NT)
    sig = jax.nn.sigmoid(gate)
    act = (gate * sig * up).astype(BF16)
    grad_act = mxu(dy, down_rows, NT)
    grad_gate = (grad_act * up * sig * (1.0 + gate * (1.0 - sig))).astype(BF16)
    grad_up = (grad_act * gate * sig).astype(BF16)

    def scatter_dp(value):
        return lax.psum_scatter(value, "dp", scatter_dimension=0, tiled=True)

    grad_ffn_in = scatter_dp((mxu(grad_gate, gate_rows, NN) + mxu(grad_up, up_rows, NN)).astype(BF16)).astype(F32)
    branch = scatter_dp(mxu(act, down_rows, NN).astype(BF16)).astype(F32)
    layer_out = (mid + branch).astype(BF16)

    def scatter_units(value):
        return lax.psum_scatter(value.astype(BF16), "seq", scatter_dimension=0, tiled=True).astype(F32)

    grad_w_down = scatter_units(mxu(act, dy, TN))
    grad_w_gate = scatter_units(mxu(grad_gate, ffn_all, TN))
    grad_w_up = scatter_units(mxu(grad_up, ffn_all, TN))

    grad_gain_ffn_all = jnp.sum(normed_mid * grad_ffn_in, axis=0)
    grad_mid = grad_out.astype(F32) + norm_back(grad_ffn_in, normed_mid, rstd_mid, gain_ffn32)
    grad_branch = grad_mid.astype(BF16)
    grad_context = jnp.einsum("td,ged->gte", grad_branch, out_split, preferred_element_type=F32).astype(BF16)
    grad_context_heads = to_heads(grad_context).reshape(flat)
    dq, dk, dv = attend_backward(high, start, query, key, value, context_heads, grad_context_heads, lse)
    dq, dk, dv = [to_heads(part.reshape(split)) for part in (dq, dk, dv)]

    def unproject(part, rows):
        return jnp.einsum(
            "gte,dge->td", part, rows.reshape(width, groups, share), preferred_element_type=F32
        )

    grad_attn_in = unproject(dq, query_rows)
    grad_memory = unproject(dk, key_rows) + unproject(dv, value_rows)
    grad_gain_attn_all = jnp.sum(normed_in * grad_attn_in, axis=0)
    grad_hidden = grad_mid + norm_back(grad_attn_in, normed_in, rstd_in, gain_attn32)

    def weight_term(left, part):
        return jnp.einsum("td,gte->dge", left, part, preferred_element_type=F32).reshape(width, width)

    def scatter_rows(value):
        part = lax.psum_scatter(value.astype(BF16), "dp", scatter_dimension=0, tiled=True)
        return lax.psum_scatter(part, "seq", scatter_dimension=0, tiled=True).astype(F32)

    grad_w_out = scatter_rows(
        jnp.einsum("gte,td->ged", context, grad_branch, preferred_element_type=F32).reshape(width, width)
    )
    grad_w_query = scatter_rows(weight_term(attn_in, dq))
    grad_w_key = scatter_rows(weight_term(mem, dk))
    grad_w_value = scatter_rows(weight_term(mem, dv))

    gains = lax.psum((grad_gain_attn_all, grad_gain_ffn_all), ALL)
    owner = lax.axis_index("dp") * groups + lax.axis_index("seq")
    here = gain_attn.shape[0]
    grad_gain_attn, grad_gain_ffn = [lax.dynamic_slice_in_dim(g, owner * here, here) for g in gains]
    cube = (seqs, piece, width)
    return (
        layer_out.reshape(cube),
        grad_hidden.reshape(cube),
        grad_memory.reshape(cube),
        grad_gain_attn,
        grad_w_query,
        grad_w_key,
        grad_w_value,
        grad_w_out,
        grad_gain_ffn,
        grad_w_gate,
        grad_w_up,
        grad_w_down,
    )


def solution(mesh):
    tokens = P("dp", "seq", None)
    rows = P(ALL, None)
    gain = P(ALL)
    in_specs = (tokens, tokens, P("dp", None), gain, rows, rows, rows, rows, gain, rows, rows, rows, tokens)
    out_specs = (tokens, tokens, tokens, gain, rows, rows, rows, rows, gain, rows, rows, rows)
    return jax.shard_map(shards, mesh=mesh, in_specs=in_specs, out_specs=out_specs, check_vma=False)
```

time: 3090 us -> 1850 us (0.60)
  local copies, waits for them, and re-layouts: 720 us -> 110 us
  waiting for transfers between devices: 1050 us -> 796 us
  matrix products: 509 us -> 302 us
  other arithmetic: 231 us -> 43.7 us
  Pallas kernels: 0 us -> 72.3 us
  starting transfers between devices: 72.7 us -> 32 us
    all_to_all x14 -> x5, waiting for transfers between devices: 710 us -> 176 us  [to_heads(): return lax.all_to_all(value, 'seq', split_axis=0, concat_axis=0, tiled=True)]
    reduce_scatter x0 -> x10, waiting for transfers between devices: none -> 216 us  [the longest x2 210 us: scatter_dp(): return lax.psum_scatter(value, 'dp', scatter_dimension=0, tiled=True)]
    dot_general x49 -> x21, matrix products: 509 us -> 302 us  [the longest x9 189 us: mxu(): return lax.dot_general(left, right, dims, preferred_element_type=F32)]
    reshape x14 -> x0, local copies, waits for them, and re-layouts: 185 us -> none  [the longest x6 131 us: regroup(): values.reshape(count, dp_count, groups, values.shape[1] // (dp_count * gr...]
    unnamed x119 -> x62, local copies, waits for them, and re-layouts: 203 us -> 33.9 us
    all_to_all x0 -> x3, blocking collectives: none -> 154 us  [to_heads(): return lax.all_to_all(value, 'seq', split_axis=0, concat_axis=0, tiled=True)]
    concatenate x1 -> x0, local copies, waits for them, and re-layouts: 144 us -> none  [shards(): jnp.concatenate([row_terms(attn_left, query_right, blocks, share_d), row_...]
    psum x1, blocking collectives: 163 us -> 38.1 us  [shards(): gains = lax.psum((grad_gain_attn_all, grad_gain_ffn_all), ALL)]
  transfers between devices with their start and end apart: 28 -> 27, of which waited for: 14 -> 12; matrix products, arithmetic and copies ran while one was open for 41% -> 29% of each run, Pallas kernels for 0% -> 4%
where the time goes in v1:
time: 1850 us; the launch traced here: 1840 us
  waiting for transfers between devices  796 us (43%)
  blocking collectives  465 us (25%)
  matrix products  302 us (16%)
  local copies, waits for them, and re-layouts  110 us (6%)
  Pallas kernels  72.3 us (4%)
  other arithmetic  43.7 us (2%)
  starting transfers between devices  32 us (2%)
    unnamed x2, blocking collectives  272 us
    reduce_scatter x2, waiting for transfers between devices, scatter_dp(): return lax.psum_scatter(value, 'dp', scatter_dimension=0, tiled=True)  210 us
    dot_general x9, matrix products, mxu(): return lax.dot_general(left, right, dims, preferred_element_type=F32)  189 us
    all_to_all x5, waiting for transfers between devices, to_heads(): return lax.all_to_all(value, 'seq', split_axis=0, concat_axis=0, tiled=True)  176 us
    all_gather x4, waiting for transfers between devices, gather_all(): return lax.all_gather(value, ALL, axis=0, tiled=True)  166 us
    all_to_all x3, blocking collectives, to_heads(): return lax.all_to_all(value, 'seq', split_axis=0, concat_axis=0, tiled=True)  154 us
    all_gather x2, waiting for transfers between devices, gather_dp(): return lax.all_gather(value, 'dp', axis=0, tiled=True)  146 us
    all_gather x3, waiting for transfers between devices, gather_units(): return lax.all_gather(weight, 'seq', axis=0, tiled=True)  87.2 us
  transfers between devices with their start and end apart: 27, of which 12 were waited for; matrix products, arithmetic and copies ran while one was open for 29% of the time, Pallas kernels for 4%

profile of v1, /device:TPU:0, one launch (start us, length us, event | category | flops | bytes accessed | tf_op | source)
XLA Modules:
  0.0 1836.1 jit_solution(2214328671289921782)
XLA Ops:
  10.0 81.1 %all-gather.18.cloned.1.call-done = bf16[2048,2048]{1,0:T(8,128)(2,1)} async-done(((bf16[64,2048]{1,0:T(8,128)(2,1)}), bf16[2048,2048]{1,0:T(8,128)(2,1)}) %all-gather.18.cloned.1.call-update) | async-done | bytes 8388624 | tf_op jit(solution)/shard_map/all_gather | solution.py:193
  91.1 12.4 copy.70
  117.1 84.9 %all-gather.16.cloned.1.call-done = bf16[2048,2048]{1,0:T(8,128)(2,1)} async-done(((bf16[64,2048]{1,0:T(8,128)(2,1)}), bf16[2048,2048]{1,0:T(8,128)(2,1)}) %all-gather.16.cloned.1.call-update) | async-done | bytes 8388624 | tf_op jit(solution)/shard_map/all_gather | solution.py:193
  201.9 12.3 copy.68
  229.2 91.8 %all-reduce.9 = (bf16[2048]{0:T(1024)(128)(2,1)S(1)}, bf16[2048]{0:T(1024)(128)(2,1)S(1)}) all-reduce(bf16[2048]{0:T(1024)(128)(2,1)S(1)} %dynamic-update-slice, bf16[2048]{0:T(1024)(128)(2,1)S(1)} %dynamic-update-slice.1), channel_id=1, replica_groups=mesh['dp'=8,'seq'=4] {'dp','seq'}, use_global_device_ids=true, to_apply=%add | all-reduce | flops 4096 | bytes 16384
  323.1 12.3 copy.66
  366.7 58.6 %all-to-all-done = bf16[4,512,512]{2,1,0:T(8,128)(2,1)} async-done(((bf16[4,512,512]{2,1,0:T(8,128)(2,1)}), bf16[4,512,512]{2,1,0:T(8,128)(2,1)}, u32[]{:S(2)}, u32[]{:S(2)}) %all-to-all-start) | async-done | bytes 2097184 | tf_op jit(solution)/shard_map/all_to_all | solution.py:199
  425.2 29.6 %attend_forward.1 = (bf16[2048,512]{1,0:T(8,128)(2,1)}, f32[4,1,2048]{2,1,0:T(1,128)}) custom-call(s32[4]{0:T(128)} %and_select_fusion.1.low_ref, s32[1,2048]{1,0:T(1,128)} %bitcast.189, bf16[2048,512]{1,0:T(8,128)(2,1)} %bitcast.7.q_ref, bf16[2048,512]{1,0:T(8,128)(2,1)} %bitcast.176, bf16[2048,512]{1,0:T(8,128)(2,1)} %bitcast.174), custom_call_target="tpu_custom_call" | custom-call | flops 8589934592 | bytes 8388608 | tf_op jit(solution)/shard_map/attend_forward/pallas_call | solution.py:226
  460.1 70.2 %all-to-all-done.3 = bf16[4,512,512]{2,1,0:T(8,128)(2,1)} async-done(((bf16[4,512,512]{2,1,0:T(8,128)(2,1)}), bf16[4,512,512]{2,1,0:T(8,128)(2,1)}, u32[]{:S(2)}, u32[]{:S(2)}) %all-to-all-start.3) | async-done | bytes 2097184 | tf_op jit(solution)/shard_map/all_to_all | solution.py:199
  547.7 30.9 %all-gather.28.cloned.1.call-done = bf16[4,172,2048]{2,1,0:T(8,128)(2,1)} async-done(((bf16[1,172,2048]{2,1,0:T(8,128)(2,1)}), bf16[4,172,2048]{2,1,0:T(8,128)(2,1)}) %all-gather.28.cloned.1.call-update) | async-done | bytes 2818064 | tf_op jit(solution)/shard_map/all_gather | solution.py:236
  581.9 56.2 %all-gather.30.cloned.1.call-done = bf16[4,172,2048]{2,1,0:T(8,128)(2,1)} async-done(((bf16[1,172,2048]{2,1,0:T(8,128)(2,1)}), bf16[4,172,2048]{2,1,0:T(8,128)(2,1)}) %all-gather.30.cloned.1.call-update) | async-done | bytes 2818064 | tf_op jit(solution)/shard_map/all_gather | solution.py:236
  641.3 87.9 %all-gather.22.cloned.1.call-done = bf16[4096,2048]{1,0:T(8,128)(2,1)} async-done(((bf16[512,2048]{1,0:T(8,128)(2,1)}), bf16[4096,2048]{1,0:T(8,128)(2,1)}) %all-gather.22.cloned.1.call-update) | async-done | bytes 16777232 | tf_op jit(solution)/shard_map/all_gather | solution.py:196
  729.2 18.8 %fusion.62 = f32[4096,688]{0,1:T(8,128)} fusion(bf16[4096,2048]{1,0:T(8,128)(2,1)} %all-gather.22.cloned.1.call-done, bf16[688,2048]{1,0:T(8,128)(2,1)} %reshape.170), kind=kOutput, calls=%fused_computation.88 | convolution fusion | flops 11542724608 | bytes 30867456 | tf_op jit(solution)/shard_map/dot_general | solution.py:24
  748.0 14.6 fusion.61
  762.6 58.3 %all-gather.24.cloned.1.call-done = bf16[1,4096,2048]{2,1,0:T(8,128)(2,1)} async-done(((bf16[1,512,2048]{2,1,0:T(8,128)(2,1)}), bf16[1,4096,2048]{2,1,0:T(8,128)(2,1)}) %all-gather.24.cloned.1.call-update) | async-done | bytes 16777232 | tf_op jit(solution)/shard_map/all_gather | solution.py:196
  821.0 29.0 %multiply_convert_fusion = (bf16[4096,688]{0,1:T(8,128)(2,1)}, bf16[4096,688]{0,1:T(8,128)(2,1)}, bf16[4096,688]{0,1:T(8,128)(2,1)}) fusion(f32[4096,688]{0,1:T(8,128)} %fusion.61, f32[4096,688]{0,1:T(8,128)} %fusion.62, bf16[688,2048]{1,0:T(8,128)(2,1)} %reshape.172, bf16[1,4096,2048]{2,1,0:T(8,128)(2,1)} %all-gather.24.cloned.1.call-done), kind=kOutput, calls=%fused_computation.10 | convolution fusion | flops 11587813376 | bytes 59047936 | tf_op jit(solution)/shard_map/dot_general | solution.py:24
  850.0 21.9 %fusion.63 = f32[4096,2048]{1,0:T(8,128)} fusion(bf16[4096,688]{0,1:T(8,128)(2,1)} %get-tuple-element.39, bf16[688,2048]{1,0:T(8,128)(2,1)} %reshape.168), kind=kOutput, calls=%fused_computation.89 | convolution fusion | flops 11542724608 | bytes 42008576 | tf_op jit(solution)/shard_map/dot_general | solution.py:24
  871.9 26.3 %add_convert_fusion = bf16[4096,2048]{1,0:T(8,128)(2,1)} fusion(f32[4096,2048]{1,0:T(8,128)} %fusion.63, bf16[4096,688]{0,1:T(8,128)(2,1)} %get-tuple-element.38, bf16[688,2048]{1,0:T(8,128)(2,1)} %reshape.170), kind=kOutput, calls=%fused_computation | convolution fusion | flops 11559501824 | bytes 58785792 | tf_op jit(solution)/shard_map/dot_general | solution.py:24
  898.3 20.9 %convolution_convert_fusion = bf16[4096,2048]{1,0:T(8,128)(2,1)} fusion(bf16[4096,688]{0,1:T(8,128)(2,1)} %get-tuple-element.40, bf16[688,2048]{1,0:T(8,128)(2,1)} %reshape.172), kind=kOutput, calls=%fused_computation.9 | convolution fusion | flops 11551113216 | bytes 25231360 | tf_op jit(solution)/shard_map/dot_general | solution.py:24
  919.3 95.0 %reduce-scatter.19.cloned.1.call-done = bf16[512,2048]{1,0:T(8,128)(2,1)} async-done(((bf16[4096,2048]{1,0:T(8,128)(2,1)}), bf16[512,2048]{1,0:T(8,128)(2,1)}) %reduce-scatter.19.cloned.1.call-update) | async-done | bytes 2097168 | tf_op jit(solution)/shard_map/reduce_scatter | solution.py:250
  1019.0 115.0 %reduce-scatter.17.cloned.1.call-done = bf16[512,2048]{1,0:T(8,128)(2,1)} async-done(((bf16[4096,2048]{1,0:T(8,128)(2,1)}), bf16[512,2048]{1,0:T(8,128)(2,1)}) %reduce-scatter.17.cloned.1.call-update) | async-done | bytes 2097168 | tf_op jit(solution)/shard_map/reduce_scatter | solution.py:250
  1166.7 47.1 %all-to-all-done.4 = bf16[4,512,512]{2,1,0:T(8,128)(2,1)} async-done(((bf16[4,512,512]{2,1,0:T(8,128)(2,1)}), bf16[4,512,512]{2,1,0:T(8,128)(2,1)}, u32[]{:S(2)}, u32[]{:S(2)}) %all-to-all-start.4) | async-done | bytes 2097184 | tf_op jit(solution)/shard_map/all_to_all | solution.py:199
  1213.9 42.7 %attend_backward.1 = (bf16[2048,512]{1,0:T(8,128)(2,1)}, bf16[2048,512]{1,0:T(8,128)(2,1)}, bf16[2048,512]{1,0:T(8,128)(2,1)}) custom-call(s32[4]{0:T(128)} %fusion.59.high_ref, s32[1,2048]{1,0:T(1,128)} %bitcast.190, bf16[2048,512]{1,0:T(8,128)(2,1)} %bitcast.7.q_ref, bf16[2048,512]{1,0:T(8,128)(2,1)} %bitcast.177, bf16[2048,512]{1,0:T(8,128)(2,1)} %bitcast.175, ...), custom_call_target="tpu_custom_call" | custom-call | flops 21474836480 | bytes 16777216 | tf_op jit(solution)/shard_map/attend_backward/pallas_call | solution.py:268
  1256.6 52.5 %all_to_all.40 = bf16[4,512,512]{2,1,0:T(8,128)(2,1)} all-to-all(bf16[4,512,512]{2,1,0:T(8,128)(2,1)} %bitcast.181), channel_id=1, replica_groups=mesh['dp'=8,'seq'=4] {'seq'}, dimensions={0} | all-to-all | bytes 4194304 | tf_op jit(solution)/shard_map/all_to_all | solution.py:199
  1323.5 50.8 %all_to_all.41 = bf16[4,512,512]{2,1,0:T(8,128)(2,1)S(1)} all-to-all(bf16[4,512,512]{2,1,0:T(8,128)(2,1)} %bitcast.180), channel_id=1, replica_groups=mesh['dp'=8,'seq'=4] {'seq'}, dimensions={0} | all-to-all | bytes 4194304 | tf_op jit(solution)/shard_map/all_to_all | solution.py:199
  1381.2 12.3 copy.79
  1393.6 50.9 %all_to_all.42 = bf16[4,512,512]{2,1,0:T(8,128)(2,1)S(1)} all-to-all(bf16[4,512,512]{2,1,0:T(8,128)(2,1)} %bitcast.179), channel_id=1, replica_groups=mesh['dp'=8,'seq'=4] {'seq'}, dimensions={0} | all-to-all | bytes 4194304 | tf_op jit(solution)/shard_map/all_to_all | solution.py:199
  1463.7 18.5 %fusion.31 = bf16[688,2048]{1,0:T(8,128)(2,1)} fusion(bf16[4096,688]{0,1:T(8,128)(2,1)} %get-tuple-element.40, bf16[1,4096,2048]{2,1,0:T(8,128)(2,1)} %all-gather.24.cloned.1.call-done), kind=kOutput, calls=%fused_computation.51 | convolution fusion | flops 11544133632 | bytes 25231360 | tf_op jit(solution)/shard_map/dot_general | solution.py:24
  1482.2 19.9 %convolution_convert_fusion.5 = bf16[688,2048]{1,0:T(8,128)(2,1)} fusion(bf16[4096,688]{0,1:T(8,128)(2,1)} %get-tuple-element.38, bf16[4096,2048]{1,0:T(8,128)(2,1)} %all-gather.22.cloned.1.call-done), kind=kOutput, calls=%fused_computation.49 | convolution fusion | flops 11544133632 | bytes 25231360 | tf_op jit(solution)/shard_map/dot_general | solution.py:24
  1502.2 18.7 %convolution_convert_fusion.6 = bf16[688,2048]{1,0:T(8,128)(2,1)} fusion(bf16[4096,688]{0,1:T(8,128)(2,1)} %get-tuple-element.39, bf16[4096,2048]{1,0:T(8,128)(2,1)} %all-gather.22.cloned.1.call-done), kind=kOutput, calls=%fused_computation.50 | convolution fusion | flops 11544133632 | bytes 25231360 | tf_op jit(solution)/shard_map/dot_general | solution.py:24
  1521.0 180.6 %fusion.60 = (bf16[176,2048]{1,0:T(8,128)(2,1)S(1)}, bf16[176,2048]{1,0:T(8,128)(2,1)S(1)}, bf16[176,2048]{1,0:T(8,128)(2,1)}) fusion(bf16[688,2048]{1,0:T(8,128)(2,1)} %convolution_convert_fusion.6, bf16[688,2048]{1,0:T(8,128)(2,1)} %convolution_convert_fusion.5, bf16[688,2048]{1,0:T(8,128)(2,1)} %fusion.31), kind=kCustom, calls=%all-reduce-scatter.3 | all-reduce-scatter fusion | flops 4325377 | bytes 10617344
  1749.7 38.1 %all-reduce.8 = (f32[2048]{0:T(1024)S(1)}, f32[2048]{0:T(1024)S(1)}) all-reduce(f32[2048]{0:T(1024)S(1)} %get-tuple-element.24, f32[2048]{0:T(1024)S(1)} %copy-done.14), channel_id=1, replica_groups=mesh['dp'=8,'seq'=4] {'dp','seq'}, use_global_device_ids=true, to_apply=%region_9.10 | all-reduce | flops 4096 | bytes 32768 | tf_op jit(solution)/shard_map/psum | solution.py:295
  (165 shorter events, 260.3 us)
Async XLA Ops:
  7.2 96.3 %copy-start = (bf16[1,512,2048]{2,1,0:T(8,128)(2,1)S(1)}, bf16[1,512,2048]{2,1,0:T(8,128)(2,1)}, u32[]{:S(2)}) copy-start(bf16[1,512,2048]{2,1,0:T(8,128)(2,1)} %param.14) | copy-start | bytes 6291460
  7.2 83.9 %all-gather.18.cloned.1.call-start = ((), (), s32[]{:S(2)}) async-start(), calls=%async_computation.20 | async-start | bytes 8650752 | tf_op jit(solution)/shard_map/all_gather | solution.py:193
  7.9 194.0 %all-gather.16.cloned.1.call-start = ((), (), s32[]{:S(2)}) async-start(), calls=%async_computation.19 | async-start | bytes 8650752 | tf_op jit(solution)/shard_map/all_gather | solution.py:193
  8.7 314.4 %all-gather.14.cloned.1.call-start = ((), (), s32[]{:S(2)}) async-start(), calls=%async_computation.18 | async-start | bytes 8650752 | tf_op jit(solution)/shard_map/all_gather | solution.py:193
  9.4 450.7 %all-gather.20.cloned.1.call-start = ((), (), s32[]{:S(2)}) async-start(), calls=%async_computation.21 | async-start | bytes 8650752 | tf_op jit(solution)/shard_map/all_gather | solution.py:193
  112.6 110.8 %all-to-all-start.2 = ((bf16[4,512,512]{1,2,0:T(8,128)(2,1)}), bf16[4,512,512]{1,2,0:T(8,128)(2,1)}, u32[]{:S(2)}, u32[]{:S(2)}) async-start(bf16[4,512,512]{1,2,0:T(8,128)(2,1)} %convert_bitcast_fusion.2), calls=%async_computation.2 | async-start | bytes 4194304 | tf_op jit(solution)/shard_map/all_to_all | solution.py:199
  223.4 121.9 %all-to-all-start.1 = ((bf16[4,512,512]{1,2,0:T(8,128)(2,1)}), bf16[4,512,512]{1,2,0:T(8,128)(2,1)}, u32[]{:S(2)}, u32[]{:S(2)}) async-start(bf16[4,512,512]{1,2,0:T(8,128)(2,1)} %convert_bitcast_fusion.3), calls=%async_computation.1 | async-start | bytes 4194304 | tf_op jit(solution)/shard_map/all_to_all | solution.py:199
  228.0 316.5 %all-gather.26.cloned.1.call-start = ((), (), s32[]{:S(2)}) async-start(), calls=%async_computation.34 | async-start | bytes 3604480 | tf_op jit(solution)/shard_map/all_gather | solution.py:236
  345.3 79.9 %all-to-all-start = ((bf16[4,512,512]{2,1,0:T(8,128)(2,1)}), bf16[4,512,512]{2,1,0:T(8,128)(2,1)}, u32[]{:S(2)}, u32[]{:S(2)}) async-start(bf16[4,512,512]{2,1,0:T(8,128)(2,1)} %convert_bitcast_fusion.4), calls=%async_computation | async-start | bytes 4194304 | tf_op jit(solution)/shard_map/all_to_all | solution.py:199
  349.9 228.7 %all-gather.28.cloned.1.call-start = ((), (), s32[]{:S(2)}) async-start(), calls=%async_computation.35 | async-start | bytes 3604480 | tf_op jit(solution)/shard_map/all_gather | solution.py:236
  454.8 75.5 %all-to-all-start.3 = ((bf16[4,512,512]{2,1,0:T(8,128)(2,1)}), bf16[4,512,512]{2,1,0:T(8,128)(2,1)}, u32[]{:S(2)}, u32[]{:S(2)}) async-start(bf16[4,512,512]{2,1,0:T(8,128)(2,1)} %bitcast.178), calls=%async_computation.3 | async-start | bytes 4194304 | tf_op jit(solution)/shard_map/all_to_all | solution.py:199
  459.3 178.9 %all-gather.30.cloned.1.call-start = ((), (), s32[]{:S(2)}) async-start(), calls=%async_computation.36 | async-start | bytes 3604480 | tf_op jit(solution)/shard_map/all_gather | solution.py:236
  460.0 269.1 %all-gather.22.cloned.1.call-start = ((), (), s32[]{:S(2)}) async-start(), calls=%async_computation.22 | async-start | bytes 18874368 | tf_op jit(solution)/shard_map/all_gather | solution.py:196
  460.1 79.5 %copy-start.8 = (f32[2048]{0:T(1024)}, f32[2048]{0:T(1024)S(1)}, u32[]{:S(2)}) copy-start(f32[2048]{0:T(1024)S(1)} %convert_element_type.149) | copy-start | bytes 24580
  543.3 277.7 %all-gather.24.cloned.1.call-start = ((), (), s32[]{:S(2)}) async-start(), calls=%async_computation.33 | async-start | bytes 18874368 | tf_op jit(solution)/shard_map/all_gather | solution.py:196
  544.0 470.3 %reduce-scatter.19.cloned.1.call-start = ((), (), s32[]{:S(2)}) async-start(), calls=%async_computation.24 | async-start | bytes 18874368 | tf_op jit(solution)/shard_map/reduce_scatter | solution.py:250
  898.3 235.7 %reduce-scatter.17.cloned.1.call-start = ((), (), s32[]{:S(2)}) async-start(), calls=%async_computation.23 | async-start | bytes 18874368 | tf_op jit(solution)/shard_map/reduce_scatter | solution.py:250
  919.3 95.1 %copy-start.9 = (f32[2048]{0:T(1024)S(1)}, f32[2048]{0:T(1024)}, u32[]{:S(2)}) copy-start(f32[2048]{0:T(1024)} %copy-done.8) | copy-start | bytes 24580
  919.3 95.1 %copy-start.11 = (f32[512]{0:T(512)S(1)}, f32[512]{0:T(512)}, u32[]{:S(2)}) copy-start(f32[512]{0:T(512)} %copy-done.10) | copy-start | bytes 6148
  919.3 582.8 %reduce-scatter.33.cloned.1.call-start = ((), (), s32[]{:S(2)}) async-start(), calls=%async_computation.31 | async-start | bytes 9437184 | tf_op jit(solution)/shard_map/reduce_scatter | solution.py:285
  1160.8 53.0 %all-to-all-start.4 = ((bf16[4,512,512]{2,1,0:T(8,128)(2,1)}), bf16[4,512,512]{2,1,0:T(8,128)(2,1)}, u32[]{:S(2)}, u32[]{:S(2)}) async-start(bf16[4,512,512]{2,1,0:T(8,128)(2,1)} %convert_bitcast_fusion.1), calls=%async_computation.6 | async-start | bytes 4194304 | tf_op jit(solution)/shard_map/all_to_all | solution.py:199
  1165.4 355.5 %reduce-scatter.21.cloned.1.call-start = ((), (), s32[]{:S(2)}) async-start(), calls=%async_computation.25 | async-start | bytes 9437184 | tf_op jit(solution)/shard_map/reduce_scatter | solution.py:285
  1323.5 414.7 %reduce-scatter.29.cloned.1.call-start = ((), (), s32[]{:S(2)}) async-start(), calls=%async_computation.29 | async-start | bytes 9437184 | tf_op jit(solution)/shard_map/reduce_scatter | solution.py:285
  1393.5 406.0 %reduce-scatter.25.cloned.1.call-start = ((), (), s32[]{:S(2)}) async-start(), calls=%async_computation.27 | async-start | bytes 9437184 | tf_op jit(solution)/shard_map/reduce_scatter | solution.py:285
  1463.7 352.6 %reduce-scatter.35.cloned.1.call-start = ((), (), s32[]{:S(2)}) async-start(), calls=%async_computation.32 | async-start | bytes 1310720 | tf_op jit(solution)/shard_map/reduce_scatter | solution.py:286
  1502.1 315.9 %reduce-scatter.23.cloned.1.call-start = ((), (), s32[]{:S(2)}) async-start(), calls=%async_computation.26 | async-start | bytes 1310720 | tf_op jit(solution)/shard_map/reduce_scatter | solution.py:286
  1520.9 191.4 %copy-start.17 = (u32[32]{0:T(128)S(1)}, u32[32]{0:T(128)}, u32[]{:S(2)}) copy-start(u32[32]{0:T(128)} %constant.74) | copy-start | bytes 388
  1521.0 298.9 %reduce-scatter.31.cloned.1.call-start = ((), (), s32[]{:S(2)}) async-start(), calls=%async_computation.30 | async-start | bytes 1310720 | tf_op jit(solution)/shard_map/reduce_scatter | solution.py:286
  1703.7 9.8 collective-permute-start.2
  1706.6 13.7 collective-permute-start.1
  1709.1 17.0 collective-permute-start
  1738.2 89.1 %reduce-scatter.27.cloned.1.call-start = ((), (), s32[]{:S(2)}) async-start(), calls=%async_computation.28 | async-start | bytes 1310720 | tf_op jit(solution)/shard_map/reduce_scatter | solution.py:286
  (19 other events, 261.3 us)
Sparse Core Ops, SparseCore 0:
  11.0 80.0 all-gather.17
  94.0 107.8 all-gather.15
  204.9 109.0 all-gather.13
  316.8 108.2 all-gather.19
  426.5 81.7 all-gather.25
  509.7 68.9 all-gather.27
  580.2 57.8 all-gather.29
  640.6 88.5 all-gather.21
  731.1 89.8 all-gather.23
  898.4 115.9 reduce-scatter.18
  1018.0 115.9 reduce-scatter.16
  1150.4 71.2 reduce-scatter.32
  1323.6 69.3 reduce-scatter.20
  1396.3 71.2 reduce-scatter.28
  1471.3 71.2 reduce-scatter.24
  1544.8 43.8 reduce-scatter.34
  1590.9 43.4 reduce-scatter.22
  1738.3 25.1 reduce-scatter.30
  1799.7 27.5 reduce-scatter.26

commit v2 on v1

--- a/solution.py
+++ b/solution.py
@@ -18,6 +18,7 @@
 NT = (((1,), (1,)), ((), ()))
 TN = (((0,), (0,)), ((), ()))
 NN = (((1,), (0,)), ((), ()))
+BY_MESH = pl.DeviceIdType.MESH
 
 
 def mxu(left, right, dims):
@@ -142,7 +143,7 @@
         ),
         out_shape=(flat, jax.ShapeDtypeStruct((heads, 1, length), F32)),
         cost_estimate=pl.CostEstimate(
-            flops=16 * pairs * HEAD_DIM, transcendentals=pairs, bytes_accessed=8 * length * heads * HEAD_DIM
+            flops=64 * pairs * HEAD_DIM, transcendentals=pairs, bytes_accessed=8 * length * heads * HEAD_DIM
         ),
         name="attend_forward",
     )
@@ -157,7 +158,7 @@
         ),
         out_shape=(flat, flat, flat),
         cost_estimate=pl.CostEstimate(
-            flops=40 * pairs * HEAD_DIM, transcendentals=pairs, bytes_accessed=16 * length * heads * HEAD_DIM
+            flops=96 * pairs * HEAD_DIM, transcendentals=pairs, bytes_accessed=16 * length * heads * HEAD_DIM
         ),
         name="attend_backward",
     )
@@ -175,127 +176,837 @@
     return first[None, :], low, high
 
 
+def remote(src, dst, send, recv, device):
+    return pltpu.make_async_remote_copy(
+        src_ref=src, dst_ref=dst, send_sem=send, recv_sem=recv, device_id=device, device_id_type=BY_MESH
+    )
+
+
+class Place:
+    def __init__(self, dp_count, groups):
+        self.groups = groups
+        self.chips = dp_count // 2
+        self.dp = lax.axis_index("dp")
+        self.seq = lax.axis_index("seq")
+        self.core = lax.rem(self.dp, 2)
+        self.chip = self.dp // 2
+        self.sibling = {"dp": self.dp + 1 - 2 * self.core, "seq": self.seq}
+
+    def chip_at(self, step):
+        return lax.rem(self.chip + step, self.chips)
+
+    def chip_device(self, chip):
+        return {"dp": 2 * chip + self.core, "seq": self.seq}
+
+    def line_at(self, step):
+        return lax.rem(self.seq + step, self.groups)
+
+    def line_device(self, seq):
+        return {"dp": self.dp, "seq": seq}
+
+    def barrier(self):
+        everyone = pltpu.get_barrier_semaphore()
+        for step in range(1, self.groups):
+            pl.semaphore_signal(everyone, inc=1, device_id=self.line_device(self.line_at(step)), device_id_type=BY_MESH)
+        for step in range(1, self.chips):
+            pl.semaphore_signal(everyone, inc=1, device_id=self.chip_device(self.chip_at(step)), device_id_type=BY_MESH)
+        pl.semaphore_signal(everyone, inc=1, device_id=self.sibling, device_id_type=BY_MESH)
+        pl.semaphore_wait(everyone, self.groups + self.chips - 1)
+
+
+def project_kernel(
+    dp_count, groups, hidden, memory, gains, w_key, w_value, w_query, w_out,
+    attn_in, gain_rows, key, value, query, all_gains, all_key, all_value, all_query, all_out,
+    weight, parts, line_send, line_recv, chip_send, chip_recv, core_send, core_recv,
+    own_sem, load_sem, part_send, part_recv, part_own,
+):
+    place = Place(dp_count, groups)
+    chips, seq = place.chips, place.seq
+    shards = (gains, w_key, w_value, w_query, w_out)
+    wholes = (all_gains, all_key, all_value, all_query, all_out)
+    count = len(shards)
+    own = place.dp * groups + seq
+    above, below = seq < groups - 1, seq > 0
+    up, down = place.line_device(lax.rem(seq + 1, groups)), place.line_device(lax.rem(seq + groups - 1, groups))
+
+    def line(m, dp):
+        return wholes[m].at[pl.ds(dp * groups, groups)]
+
+    def along(m, src, block, distance, upward):
+        slot = 0 if upward else 1
+        return remote(
+            src, wholes[m].at[block], line_send.at[m, slot, distance - 1], line_recv.at[m, slot, distance - 1],
+            up if upward else down,
+        )
+
+    def to_chip(m, src, block, step):
+        return remote(
+            src, wholes[m].at[block], chip_send.at[m, step - 1], chip_recv.at[m, step - 1],
+            place.chip_device(place.chip_at(step)),
+        )
+
+    def to_sibling(m, src, dst, step):
+        return remote(src, dst, core_send.at[m, step], core_recv.at[m, step], place.sibling)
+
+    def spread(m, src, block):
+        for step in range(1, chips):
+            to_chip(m, src, block, step).start()
+        to_sibling(m, src, wholes[m].at[block], 0).start()
+
+    def own_copy(m):
+        return pltpu.make_async_copy(shards[m], wholes[m].at[own], own_sem.at[m])
+
+    def start_own(m):
+        own_copy(m).start()
+
+        @pl.when(above)
+        def _():
+            along(m, shards[m], own, 1, True).start()
+
+        @pl.when(below)
+        def _():
+            along(m, shards[m], own, 1, False).start()
+
+        spread(m, shards[m], own)
+
+    def serve_line(m):
+        for distance in range(1, groups):
+            for upward in (True, False):
+                block = own - distance if upward else own + distance
+                there = seq >= distance if upward else seq < groups - distance
+                onward = above if upward else below
+
+                @pl.when(there)
+                def _():
+                    landed = wholes[m].at[block]
+                    along(m, landed, block, distance, upward).wait_recv()
+
+                    @pl.when(onward)
+                    def _():
+                        along(m, landed, block, distance + 1, upward).start()
+
+                    spread(m, landed, block)
+
+    def serve_chips(m):
+        for step in range(1, chips):
+            dp = 2 * lax.rem(place.chip + chips - step, chips) + place.core
+            remote(
+                line(m, dp), line(m, dp), chip_send.at[m, step - 1], chip_recv.at[m, step - 1], place.sibling
+            ).wait_recv()
+            to_sibling(m, line(m, dp), line(m, dp), step).start()
+
+    def finish(m):
+        for step in range(chips):
+            dp = 2 * lax.rem(place.chip + chips - step, chips) + 1 - place.core
+            to_sibling(m, line(m, dp), line(m, dp), step).wait_recv()
+        own_copy(m).wait()
+
+    targets = (None, key, value, query, None)
+    lefts = (None, memory, memory, attn_in, None)
+    share = weight.shape[2] // groups
+
+    def part_copy(m, step):
+        other = place.line_at(step)
+        return remote(
+            parts.at[m - 1, other], targets[m].at[seq], part_send.at[m - 1, step - 1], part_recv.at[m - 1, step - 1],
+            place.line_device(other),
+        )
+
+    def own_part(m):
+        return pltpu.make_async_copy(parts.at[m - 1, seq], targets[m].at[seq], part_own.at[m - 1])
+
+    def load(m):
+        return pltpu.make_async_copy(wholes[m], weight, load_sem)
+
+    def project(m):
+        load(m).start()
+        load(m).wait()
+        rows = weight.shape[0] * weight.shape[1]
+        left = lefts[m][...]
+
+        def one(step, _):
+            group = place.line_at(step)
+            columns = pl.ds(pl.multiple_of(group * share, share), share)
+            right = weight[:, :, columns].reshape(rows, share)
+            parts[m - 1, group] = jnp.dot(left, right, preferred_element_type=F32).astype(BF16)
+
+            @pl.when(step > 0)
+            def _():
+                remote(
+                    parts.at[m - 1, group], targets[m].at[seq], part_send.at[m - 1, step - 1],
+                    part_recv.at[m - 1, step - 1], place.line_device(group),
+                ).start()
+
+            return 0
+
+        lax.fori_loop(1, groups, one, 0)
+        one(0, 0)
+        own_part(m).start()
+
+    def normalize():
+        here = 128 // (weight.shape[1])
+        tiles = weight.shape[2] // 128
+        for tile in range(tiles):
+            total = all_gains_v[tile * here]
+            for i in range(1, here):
+                total = total + pltpu.roll(all_gains_v[tile * here + i], i * weight.shape[1], 1)
+            gain_rows[:, tile * 128 : (tile + 1) * 128] = total
+        step_rows = 128 if hidden.shape[0] % 128 == 0 else hidden.shape[0]
+
+        def some(i, _):
+            rows = pl.ds(pl.multiple_of(i * step_rows, step_rows), step_rows)
+            x = hidden[rows, :].astype(F32)
+            normed = x * lax.rsqrt(jnp.mean(x * x, axis=-1, keepdims=True) + EPSILON)
+            attn_in[rows, :] = (normed * gain_rows[0:1, :]).astype(BF16)
+            return 0
+
+        lax.fori_loop(0, hidden.shape[0] // step_rows, some, 0)
+
+    all_gains_v = all_gains
+    place.barrier()
+    start_own(0)
+    start_own(1)
+    serve_line(0)
+    start_own(2)
+    serve_line(1)
+    serve_chips(0)
+    serve_chips(1)
+    start_own(3)
+    serve_line(2)
+    finish(0)
+    normalize()
+    finish(1)
+    project(1)
+    serve_chips(2)
+    start_own(4)
+    serve_line(3)
+    finish(2)
+    project(2)
+    serve_chips(3)
+    serve_line(4)
+    finish(3)
+    project(3)
+    serve_chips(4)
+    finish(4)
+    for m in range(count):
+        for distance in range(1, groups):
+            for upward in (True, False):
+                came = seq >= distance - 1 if upward else seq < groups - distance + 1
+                onward = above if upward else below
+
+                @pl.when(came & onward)
+                def _():
+                    along(m, wholes[m].at[own], own, distance, upward).wait_send()
+
+        mine = line(m, place.dp)
+        for step in range(1, chips):
+            remote(
+                mine, mine, chip_send.at[m, step - 1], chip_recv.at[m, step - 1], place.sibling
+            ).wait_send()
+        for step in range(chips):
+            to_sibling(m, mine, mine, step).wait_send()
+    for m in (1, 2, 3):
+        own_part(m).wait()
+        for step in range(1, groups):
+            part_copy(m, step).wait()
+
+
+def project_call(dp_count, groups, piece, width, here):
+    chips = dp_count // 2
+    blocks = dp_count * groups
+    share = width // groups
+    hbm = pl.BlockSpec(memory_space=pl.ANY)
+    vmem = pl.BlockSpec(memory_space=pltpu.VMEM)
+    heads = jax.ShapeDtypeStruct((groups, piece, share), BF16)
+    whole = jax.ShapeDtypeStruct((blocks, here, width), BF16)
+    dma = pltpu.SemaphoreType.DMA
+    return pl.pallas_call(
+        functools.partial(project_kernel, dp_count, groups),
+        in_specs=[vmem, vmem, hbm, hbm, hbm, hbm, hbm],
+        out_specs=[vmem, vmem, hbm, hbm, hbm, vmem, hbm, hbm, hbm, hbm],
+        out_shape=(
+            jax.ShapeDtypeStruct((piece, width), BF16),
+            jax.ShapeDtypeStruct((8, width), F32),
+            heads, heads, heads,
+            jax.ShapeDtypeStruct((blocks, 8, 128), F32),
+            whole, whole, whole, whole,
+        ),
+        scratch_shapes=[
+            pltpu.VMEM((blocks, here, width), BF16),
+            pltpu.VMEM((3, groups, piece, share), BF16),
+            dma((5, 2, groups)), dma((5, 2, groups)),
+            dma((5, max(chips - 1, 1))), dma((5, max(chips - 1, 1))),
+            dma((5, chips)), dma((5, chips)),
+            dma((5,)), dma, dma((3, groups - 1)), dma((3, groups - 1)), dma((3,)),
+        ],
+        compiler_params=pltpu.CompilerParams(
+            collective_id=1, has_side_effects=True, vmem_limit_bytes=48 * 1024 * 1024
+        ),
+        cost_estimate=pl.CostEstimate(
+            flops=128 * piece * width * width, transcendentals=0, bytes_accessed=16 * width * width
+        ),
+        name="gather_project",
+    )
+
+
+def gain_tile(gain_attn, gain_ffn):
+    here = gain_attn.shape[0]
+    both = jnp.stack((gain_attn, gain_ffn)).astype(F32)
+    return jnp.pad(both, ((0, 6), (0, 128 - here)))
+
+
+def reduce_kernel(
+    dp_count, groups, here, context, memory, attn_in, gain_rows, gain_ffn_term, grad_branch, dv, dk, dq,
+    all_value, all_key, all_query, hidden, grad_mid,
+    out_v, out_k, out_q, grad_out, grad_value, grad_key, grad_query, grad_memory, grad_hidden, grad_gains,
+    right, core_buf, core_in, chip_buf, chip_in, kept, line_buf, line_in, line_own,
+    part_send, part_recv, part_own, load_sem, core_send, core_recv, chip_send, chip_recv,
+    line_send, line_recv, store_sem, core_free, chip_free,
+    weight, panel_out, grad_attn_in, mid_buf, hidden_buf, gain_term, gain_buf, gain_in,
+    weight_sem, panel_sem, mid_sem, hidden_sem, gain_send, gain_recv,
+):
+    place = Place(dp_count, groups)
+    chips, seq = place.chips, place.seq
+    panel = groups * here
+    share = right.shape[3]
+    lefts = (context, memory, memory, attn_in)
+    parts = (None, dv, dk, dq)
+    wholes = (None, out_v, out_k, out_q)
+    grads = (grad_out, grad_value, grad_key, grad_query)
+    count = 4
+
+    def part_copy(m, step):
+        other = place.line_at(step)
+        return remote(
+            parts[m].at[other], wholes[m].at[seq], part_send.at[m, step - 1], part_recv.at[m, step - 1],
+            place.line_device(other),
+        )
+
+    def own_part(m):
+        return pltpu.make_async_copy(parts[m].at[seq], wholes[m].at[seq], part_own.at[m])
+
+    def send_parts(m):
+        own_part(m).start()
+        for step in range(1, groups):
+            part_copy(m, step).start()
+
+    def sent_parts(m):
+        for step in range(1, groups):
+            part_copy(m, step).wait_send()
+
+    def load_copy(m, group):
+        source = grad_branch.at[:, pl.ds(group * share, share)] if m == 0 else wholes[m].at[group]
+        return pltpu.make_async_copy(source, right.at[m % 2, group], load_sem.at[group])
+
+    def load_right(m):
+        if m > 0:
+            own_part(m).wait()
+            for step in range(1, groups):
+                part_copy(m, step).wait_recv()
+        for group in range(groups):
+            load_copy(m, group).start()
+        for group in range(groups):
+            load_copy(m, group).wait()
+
+    def product(m, dp, store):
+        rows = pl.ds(pl.multiple_of(dp * panel, panel), panel)
+        left = lefts[m][:, rows].T
+
+        def one(group, _):
+            columns = pl.ds(pl.multiple_of(group * share, share), share)
+            store(columns, jnp.dot(left, right[m % 2, group], preferred_element_type=F32))
+            return 0
+
+        lax.fori_loop(0, groups, one, 0)
+
+    def core_copy(m, step):
+        return remote(
+            core_buf.at[step], core_in.at[m % 2, step], core_send.at[step], core_recv.at[m % 2, step], place.sibling
+        )
+
+    def chip_copy(m, step):
+        return remote(
+            chip_buf.at[m % 2, step - 1], chip_in.at[m % 2, step - 1], chip_send.at[m % 2, step - 1],
+            chip_recv.at[m % 2, step - 1], place.chip_device(place.chip_at(step)),
+        )
+
+    def line_copy(m, step):
+        return remote(
+            line_buf.at[m, step - 1], line_in.at[m, step - 1], line_send.at[m, step - 1], line_recv.at[m, step - 1],
+            place.line_device(place.line_at(step)),
+        )
+
+    order = tuple(range(1, chips)) + (0,)
+
+    def to_sibling(m):
+        if m >= 2:
+            pl.semaphore_wait(core_free, 1)
+        for step in order:
+            if m >= 1:
+                core_copy(m - 1, step).wait_send()
+            dp = 2 * place.chip_at(step) + 1 - place.core
+
+            def store(columns, value, step=step):
+                core_buf[step, :, columns] = value.astype(BF16)
+
+            product(m, dp, store)
+            core_copy(m, step).start()
+
+    def to_chips(m):
+        for step in order:
+            dp = 2 * place.chip_at(step) + place.core
+            core_copy(m, step).wait_recv()
+            if step > 0:
+                if m >= 2:
+                    chip_copy(m - 2, step).wait_send()
+                    pl.semaphore_wait(chip_free.at[step - 1], 1)
+
+                def store(columns, value, step=step):
+                    total = value + core_in[m % 2, step, :, columns].astype(F32)
+                    chip_buf[m % 2, step - 1, :, columns] = total.astype(BF16)
+
+            else:
+
+                def store(columns, value):
+                    kept[m % 2, :, columns] = value + core_in[m % 2, 0, :, columns].astype(F32)
+
+            product(m, dp, store)
+            if step > 0:
+                chip_copy(m, step).start()
+        if m + 2 < count:
+            pl.semaphore_signal(core_free, inc=1, device_id=place.sibling, device_id_type=BY_MESH)
+
+    def to_line(m):
+        for step in range(1, chips):
+            chip_copy(m, step).wait_recv()
+        for step in tuple(range(1, groups)) + (0,):
+            block = place.line_at(step)
+            rows = pl.ds(pl.multiple_of(block * here, here), here)
+            total = kept[m % 2, rows, :]
+            for other in range(1, chips):
+                total = total + chip_in[m % 2, other - 1, rows, :].astype(F32)
+            if step > 0:
+                line_buf[m, step - 1] = total.astype(BF16)
+                line_copy(m, step).start()
+            else:
+                line_own[m] = total
+        if m + 2 < count:
+            for step in range(1, chips):
+                behind = lax.rem(place.chip + chips - step, chips)
+                pl.semaphore_signal(
+                    chip_free.at[step - 1], inc=1, device_id=place.chip_device(behind), device_id_type=BY_MESH
+                )
+
+    def store_grad(m):
+        return pltpu.make_async_copy(line_own.at[m], grads[m], store_sem.at[m])
+
+    def settle(m):
+        total = line_own[m]
+        for step in range(1, groups):
+            line_copy(m, step).wait_recv()
+            total = total + line_in[m, step - 1].astype(F32)
+        line_own[m] = total
+        store_grad(m).start()
+
+    width = memory.shape[1]
+    panels = width // panel
+    piece = memory.shape[0]
+
+    def weight_copy(slot, which, source, index):
+        rows = pl.ds(pl.multiple_of(index * panel, panel), panel)
+        return pltpu.make_async_copy(source.at[rows, :], weight.at[slot, which], weight_sem.at[slot, which])
+
+    def panel_copy(slot, index):
+        columns = pl.ds(pl.multiple_of(index * panel, panel), panel)
+        return pltpu.make_async_copy(panel_out.at[slot], grad_memory.at[:, columns], panel_sem.at[slot])
+
+    def back(slot, which, m):
+        total = jnp.zeros((piece, panel), F32)
+        for group in range(groups):
+            columns = slice(group * share, (group + 1) * share)
+            total = total + lax.dot_general(
+                right[m % 2, group], weight[slot, which, :, columns], NT, preferred_element_type=F32
+            )
+        return total
+
+    def memory_gradient():
+        weight_copy(0, 0, all_value, 0).start()
+        weight_copy(0, 1, all_key, 0).start()
+
+        def one(index, _):
+            slot = lax.rem(index, 2)
+
+            @pl.when(index + 1 < panels)
+            def _():
+                weight_copy(1 - slot, 0, all_value, index + 1).start()
+                weight_copy(1 - slot, 1, all_key, index + 1).start()
+
+            weight_copy(slot, 0, all_value, index).wait()
+            weight_copy(slot, 1, all_key, index).wait()
+
+            @pl.when(index >= 2)
+            def _():
+                panel_copy(slot, index - 2).wait()
+
+            panel_out[slot] = back(slot, 0, 1) + back(slot, 1, 2)
+            panel_copy(slot, index).start()
+            return 0
+
+        lax.fori_loop(0, panels, one, 0)
+        for index in range(max(panels - 2, 0), panels):
+            panel_copy(index % 2, index).wait()
+
+    def query_gradient():
+        weight_copy(0, 0, all_query, 0).start()
+
+        def one(index, _):
+            slot = lax.rem(index, 2)
+
+            @pl.when(index + 1 < panels)
+            def _():
+                weight_copy(1 - slot, 0, all_query, index + 1).start()
+
+            weight_copy(slot, 0, all_query, index).wait()
+            columns = pl.ds(pl.multiple_of(index * panel, panel), panel)
+            grad_attn_in[:, columns] = back(slot, 0, 3)
+            return 0
+
+        lax.fori_loop(0, panels, one, 0)
+
+    some = mid_buf.shape[1]
+    batches = piece // some
+
+    def batch_rows(index):
+        return pl.ds(pl.multiple_of(index * some, some), some)
+
+    def mid_copy(slot, index):
+        return pltpu.make_async_copy(grad_mid.at[batch_rows(index), :], mid_buf.at[slot], mid_sem.at[slot])
+
+    def hidden_copy(slot, index):
+        return pltpu.make_async_copy(hidden.at[batch_rows(index), :], hidden_buf.at[slot], hidden_sem.at[slot])
+
+    def hidden_store(index):
+        rows = batch_rows(index)
+        return pltpu.make_async_copy(grad_attn_in.at[rows, :], grad_hidden.at[rows, :], panel_sem.at[0])
+
+    def hidden_gradient():
+        gain_term[...] = jnp.zeros_like(gain_term)
+        mid_copy(0, 0).start()
+        hidden_copy(0, 0).start()
+
+        def one(index, _):
+            slot = lax.rem(index, 2)
+
+            @pl.when(index + 1 < batches)
+            def _():
+                mid_copy(1 - slot, index + 1).start()
+                hidden_copy(1 - slot, index + 1).start()
+
+            mid_copy(slot, index).wait()
+            hidden_copy(slot, index).wait()
+            rows = batch_rows(index)
+            x = hidden_buf[slot].astype(F32)
+            rstd = lax.rsqrt(jnp.mean(x * x, axis=-1, keepdims=True) + EPSILON)
+            normed = x * rstd
+            grad = grad_attn_in[rows, :]
+            gain_term[0:1, :] += jnp.sum(normed * grad, axis=0, keepdims=True)
+            scaled = grad * gain_rows[0:1, :]
+            shift = jnp.mean(scaled * normed, axis=-1, keepdims=True)
+            grad_attn_in[rows, :] = mid_buf[slot] + rstd * (scaled - normed * shift)
+            hidden_store(index).start()
+            return 0
+
+        lax.fori_loop(0, batches, one, 0)
+
+    devices = dp_count * groups
+    me = place.dp * groups + seq
+
+    def gain_copy(step):
+        owner = lax.rem(me + step, devices)
+        return remote(
+            gain_buf.at[owner], gain_in.at[step], gain_send, gain_recv, {"dp": owner // groups, "seq": owner % groups}
+        )
+
+    def send_gains():
+        gain_term[1:2, :] = gain_ffn_term[0:1, :]
+        per = 128 // here
+        for owner in range(devices):
+            tile = gain_term[:, owner // per * 128 : (owner // per + 1) * 128]
+            shift = owner % per * here
+            gain_buf[owner] = pltpu.roll(tile, 128 - shift, 1) if shift else tile
+
+        def one(step, _):
+            gain_copy(step).start()
+            return 0
+
+        lax.fori_loop(1, devices, one, 0)
+
+    def sum_gains():
+        remote(
+            gain_buf.at[pl.ds(0, devices - 1)], gain_in.at[pl.ds(1, devices - 1)], gain_send, gain_recv, place.sibling
+        ).wait()
+        total = gain_buf[me]
+        for step in range(1, devices):
+            total = total + gain_in[step]
+        grad_gains[...] = total
+
+    everyone = pltpu.get_barrier_semaphore()
+
+    def greet(step, _):
+        other = lax.rem(me + step, devices)
+        pl.semaphore_signal(
+            everyone, inc=1, device_id={"dp": other // groups, "seq": other % groups}, device_id_type=BY_MESH
+        )
+        return 0
+
+    lax.fori_loop(1, devices, greet, 0)
+    pl.semaphore_wait(everyone, devices - 1)
+    send_parts(1)
+    load_right(0)
+    to_sibling(0)
+    to_chips(0)
+    sent_parts(1)
+    send_parts(2)
+    load_right(1)
+    to_sibling(1)
+    to_chips(1)
+    to_line(0)
+    sent_parts(2)
+    send_parts(3)
+    load_right(2)
+    to_sibling(2)
+    to_chips(2)
+    to_line(1)
+    settle(0)
+    memory_gradient()
+    sent_parts(3)
+    load_right(3)
+    to_sibling(3)
+    to_chips(3)
+    to_line(2)
+    settle(1)
+    query_gradient()
+    hidden_gradient()
+    send_gains()
+    to_line(3)
+    settle(2)
+    settle(3)
+    sum_gains()
+    pltpu.make_async_copy(grad_attn_in, grad_hidden, panel_sem.at[0]).wait()
+    for step in range(chips):
+        core_copy(3, step).wait_send()
+    for m in (2, 3):
+        for step in range(1, chips):
+            chip_copy(m, step).wait_send()
+    for m in range(count):
+        for step in range(1, groups):
+            line_copy(m, step).wait_send()
+        store_grad(m).wait()
+
+
+def reduce_call(dp_count, groups, piece, width, here):
+    chips = dp_count // 2
+    share = width // groups
+    panel = groups * here
+    hbm = pl.BlockSpec(memory_space=pl.ANY)
+    vmem = pl.BlockSpec(memory_space=pltpu.VMEM)
+    part = jax.ShapeDtypeStruct((groups, piece, share), BF16)
+    grad = jax.ShapeDtypeStruct((here, width), F32)
+    tokens = jax.ShapeDtypeStruct((piece, width), F32)
+    some = min(64, piece)
+    devices = dp_count * groups
+    dma = pltpu.SemaphoreType.DMA
+    others = max(chips - 1, 1)
+    return pl.pallas_call(
+        functools.partial(reduce_kernel, dp_count, groups, here),
+        in_specs=[vmem] * 5 + [hbm] * 9,
+        out_specs=[hbm] * 9 + [vmem],
+        out_shape=(part, part, part, grad, grad, grad, grad, tokens, tokens, jax.ShapeDtypeStruct((8, 128), F32)),
+        scratch_shapes=[
+            pltpu.VMEM((2, groups, piece, share), BF16),
+            pltpu.VMEM((chips, panel, width), BF16),
+            pltpu.VMEM((2, chips, panel, width), BF16),
+            pltpu.VMEM((2, others, panel, width), BF16),
+            pltpu.VMEM((2, others, panel, width), BF16),
+            pltpu.VMEM((2, panel, width), F32),
+            pltpu.VMEM((4, groups - 1, here, width), BF16),
+            pltpu.VMEM((4, groups - 1, here, width), BF16),
+            pltpu.VMEM((4, here, width), F32),
+            dma((4, groups - 1)), dma((4, groups - 1)), dma((4,)), dma((groups,)),
+            dma((chips,)), dma((2, chips)),
+            dma((2, others)), dma((2, others)),
+            dma((4, groups - 1)), dma((4, groups - 1)), dma((4,)),
+            pltpu.SemaphoreType.REGULAR, pltpu.SemaphoreType.REGULAR((others,)),
+            pltpu.VMEM((2, 2, panel, width), BF16),
+            pltpu.VMEM((2, piece, panel), F32),
+            pltpu.VMEM((piece, width), F32),
+            pltpu.VMEM((2, some, width), F32),
+            pltpu.VMEM((2, some, width), BF16),
+            pltpu.VMEM((8, width), F32),
+            pltpu.VMEM((devices, 8, 128), F32),
+            pltpu.VMEM((devices, 8, 128), F32),
+            dma((2, 2)), dma((2,)), dma((2,)), dma((2,)), dma, dma,
+        ],
+        compiler_params=pltpu.CompilerParams(
+            collective_id=2, has_side_effects=True, vmem_limit_bytes=63 * 1024 * 1024
+        ),
+        cost_estimate=pl.CostEstimate(
+            flops=128 * piece * width * width, transcendentals=0, bytes_accessed=16 * width * width
+        ),
+        name="weight_gradients",
+    )
+
+
+def exchange_kernel(dp_count, groups, spread, source, target, send_sem, recv_sem, own_sem):
+    place = Place(dp_count, groups)
+    share = source.shape[1] // groups if spread else source.shape[2]
+    everyone = pltpu.get_barrier_semaphore()
+    for step in range(1, groups):
+        pl.semaphore_signal(
+            everyone, inc=1, device_id=place.line_device(place.line_at(step)), device_id_type=BY_MESH
+        )
+    pl.semaphore_wait(everyone, groups - 1)
+
+    def columns(group):
+        return pl.ds(pl.multiple_of(group * share, share), share)
+
+    def ends(other):
+        if spread:
+            return source.at[:, columns(other)], target.at[place.seq]
+        return source.at[other], target.at[:, columns(place.seq)]
+
+    def copy(step):
+        other = place.line_at(step)
+        src, dst = ends(other)
+        return remote(src, dst, send_sem.at[step - 1], recv_sem.at[step - 1], place.line_device(other))
+
+    own = pltpu.make_async_copy(*ends(place.seq), own_sem)
+    for step in range(1, groups):
+        copy(step).start()
+    own.start()
+    own.wait()
+    for step in range(1, groups):
+        copy(step).wait()
+
+
+def exchange_call(dp_count, groups, piece, width, spread):
+    share = width // groups
+    hbm = pl.BlockSpec(memory_space=pl.ANY)
+    dma = pltpu.SemaphoreType.DMA
+    shape = (groups, piece, share) if spread else (piece, width)
+    return pl.pallas_call(
+        functools.partial(exchange_kernel, dp_count, groups, spread),
+        in_specs=[hbm],
+        out_specs=hbm,
+        out_shape=jax.ShapeDtypeStruct(shape, BF16),
+        scratch_shapes=[dma((groups - 1,)), dma((groups - 1,)), dma],
+        compiler_params=pltpu.CompilerParams(collective_id=3 + spread, has_side_effects=True),
+        cost_estimate=pl.CostEstimate(flops=32 * piece * width * width // 8, transcendentals=0, bytes_accessed=4 * piece * width),
+        name="spread_features" if spread else "collect_features",
+    )
+
+
 def shards(
     hidden_in, memory, segments, gain_attn, w_query, w_key, w_value, w_out, gain_ffn, w_gate, w_up, w_down, cotangent
 ):
     seqs, piece, width = hidden_in.shape
     groups = lax.axis_size("seq")
+    dp_count = lax.axis_size("dp")
     assert seqs == 1
     length = piece * groups
     share = width // groups
     heads = share // HEAD_DIM
+    here = w_query.shape[0]
     block = min(512, length)
+    chunks = 2
     tokens = hidden_in.reshape(piece, width)
     mem = memory.reshape(piece, width)
     grad_out = cotangent.reshape(piece, width)
 
-    def gather_all(value):
-        return lax.all_gather(value, ALL, axis=0, tiled=True)
-
     def gather_dp(value):
         return lax.all_gather(value, "dp", axis=0, tiled=True)
 
-    def to_heads(value):
-        return lax.all_to_all(value, "seq", split_axis=0, concat_axis=0, tiled=True)
+    def pieces(value):
+        return [value[i * piece // chunks : (i + 1) * piece // chunks] for i in range(chunks)]
 
     attend_forward, attend_backward = attention_calls(length, heads, block)
     start, low, high = document_bounds(segments[0], block)
-
-    hidden32 = tokens.astype(F32)
-    rstd_in = rms_scale(hidden32)
-    normed_in = hidden32 * rstd_in
-    gain_attn32 = gather_all(gain_attn).astype(F32)
-    gain_ffn32 = gather_all(gain_ffn).astype(F32)
-    attn_in = (normed_in * gain_attn32).astype(BF16)
-
-    key_rows = gather_all(w_key)
-    value_rows = gather_all(w_value)
-    query_rows = gather_all(w_query)
-    out_rows = gather_all(w_out)
-
-    def project(left, rows):
-        return jnp.einsum(
-            "td,dge->gte", left, rows.reshape(width, groups, share), preferred_element_type=F32
-        ).astype(BF16)
-
     flat = (length, share)
     split = (groups, piece, share)
-    key = to_heads(project(mem, key_rows)).reshape(flat)
-    value = to_heads(project(mem, value_rows)).reshape(flat)
-    query = to_heads(project(attn_in, query_rows)).reshape(flat)
+
+    attn_in, gain_rows, key, value, query, _, key_rows, value_rows, query_rows, out_rows = project_call(
+        dp_count, groups, piece, width, here
+    )(tokens, mem, gain_tile(gain_attn, gain_ffn), w_key, w_value, w_query, w_out)
+    gain_attn32, gain_ffn32 = gain_rows[0], gain_rows[1]
+    key, value, query = [part.reshape(flat) for part in (key, value, query)]
+    key_rows, value_rows, query_rows, out_rows = [
+        rows.reshape(width, width) for rows in (key_rows, value_rows, query_rows, out_rows)
+    ]
+
+    units = w_gate.shape[0]
+    padded = -(-units // 16) * 16
+
+    units_here = jnp.pad(jnp.stack((w_gate, w_up, w_down)), ((0, 0), (0, padded - units), (0, 0)))
+    units_all = lax.all_gather(units_here, "seq", axis=0, tiled=False)
+    gate_rows, up_rows, down_rows = [units_all[:, i].reshape(groups * padded, width) for i in range(3)]
+    dy = [gather_dp(part) for part in pieces(grad_out)]
+
     context_heads, lse = attend_forward(low, start, query, key, value)
-    context = to_heads(context_heads.reshape(split))
-
-    out_split = out_rows.reshape(groups, share, width)
-    mid = hidden32 + jnp.einsum("gte,ged->td", context, out_split, preferred_element_type=F32)
+    context = exchange_call(dp_count, groups, piece, width, False)(context_heads.reshape(split))
+
+    hidden32 = tokens.astype(F32)
+    mid = hidden32 + mxu(context, out_rows, NN)
     rstd_mid = rms_scale(mid)
     normed_mid = mid * rstd_mid
     ffn_in = (normed_mid * gain_ffn32).astype(BF16)
 
-    def gather_units(weight):
-        return lax.all_gather(weight, "seq", axis=0, tiled=True)
-
-    gate_rows, up_rows, down_rows = gather_units(w_gate), gather_units(w_up), gather_units(w_down)
-    dy = gather_dp(grad_out)
-    ffn_all = gather_dp(ffn_in)
-    gate = mxu(ffn_all, gate_rows, NT)
-    up = mxu(ffn_all, up_rows, NT)
-    sig = jax.nn.sigmoid(gate)
-    act = (gate * sig * up).astype(BF16)
-    grad_act = mxu(dy, down_rows, NT)
-    grad_gate = (grad_act * up * sig * (1.0 + gate * (1.0 - sig))).astype(BF16)
-    grad_up = (grad_act * gate * sig).astype(BF16)
-
     def scatter_dp(value):
         return lax.psum_scatter(value, "dp", scatter_dimension=0, tiled=True)
 
-    grad_ffn_in = scatter_dp((mxu(grad_gate, gate_rows, NN) + mxu(grad_up, up_rows, NN)).astype(BF16)).astype(F32)
-    branch = scatter_dp(mxu(act, down_rows, NN).astype(BF16)).astype(F32)
-    layer_out = (mid + branch).astype(BF16)
-
-    def scatter_units(value):
-        return lax.psum_scatter(value.astype(BF16), "seq", scatter_dimension=0, tiled=True).astype(F32)
-
-    grad_w_down = scatter_units(mxu(act, dy, TN))
-    grad_w_gate = scatter_units(mxu(grad_gate, ffn_all, TN))
-    grad_w_up = scatter_units(mxu(grad_up, ffn_all, TN))
+    ffn_all = [gather_dp(part) for part in pieces(ffn_in)]
+    acts, grad_gates, grad_ups, scattered = [], [], [], []
+    for part, dy_part in zip(ffn_all, dy):
+        gate = mxu(part, gate_rows, NT)
+        up = mxu(part, up_rows, NT)
+        sig = jax.nn.sigmoid(gate)
+        acts.append((gate * sig * up).astype(BF16))
+        grad_act = mxu(dy_part, down_rows, NT)
+        grad_gates.append((grad_act * up * sig * (1.0 + gate * (1.0 - sig))).astype(BF16))
+        grad_ups.append((grad_act * gate * sig).astype(BF16))
+        scattered.append(
+            scatter_dp((mxu(grad_gates[-1], gate_rows, NN) + mxu(grad_ups[-1], up_rows, NN)).astype(BF16))
+        )
+
+    first, acts, grad_gates, grad_ups = lax.optimization_barrier((scattered[0], acts, grad_gates, grad_ups))
+
+    def unit_terms(lefts, rights):
+        return sum(mxu(left, right, TN) for left, right in zip(lefts, rights)).astype(BF16)
+
+    terms = [unit_terms(acts, dy), unit_terms(grad_gates, ffn_all), unit_terms(grad_ups, ffn_all)]
+    branches = [mxu(act, down_rows, NN).astype(BF16) for act in acts]
+    second, terms, branches = lax.optimization_barrier((scattered[1], terms, branches))
+    grad_ffn_in = jnp.concatenate((first, second)).astype(F32)
+    terms = [lax.psum_scatter(term, "seq", scatter_dimension=0, tiled=True) for term in terms]
+    branches = [scatter_dp(part) for part in branches]
 
     grad_gain_ffn_all = jnp.sum(normed_mid * grad_ffn_in, axis=0)
     grad_mid = grad_out.astype(F32) + norm_back(grad_ffn_in, normed_mid, rstd_mid, gain_ffn32)
     grad_branch = grad_mid.astype(BF16)
-    grad_context = jnp.einsum("td,ged->gte", grad_branch, out_split, preferred_element_type=F32).astype(BF16)
-    grad_context_heads = to_heads(grad_context).reshape(flat)
+    grad_context = mxu(grad_branch, out_rows, NT).astype(BF16)
+    grad_context_heads = exchange_call(dp_count, groups, piece, width, True)(grad_context).reshape(flat)
     dq, dk, dv = attend_backward(high, start, query, key, value, context_heads, grad_context_heads, lse)
-    dq, dk, dv = [to_heads(part.reshape(split)) for part in (dq, dk, dv)]
-
-    def unproject(part, rows):
-        return jnp.einsum(
-            "gte,dge->td", part, rows.reshape(width, groups, share), preferred_element_type=F32
-        )
-
-    grad_attn_in = unproject(dq, query_rows)
-    grad_memory = unproject(dk, key_rows) + unproject(dv, value_rows)
-    grad_gain_attn_all = jnp.sum(normed_in * grad_attn_in, axis=0)
-    grad_hidden = grad_mid + norm_back(grad_attn_in, normed_in, rstd_in, gain_attn32)
-
-    def weight_term(left, part):
-        return jnp.einsum("td,gte->dge", left, part, preferred_element_type=F32).reshape(width, width)
-
-    def scatter_rows(value):
-        part = lax.psum_scatter(value.astype(BF16), "dp", scatter_dimension=0, tiled=True)
-        return lax.psum_scatter(part, "seq", scatter_dimension=0, tiled=True).astype(F32)
-
-    grad_w_out = scatter_rows(
-        jnp.einsum("gte,td->ged", context, grad_branch, preferred_element_type=F32).reshape(width, width)
+
+    gain_term = jnp.pad(grad_gain_ffn_all[None], ((0, 7), (0, 0)))
+    _, _, _, grad_w_out, grad_w_value, grad_w_key, grad_w_query, grad_memory, grad_hidden, gains = reduce_call(
+        dp_count, groups, piece, width, here
+    )(
+        context, mem, attn_in, gain_rows, gain_term, grad_branch, dv.reshape(split), dk.reshape(split),
+        dq.reshape(split), value_rows, key_rows, query_rows, tokens, grad_mid,
     )
-    grad_w_query = scatter_rows(weight_term(attn_in, dq))
-    grad_w_key = scatter_rows(weight_term(mem, dk))
-    grad_w_value = scatter_rows(weight_term(mem, dv))
-
-    gains = lax.psum((grad_gain_attn_all, grad_gain_ffn_all), ALL)
-    owner = lax.axis_index("dp") * groups + lax.axis_index("seq")
-    here = gain_attn.shape[0]
-    grad_gain_attn, grad_gain_ffn = [lax.dynamic_slice_in_dim(g, owner * here, here) for g in gains]
+    gains, terms, branches, mid = lax.optimization_barrier((gains, terms, branches, mid))
+    grad_w_down, grad_w_gate, grad_w_up = [term[:units].astype(F32) for term in terms]
+    layer_out = (mid + jnp.concatenate(branches).astype(F32)).astype(BF16)
+    grad_gain_attn, grad_gain_ffn = gains[0, :here], gains[1, :here]
     cube = (seqs, piece, width)
     return (
         layer_out.reshape(cube),

time: 1850 us -> 1350 us (0.73)
  Pallas kernels: 72.3 us -> 878 us
  waiting for transfers between devices: 796 us -> 164 us
  blocking collectives: 465 us -> 0 us
  local copies, waits for them, and re-layouts: 110 us -> 26.2 us
  matrix products: 302 us -> 224 us
  starting transfers between devices: 32 us -> 0.48 us
    pallas_call x0 -> x4, Pallas kernels: none -> 806 us  [the longest x1 368 us: shards(): project_call(dp_count, groups, piece, width, here)]
    unnamed x2 -> x0, blocking collectives: 272 us -> none
    all_gather x7 -> x1, waiting for transfers between devices: 253 us -> 0.02 us  [shards(): units_all = lax.all_gather(units_here, 'seq', axis=0, tiled=False)]
    all_to_all x5 -> x0, waiting for transfers between devices: 176 us -> none  [to_heads(): return lax.all_to_all(value, 'seq', split_axis=0, concat_axis=0, tiled=True)]
    all_to_all x3 -> x0, blocking collectives: 154 us -> none  [to_heads(): return lax.all_to_all(value, 'seq', split_axis=0, concat_axis=0, tiled=True)]
    reduce_scatter x2 -> x4, waiting for transfers between devices: 210 us -> 59.5 us  [scatter_dp(): return lax.psum_scatter(value, 'dp', scatter_dimension=0, tiled=True)]
    dot_general x12 -> x0, matrix products: 113 us -> none  [the longest x3 31.4 us: unproject(): jnp.einsum('gte,dge->td', part, rows.reshape(width, groups, share), prefe...]
    all_gather x2 -> x4, waiting for transfers between devices: 146 us -> 101 us  [gather_dp(): return lax.all_gather(value, 'dp', axis=0, tiled=True)]
  transfers between devices with their start and end apart: 27 -> 12, of which waited for: 12 -> 5; matrix products, arithmetic and copies ran while one was open for 29% -> 19% of each run, Pallas kernels for 4% -> 66%
where the time goes in v2:
time: 1350 us; the launch traced here: 1340 us
  Pallas kernels  878 us (65%)
  matrix products  224 us (17%)
  waiting for transfers between devices  164 us (12%)
  other arithmetic  28.5 us (2%)
  local copies, waits for them, and re-layouts  26.2 us (2%)
  between operations  15.1 us (1%)
    pallas_call x1, Pallas kernels, shards(): project_call(dp_count, groups, piece, width, here)  368 us
    pallas_call x1, Pallas kernels, shards(): reduce_call(dp_count, groups, piece, width, here)  336 us
    dot_general x20, matrix products, mxu(): return lax.dot_general(left, right, dims, preferred_element_type=F32)  224 us
    all_gather x4, waiting for transfers between devices, gather_dp(): return lax.all_gather(value, 'dp', axis=0, tiled=True)  101 us
    pallas_call x1, Pallas kernels, shards(): exchange_call(dp_count, groups, piece, width, True)(grad_context)  63.5 us
    reduce_scatter x4, waiting for transfers between devices, scatter_dp(): return lax.psum_scatter(value, 'dp', scatter_dimension=0, tiled=True)  59.5 us
    pallas_call x1, Pallas kernels, shards(): attend_backward(high, start, query, key, value, context_heads, grad_conte...  42.8 us
    pallas_call x1, Pallas kernels, shards(): exchange_call(dp_count, groups, piece, width, False)  38.5 us
  transfers between devices with their start and end apart: 12, of which 5 were waited for; matrix products, arithmetic and copies ran while one was open for 19% of the time, Pallas kernels for 66%

profile of v2, /device:TPU:0, one launch (start us, length us, event | category | flops | bytes accessed | tf_op | source)
XLA Modules:
  0.0 1335.7 jit_solution(18001696052059780105)
XLA Ops:
  12.3 367.6 %gather_project.1 = (bf16[512,2048]{1,0:T(8,128)(2,1)S(1)}, f32[8,2048]{1,0:T(8,128)S(1)}, bf16[4,512,512]{2,1,0:T(8,128)(2,1)S(1)}, bf16[4,512,512]{2,1,0:T(8,1...) custom-call(bf16[512,2048]{1,0:T(8,128)(2,1)} %bitcast.140, ...), custom_call_target="tpu_custom_call" | custom-call | flops 274877906944 | bytes 67108864 | tf_op jit(solution)/shard_map/gather_project/pallas_call | solution.py:937
  382.5 7.2 fusion.1
  390.4 29.6 %attend_forward.1 = (bf16[2048,512]{1,0:T(8,128)(2,1)}, f32[4,1,2048]{2,1,0:T(1,128)}) custom-call(s32[4]{0:T(128)} %and_select_fusion.1.low_ref, s32[1,2048]{1,0:T(1,128)} %bitcast.159, bf16[2048,512]{1,0:T(8,128)(2,1)} %bitcast.152, bf16[2048,512]{1,0:T(8,128)(2,1)} %bitcast.114, bf16[2048,512]{1,0:T(8,128)(2,1)} %bitcast.150), custom_call_target="tpu_custom_call" | custom-call | flops 34359738368 | bytes 8388608 | tf_op jit(solution)/shard_map/attend_forward/pallas_call | solution.py:954
  420.0 38.5 %collect_features.1.context = bf16[512,2048]{1,0:T(8,128)(2,1)} custom-call(bf16[4,512,512]{2,1,0:T(8,128)(2,1)} %bitcast.154), custom_call_target="tpu_custom_call" | custom-call | flops 8589934592 | bytes 4194304 | tf_op jit(solution)/shard_map/collect_features/pallas_call | solution.py:955
  458.5 8.0 multiply_reduce_fusion
  476.0 10.1 fusion.8
  486.1 48.2 %all-gather.9.cloned.1.call-done = bf16[2048,2048]{1,0:T(8,128)(2,1)} async-done(((bf16[256,2048]{1,0:T(8,128)(2,1)}), bf16[2048,2048]{1,0:T(8,128)(2,1)}) %all-gather.9.cloned.1.call-update) | async-done | bytes 8388624 | tf_op jit(solution)/shard_map/all_gather | solution.py:927
  534.4 11.1 fusion.47
  545.5 13.4 %multiply_convert_fusion.1 = (bf16[2048,704]{0,1:T(8,128)(2,1)}, bf16[2048,704]{0,1:T(8,128)(2,1)}, bf16[2048,704]{0,1:T(8,128)(2,1)}) fusion(f32[2048,704]{0,1:T(8,128)} %fusion.47, f32[704,2048]{1,0:T(8,128)} %fusion.8, bf16[2048,2048]{1,0:T(8,128)(2,1)S(1)} %copy-done.32, bf16[704,2048]{1,0:T(8,128)(2,1)S(1)} %bitcast.123), kind=kOutput, calls=%fused_computation.35 | convolution fusion | flops 5928648704 | bytes 31457280 | tf_op jit(solution)/shard_map/dot_general | solution.py:25
  558.9 12.6 fusion.48
  571.6 12.7 add_convert_fusion.1
  584.4 6.2 all-gather.17.cloned.1.call-done
  590.5 10.2 fusion.4
  600.8 46.5 %all-gather.11.cloned.1.call-done = bf16[2048,2048]{1,0:T(8,128)(2,1)} async-done(((bf16[256,2048]{1,0:T(8,128)(2,1)}), bf16[2048,2048]{1,0:T(8,128)(2,1)}) %all-gather.11.cloned.1.call-update) | async-done | bytes 8388624 | tf_op jit(solution)/shard_map/all_gather | solution.py:927
  647.3 11.1 fusion.49
  658.4 14.5 %multiply_convert_fusion = (bf16[2048,704]{0,1:T(8,128)(2,1)}, bf16[2048,704]{0,1:T(8,128)(2,1)}, bf16[2048,704]{0,1:T(8,128)(2,1)}) fusion(f32[2048,704]{0,1:T(8,128)} %fusion.49, f32[704,2048]{1,0:T(8,128)} %fusion.4, bf16[2048,2048]{1,0:T(8,128)(2,1)S(1)} %copy-done.33, bf16[704,2048]{1,0:T(8,128)(2,1)S(1)} %bitcast.125), kind=kOutput, calls=%fused_computation.33 | convolution fusion | flops 5928648704 | bytes 31457280 | tf_op jit(solution)/shard_map/dot_general | solution.py:25
  672.9 12.4 fusion.50
  685.3 12.9 add_convert_fusion
  698.3 23.6 %reduce-scatter.8.cloned.1.call-done = bf16[256,2048]{1,0:T(8,128)(2,1)} async-done(((bf16[2048,2048]{1,0:T(8,128)(2,1)}), bf16[256,2048]{1,0:T(8,128)(2,1)}) %reduce-scatter.8.cloned.1.call-update) | async-done | bytes 1048592 | tf_op jit(solution)/shard_map/reduce_scatter | solution.py:964
  721.9 10.0 fusion.52
  731.9 12.1 add_convert_fusion.2
  744.0 9.5 fusion.51
  753.6 10.9 add_convert_fusion.3
  764.5 9.8 fusion.2
  774.3 11.2 add_convert_fusion.4
  785.5 10.9 convolution_convert_fusion
  796.4 10.9 convolution_convert_fusion.1
  821.5 9.1 convolution_convert_fusion.2.source
  830.6 63.5 %spread_features.1 = bf16[4,512,512]{2,1,0:T(8,128)(2,1)} custom-call(bf16[512,2048]{1,0:T(8,128)(2,1)} %convolution_convert_fusion.2.source), custom_call_target="tpu_custom_call" | custom-call | flops 8589934592 | bytes 4194304 | tf_op jit(solution)/shard_map/spread_features/pallas_call | solution.py:996
  894.2 42.8 %attend_backward.1 = (bf16[2048,512]{1,0:T(8,128)(2,1)}, bf16[2048,512]{1,0:T(8,128)(2,1)}, bf16[2048,512]{1,0:T(8,128)(2,1)}) custom-call(s32[4]{0:T(128)} %fusion.41.high_ref, s32[1,2048]{1,0:T(1,128)} %bitcast.160, bf16[2048,512]{1,0:T(8,128)(2,1)} %bitcast.153, bf16[2048,512]{1,0:T(8,128)(2,1)} %bitcast.115, bf16[2048,512]{1,0:T(8,128)(2,1)} %bitcast.151, ...), custom_call_target="tpu_custom_call" | custom-call | flops 51539607552 | bytes 16777216 | tf_op jit(solution)/shard_map/attend_backward/pallas_call | solution.py:997
  937.0 336.4 %weight_gradients.1 = (bf16[4,512,512]{2,1,0:T(8,128)(2,1)}, bf16[4,512,512]{2,1,0:T(8,128)(2,1)}, bf16[4,512,512]{2,1,0:T(8,128)(2,1)}, f32[64,2048]{1,0:T(8,12...) custom-call(bf16[512,2048]{1,0:T(8,128)(2,1)} %collect_features.1.co, ...), custom_call_target="tpu_custom_call" | custom-call | flops 274877906944 | bytes 67108864 | tf_op jit(solution)/shard_map/weight_gradients/pallas_call | solution.py:1000
  1273.5 35.9 %reduce-scatter.20.cloned.1.call-done = bf16[256,2048]{1,0:T(8,128)(2,1)} async-done(((bf16[2048,2048]{1,0:T(8,128)(2,1)}), bf16[256,2048]{1,0:T(8,128)(2,1)}) %reduce-scatter.20.cloned.1.call-update) | async-done | bytes 1048592 | tf_op jit(solution)/shard_map/reduce_scatter | solution.py:964
  (141 shorter events, 51.1 us)
Async XLA Ops:
  7.2 463.2 %all-gather.13.cloned.1.call-start = ((), (), s32[]{:S(2)}) async-start(), calls=%async_computation.16 | async-start | bytes 10813440 | tf_op jit(solution)/shard_map/all_gather | solution.py:950
  10.6 465.4 %all-gather.15.cloned.1.call-start = ((), (), s32[]{:S(2)}) async-start(), calls=%async_computation.17 | async-start | bytes 9437184 | tf_op jit(solution)/shard_map/all_gather | solution.py:927
  12.1 522.2 %all-gather.9.cloned.1.call-start = ((), (), s32[]{:S(2)}) async-start(), calls=%async_computation.7 | async-start | bytes 9437184 | tf_op jit(solution)/shard_map/all_gather | solution.py:927
  12.3 370.3 %copy-start.35 = (s32[1,2048]{1,0:T(1,128)S(1)}, s32[1,2048]{1,0:T(1,128)}, u32[]{:S(2)}) copy-start(s32[1,2048]{1,0:T(1,128)} %param.15) | copy-start | bytes 24580
  382.5 37.4 %copy-start = (f32[8,2048]{1,0:T(8,128)}, f32[8,2048]{1,0:T(8,128)S(1)}, u32[]{:S(2)}) copy-start(f32[8,2048]{1,0:T(8,128)S(1)} %get-tuple-element.58.gain_rows) | copy-start | bytes 196612
  389.8 76.7 %copy-start.26 = (f32[1,2048]{1,0:T(1,128)}, f32[1,2048]{1,0:T(1,128)S(1)}, u32[]{:S(2)}) copy-start(f32[1,2048]{1,0:T(1,128)S(1)} %slice.55) | copy-start | bytes 24580
  420.0 38.5 %copy-start.34 = (bf16[1,512,2048]{2,1,0:T(8,128)(2,1)S(1)}, bf16[1,512,2048]{2,1,0:T(8,128)(2,1)}, u32[]{:S(2)}) copy-start(bf16[1,512,2048]{2,1,0:T(8,128)(2,1)} %param.13) | copy-start | bytes 6291460
  469.2 121.4 %all-gather.17.cloned.1.call-start = ((), (), s32[]{:S(2)}) async-start(), calls=%async_computation.18 | async-start | bytes 9437184 | tf_op jit(solution)/shard_map/all_gather | solution.py:927
  469.7 177.5 %all-gather.11.cloned.1.call-start = ((), (), s32[]{:S(2)}) async-start(), calls=%async_computation.9 | async-start | bytes 9437184 | tf_op jit(solution)/shard_map/all_gather | solution.py:927
  470.3 251.6 %reduce-scatter.8.cloned.1.call-start = ((), (), s32[]{:S(2)}) async-start(), calls=%async_computation.8 | async-start | bytes 9437184 | tf_op jit(solution)/shard_map/reduce_scatter | solution.py:964
  534.4 11.1 copy-start.15
  534.4 11.1 copy-start.32
  545.5 13.4 %copy-start.17 = (bf16[4,1,176,2048]{3,2,1,0:T(8,128)(2,1)S(1)}, bf16[4,1,176,2048]{3,2,1,0:T(8,128)(2,1)}, u32[]{:S(2)}) copy-start(bf16[4,1,176,2048]{3,2,1,0:T(8,128)(2,1)} %get-tuple-element.106) | copy-start | bytes 8650756
  558.9 12.7 copy-start.38
  584.3 223.0 %reduce-scatter.10.cloned.1.call-start = ((), (), s32[]{:S(2)}) async-start(), calls=%async_computation.10 | async-start | bytes 9437184 | tf_op jit(solution)/shard_map/reduce_scatter | solution.py:964
  647.3 11.1 copy-start.16
  647.3 11.1 copy-start.33
  658.4 14.5 %copy-start.18 = (bf16[4,1,176,2048]{3,2,1,0:T(8,128)(2,1)S(1)}, bf16[4,1,176,2048]{3,2,1,0:T(8,128)(2,1)}, u32[]{:S(2)}) copy-start(bf16[4,1,176,2048]{3,2,1,0:T(8,128)(2,1)} %get-tuple-element.106) | copy-start | bytes 8650756
  672.9 12.4 copy-start.39
  698.2 575.2 %reduce-scatter.12.cloned.1.call-start = ((), (), s32[]{:S(2)}) async-start(), calls=%async_computation.11 | async-start | bytes 3604480 | tf_op jit(solution)/shard_map/reduce_scatter | solution.py:989
  721.9 10.0 copy-start.40
  744.0 9.5 copy-start.37
  764.5 9.8 copy-start.41
  807.3 466.1 %reduce-scatter.14.cloned.1.call-start = ((), (), s32[]{:S(2)}) async-start(), calls=%async_computation.12 | async-start | bytes 3604480 | tf_op jit(solution)/shard_map/reduce_scatter | solution.py:989
  808.0 465.4 %reduce-scatter.16.cloned.1.call-start = ((), (), s32[]{:S(2)}) async-start(), calls=%async_computation.13 | async-start | bytes 3604480 | tf_op jit(solution)/shard_map/reduce_scatter | solution.py:989
  808.7 464.8 %reduce-scatter.18.cloned.1.call-start = ((), (), s32[]{:S(2)}) async-start(), calls=%async_computation.14 | async-start | bytes 9437184 | tf_op jit(solution)/shard_map/reduce_scatter | solution.py:964
  809.4 6.4 copy-start.11
  809.4 500.0 %reduce-scatter.20.cloned.1.call-start = ((), (), s32[]{:S(2)}) async-start(), calls=%async_computation.15 | async-start | bytes 9437184 | tf_op jit(solution)/shard_map/reduce_scatter | solution.py:964
  810.4 5.4 copy-start.8
  1273.5 42.9 %copy-start.20 = (bf16[256,2048]{1,0:T(8,128)(2,1)S(1)}, bf16[256,2048]{1,0:T(8,128)(2,1)}, u32[]{:S(2)}) copy-start(bf16[256,2048]{1,0:T(8,128)(2,1)} %reduce-scatter.18.cloned.1.call-done) | copy-start | bytes 3145732
  1309.4 7.0 copy-start.9
  1309.4 7.0 copy-start.21
  (22 other events, 50.2 us)
Sparse Core Ops, SparseCore 0:
  10.7 235.1 all-gather.12
  248.3 86.0 all-gather.14
  469.3 65.0 all-gather.8
  536.1 54.3 all-gather.16
  592.8 54.3 all-gather.10
  650.6 71.2 reduce-scatter.7
  725.7 71.2 reduce-scatter.9
  807.4 89.0 reduce-scatter.11
  898.8 59.3 reduce-scatter.13
  960.4 101.2 reduce-scatter.15
  1065.2 163.3 reduce-scatter.17
  1232.3 76.9 reduce-scatter.19

commit v3 on v2

--- a/solution.py
+++ b/solution.py
@@ -193,7 +193,11 @@
         self.sibling = {"dp": self.dp + 1 - 2 * self.core, "seq": self.seq}
 
     def chip_at(self, step):
-        return lax.rem(self.chip + step, self.chips)
+        chip, bit = self.chip, 1
+        while bit < self.chips:
+            chip = chip + (step // bit % 2) * bit * (1 - 2 * lax.rem(self.chip // bit, 2))
+            bit *= 2
+        return chip
 
     def chip_device(self, chip):
         return {"dp": 2 * chip + self.core, "seq": self.seq}
@@ -215,17 +219,23 @@
 
 
 def project_kernel(
-    dp_count, groups, hidden, memory, gains, w_key, w_value, w_query, w_out,
+    dp_count, groups, hidden, memory, gains, w_key, w_value, w_query, w_out, w_gate, w_up, w_down, grad,
     attn_in, gain_rows, key, value, query, all_gains, all_key, all_value, all_query, all_out,
+    all_gate, all_up, all_down, all_grad,
     weight, parts, line_send, line_recv, chip_send, chip_recv, core_send, core_recv,
     own_sem, load_sem, part_send, part_recv, part_own,
+    dy_own, dy_chip_send, dy_chip_recv, dy_core_send, dy_core_recv,
 ):
     place = Place(dp_count, groups)
     chips, seq = place.chips, place.seq
-    shards = (gains, w_key, w_value, w_query, w_out)
-    wholes = (all_gains, all_key, all_value, all_query, all_out)
-    count = len(shards)
-    own = place.dp * groups + seq
+    shards = (gains, w_key, w_value, w_query, w_out, w_gate, w_up, w_down)
+    wholes = (all_gains, all_key, all_value, all_query, all_out, all_gate, all_up, all_down)
+    count = 5
+    whole_own = place.dp * groups + seq
+
+    def own_block(m):
+        return whole_own if m < count else seq
+
     above, below = seq < groups - 1, seq > 0
     up, down = place.line_device(lax.rem(seq + 1, groups)), place.line_device(lax.rem(seq + groups - 1, groups))
 
@@ -254,9 +264,10 @@
         to_sibling(m, src, wholes[m].at[block], 0).start()
 
     def own_copy(m):
-        return pltpu.make_async_copy(shards[m], wholes[m].at[own], own_sem.at[m])
+        return pltpu.make_async_copy(shards[m], wholes[m].at[own_block(m)], own_sem.at[m])
 
     def start_own(m):
+        own = own_block(m)
         own_copy(m).start()
 
         @pl.when(above)
@@ -267,12 +278,13 @@
         def _():
             along(m, shards[m], own, 1, False).start()
 
-        spread(m, shards[m], own)
+        if m < count:
+            spread(m, shards[m], own)
 
     def serve_line(m):
         for distance in range(1, groups):
             for upward in (True, False):
-                block = own - distance if upward else own + distance
+                block = own_block(m) - distance if upward else own_block(m) + distance
                 there = seq >= distance if upward else seq < groups - distance
                 onward = above if upward else below
 
@@ -285,11 +297,52 @@
                     def _():
                         along(m, landed, block, distance + 1, upward).start()
 
-                    spread(m, landed, block)
+                    if m < count:
+                        spread(m, landed, block)
+
+    chunks = all_grad.shape[0]
+    chunk_rows = grad.shape[0] // chunks
+
+    def grad_rows(chunk):
+        return grad.at[pl.ds(chunk * chunk_rows, chunk_rows), :]
+
+    def grad_own(chunk):
+        return pltpu.make_async_copy(grad_rows(chunk), all_grad.at[chunk, place.dp], dy_own.at[chunk])
+
+    def grad_to_chip(chunk, step):
+        return remote(
+            grad_rows(chunk), all_grad.at[chunk, place.dp], dy_chip_send.at[chunk, step - 1],
+            dy_chip_recv.at[chunk, step - 1], place.chip_device(place.chip_at(step)),
+        )
+
+    def grad_to_sibling(chunk, step):
+        dp = 2 * place.chip_at(step) + place.core
+        src = all_grad.at[chunk, dp] if step > 0 else grad_rows(chunk)
+        return remote(
+            src, all_grad.at[chunk, dp], dy_core_send.at[chunk, step], dy_core_recv.at[chunk, step], place.sibling
+        )
+
+    def start_grad(chunk):
+        grad_own(chunk).start()
+        for step in range(1, chips):
+            grad_to_chip(chunk, step).start()
+        grad_to_sibling(chunk, 0).start()
+
+    def serve_grad(chunk):
+        for step in range(1, chips):
+            grad_to_chip(chunk, step).wait_recv()
+            grad_to_sibling(chunk, step).start()
+
+    def finish_grad(chunk):
+        grad_own(chunk).wait()
+        for step in range(1, chips):
+            grad_to_chip(chunk, step).wait_send()
+        for step in range(chips):
+            grad_to_sibling(chunk, step).wait()
 
     def serve_chips(m):
         for step in range(1, chips):
-            dp = 2 * lax.rem(place.chip + chips - step, chips) + place.core
+            dp = 2 * place.chip_at(step) + place.core
             remote(
                 line(m, dp), line(m, dp), chip_send.at[m, step - 1], chip_recv.at[m, step - 1], place.sibling
             ).wait_recv()
@@ -297,7 +350,7 @@
 
     def finish(m):
         for step in range(chips):
-            dp = 2 * lax.rem(place.chip + chips - step, chips) + 1 - place.core
+            dp = 2 * place.chip_at(step) + 1 - place.core
             to_sibling(m, line(m, dp), line(m, dp), step).wait_recv()
         own_copy(m).wait()
 
@@ -369,26 +422,40 @@
     serve_line(0)
     start_own(2)
     serve_line(1)
+    start_own(3)
     serve_chips(0)
+    serve_line(2)
+    start_own(4)
     serve_chips(1)
-    start_own(3)
-    serve_line(2)
     finish(0)
     normalize()
+    serve_line(3)
+    start_own(5)
     finish(1)
     project(1)
+    serve_line(4)
+    start_own(6)
+    for chunk in range(chunks):
+        start_grad(chunk)
     serve_chips(2)
-    start_own(4)
-    serve_line(3)
     finish(2)
     project(2)
+    serve_line(5)
+    start_own(7)
     serve_chips(3)
-    serve_line(4)
     finish(3)
     project(3)
+    serve_line(6)
     serve_chips(4)
+    serve_line(7)
+    for chunk in range(chunks):
+        serve_grad(chunk)
     finish(4)
-    for m in range(count):
+    for chunk in range(chunks):
+        finish_grad(chunk)
+    for m in range(count, len(shards)):
+        own_copy(m).wait()
+    for m in range(len(shards)):
         for distance in range(1, groups):
             for upward in (True, False):
                 came = seq >= distance - 1 if upward else seq < groups - distance + 1
@@ -396,8 +463,10 @@
 
                 @pl.when(came & onward)
                 def _():
-                    along(m, wholes[m].at[own], own, distance, upward).wait_send()
-
+                    along(m, wholes[m].at[own_block(m)], own_block(m), distance, upward).wait_send()
+
+        if m >= count:
+            continue
         mine = line(m, place.dp)
         for step in range(1, chips):
             remote(
@@ -411,7 +480,7 @@
             part_copy(m, step).wait()
 
 
-def project_call(dp_count, groups, piece, width, here):
+def project_call(dp_count, groups, piece, width, here, padded, chunks):
     chips = dp_count // 2
     blocks = dp_count * groups
     share = width // groups
@@ -419,25 +488,29 @@
     vmem = pl.BlockSpec(memory_space=pltpu.VMEM)
     heads = jax.ShapeDtypeStruct((groups, piece, share), BF16)
     whole = jax.ShapeDtypeStruct((blocks, here, width), BF16)
+    units = jax.ShapeDtypeStruct((groups, padded, width), BF16)
     dma = pltpu.SemaphoreType.DMA
+    others = max(chips - 1, 1)
     return pl.pallas_call(
         functools.partial(project_kernel, dp_count, groups),
-        in_specs=[vmem, vmem, hbm, hbm, hbm, hbm, hbm],
-        out_specs=[vmem, vmem, hbm, hbm, hbm, vmem, hbm, hbm, hbm, hbm],
+        in_specs=[vmem, vmem] + [hbm] * 9,
+        out_specs=[vmem, vmem, hbm, hbm, hbm, vmem] + [hbm] * 8,
         out_shape=(
             jax.ShapeDtypeStruct((piece, width), BF16),
             jax.ShapeDtypeStruct((8, width), F32),
             heads, heads, heads,
             jax.ShapeDtypeStruct((blocks, 8, 128), F32),
-            whole, whole, whole, whole,
+            whole, whole, whole, whole, units, units, units,
+            jax.ShapeDtypeStruct((chunks, dp_count, piece // chunks, width), BF16),
         ),
         scratch_shapes=[
             pltpu.VMEM((blocks, here, width), BF16),
             pltpu.VMEM((3, groups, piece, share), BF16),
-            dma((5, 2, groups)), dma((5, 2, groups)),
-            dma((5, max(chips - 1, 1))), dma((5, max(chips - 1, 1))),
+            dma((8, 2, groups)), dma((8, 2, groups)),
+            dma((5, others)), dma((5, others)),
             dma((5, chips)), dma((5, chips)),
-            dma((5,)), dma, dma((3, groups - 1)), dma((3, groups - 1)), dma((3,)),
+            dma((8,)), dma, dma((3, groups - 1)), dma((3, groups - 1)), dma((3,)),
+            dma((chunks,)), dma((chunks, others)), dma((chunks, others)), dma((chunks, chips)), dma((chunks, chips)),
         ],
         compiler_params=pltpu.CompilerParams(
             collective_id=1, has_side_effects=True, vmem_limit_bytes=48 * 1024 * 1024
@@ -592,9 +665,9 @@
                 line_own[m] = total
         if m + 2 < count:
             for step in range(1, chips):
-                behind = lax.rem(place.chip + chips - step, chips)
+                partner = place.chip_at(step)
                 pl.semaphore_signal(
-                    chip_free.at[step - 1], inc=1, device_id=place.chip_device(behind), device_id_type=BY_MESH
+                    chip_free.at[step - 1], inc=1, device_id=place.chip_device(partner), device_id_type=BY_MESH
                 )
 
     def store_grad(m):
@@ -857,52 +930,522 @@
     )
 
 
-def exchange_kernel(dp_count, groups, spread, source, target, send_sem, recv_sem, own_sem):
+def middle_kernel(
+    dp_count, groups,
+    gain_rows, hidden, context_heads, grad_own, out_rows, gate_rows, up_rows, down_rows, all_grad,
+    context, gain_term, mid_out, grad_mid, grad_branch, grad_heads, branch, grad_down, grad_gate, grad_up,
+    all_ffn, acts, grad_gates, grad_ups, core_in, chip_in, term_in,
+    gate_w, up_w, down_w, out_w, mid, ffn_in, own_total, term_buf,
+    col_send, col_recv, col_own, weight_sem, out_sem, mid_sem, chip_send, chip_recv, core_send, core_recv, own_sem,
+    x_sem, dy_sem, act_sem, sum_send, sum_recv, load_sem, far_send, far_recv, branch_sem, left_sem, right_sem,
+    term_send, term_recv, rows_sem, gm_sem, gb_sem, head_send, head_recv, head_own,
+):
     place = Place(dp_count, groups)
-    share = source.shape[1] // groups if spread else source.shape[2]
-    everyone = pltpu.get_barrier_semaphore()
+    chips, seq, core = place.chips, place.seq, place.core
+    piece, width = hidden.shape
+    share = width // groups
+    unit_rows = gate_rows.shape[0]
+    padded = gate_w.shape[0]
+    wide = (gate_rows, up_rows, down_rows)
+    kept = (gate_w, up_w, down_w)
+
+    def weight_copy(i):
+        return pltpu.make_async_copy(wide[i], kept[i].at[pl.ds(0, unit_rows), :], weight_sem.at[i])
+
+    def group_columns(group):
+        return pl.ds(pl.multiple_of(group * share, share), share)
+
+    def out_copy(group, slot):
+        rows = pl.ds(pl.multiple_of(group * share, share), share)
+        return pltpu.make_async_copy(out_rows.at[rows, :], out_w.at[slot], out_sem.at[slot])
+
+    def collect(step):
+        other = place.line_at(step)
+        return remote(
+            context_heads.at[other], context.at[:, group_columns(seq)], col_send.at[step - 1], col_recv.at[step - 1],
+            place.line_device(other),
+        )
+
+    def came_from(step):
+        return lax.rem(seq + groups - step, groups)
+
+    place.barrier()
     for step in range(1, groups):
-        pl.semaphore_signal(
-            everyone, inc=1, device_id=place.line_device(place.line_at(step)), device_id_type=BY_MESH
+        collect(step).start()
+    own_columns = pltpu.make_async_copy(context_heads.at[seq], context.at[:, group_columns(seq)], col_own)
+    own_columns.start()
+    out_copy(seq, 0).start()
+    hidden_copy = pltpu.make_async_copy(hidden, ffn_in, own_sem)
+    hidden_copy.start()
+    for i in range(3):
+        weight_copy(i).start()
+        if padded > unit_rows:
+            kept[i][unit_rows:, :] = jnp.zeros((padded - unit_rows, width), BF16)
+
+    for step in range(groups):
+        slot = step % 2
+        group = came_from(step)
+        if step + 1 < groups:
+            out_copy(came_from(step + 1), 1 - slot).start()
+        if step == 0:
+            own_columns.wait()
+        else:
+            columns = context.at[:, group_columns(group)]
+            remote(columns, columns, col_send.at[step - 1], col_recv.at[step - 1], place.sibling).wait_recv()
+        out_copy(group, slot).wait()
+        left = context[:, group_columns(group)]
+        if step == 0:
+            hidden_copy.wait()
+
+        def project(part, _, left=left, slot=slot, step=step):
+            columns = pl.ds(pl.multiple_of(part * share, share), share)
+            value = mxu(left, out_w[slot, :, columns], NN)
+            if step == 0:
+                mid[:, columns] = ffn_in[:, columns].astype(F32) + value
+            else:
+                mid[:, columns] += value
+            return 0
+
+        lax.fori_loop(0, groups, project, 0)
+
+    some = min(64, piece)
+    batches = piece // some
+
+    def batch(index):
+        return pl.ds(pl.multiple_of(index * some, some), some)
+
+    def normalize(index, _):
+        rows = batch(index)
+        x = mid[rows, :]
+        rstd = lax.rsqrt(jnp.mean(x * x, axis=-1, keepdims=True) + EPSILON)
+        ffn_in[rows, :] = (x * rstd * gain_rows[1:2, :]).astype(BF16)
+        return 0
+
+    lax.fori_loop(0, batches, normalize, 0)
+    mid_copy = pltpu.make_async_copy(mid, mid_out, mid_sem)
+    mid_copy.start()
+
+    def to_chip(step):
+        return remote(
+            ffn_in, all_ffn.at[place.dp], chip_send.at[step - 1], chip_recv.at[step - 1],
+            place.chip_device(place.chip_at(step)),
         )
-    pl.semaphore_wait(everyone, groups - 1)
-
-    def columns(group):
-        return pl.ds(pl.multiple_of(group * share, share), share)
-
-    def ends(other):
-        if spread:
-            return source.at[:, columns(other)], target.at[place.seq]
-        return source.at[other], target.at[:, columns(place.seq)]
-
-    def copy(step):
+
+    def to_sibling(step):
+        dp = 2 * place.chip_at(step) + core
+        return remote(all_ffn.at[dp], all_ffn.at[dp], core_send.at[step], core_recv.at[step], place.sibling)
+
+    own_ffn = pltpu.make_async_copy(ffn_in, all_ffn.at[place.dp], own_sem)
+    own_ffn.start()
+    for step in range(1, chips):
+        to_chip(step).start()
+    own_ffn.wait()
+    to_sibling(0).start()
+    for i in range(3):
+        weight_copy(i).wait()
+
+    pieces = 2 * chips
+    stored = (acts, grad_gates, grad_ups)
+
+    def piece_of(u, own_first):
+        step, which = u // 2, u % 2
+        mine = 1 - which if own_first else which
+        return step, which, 2 * place.chip_at(step) + mine * core + (1 - mine) * (1 - core)
+
+    def hidden_units(x_buf, dy_buf, act_buf):
+        def x_copy(u):
+            dp = piece_of(u, True)[2]
+            return pltpu.make_async_copy(all_ffn.at[dp], x_buf, x_sem)
+
+        def dy_copy(u):
+            dp = piece_of(u, True)[2]
+            return pltpu.make_async_copy(all_grad.at[dp], dy_buf.at[u % 2], dy_sem.at[u % 2])
+
+        def act_copy(u, i):
+            dp = piece_of(u, True)[2]
+            return pltpu.make_async_copy(act_buf.at[u % 2, i], stored[i].at[dp], act_sem.at[u % 2, i])
+
+        dy_copy(0).start()
+
+        def one(u, _):
+            step, which, dp = piece_of(u, True)
+            slot = u % 2
+
+            @pl.when((which == 0) & (step > 0))
+            def _():
+                to_chip(step).wait_recv()
+                to_sibling(step).start()
+
+            @pl.when(which == 1)
+            def _():
+                to_sibling(step).wait_recv()
+
+            x_copy(u).start()
+
+            @pl.when(u + 1 < pieces)
+            def _():
+                dy_copy(u + 1).start()
+
+            @pl.when(u >= 2)
+            def _():
+                for i in range(3):
+                    act_copy(u - 2, i).wait()
+
+            dy_copy(u).wait()
+            grad_act = mxu(dy_buf[slot], down_w[...], NT)
+            x_copy(u).wait()
+            gate = mxu(x_buf[...], gate_w[...], NT)
+            up = mxu(x_buf[...], up_w[...], NT)
+            sig = 1.0 / (1.0 + jnp.exp(-gate))
+            act_buf[slot, 0] = (gate * sig * up).astype(BF16)
+            act_buf[slot, 1] = (grad_act * up * sig * (1.0 + gate * (1.0 - sig))).astype(BF16)
+            act_buf[slot, 2] = (grad_act * gate * sig).astype(BF16)
+            for i in range(3):
+                act_copy(u, i).start()
+            return 0
+
+        lax.fori_loop(0, pieces, one, 0)
+        for u in range(max(pieces - 2, 0), pieces):
+            for i in range(3):
+                act_copy(u, i).wait()
+
+    pl.run_scoped(
+        hidden_units,
+        pltpu.VMEM((piece, width), BF16), pltpu.VMEM((2, piece, width), BF16), pltpu.VMEM((2, 3, piece, padded), BF16),
+    )
+
+    block = unit_rows // groups
+
+    def term_copy(i, step):
         other = place.line_at(step)
-        src, dst = ends(other)
-        return remote(src, dst, send_sem.at[step - 1], recv_sem.at[step - 1], place.line_device(other))
-
-    own = pltpu.make_async_copy(*ends(place.seq), own_sem)
+        return remote(
+            term_buf.at[i, pl.ds(other * block, block), :], term_in.at[i, step - 1], term_send.at[i, step - 1],
+            term_recv.at[i, step - 1], place.line_device(other),
+        )
+
+    def weight_terms(left_buf, acc):
+        for i, (lefts, rights) in enumerate(((acts, all_grad), (grad_gates, all_ffn), (grad_ups, all_ffn))):
+
+            def copies(dp, slot, lefts=lefts, rights=rights):
+                return (
+                    pltpu.make_async_copy(lefts.at[dp], left_buf.at[slot], left_sem.at[slot]),
+                    pltpu.make_async_copy(rights.at[dp], out_w.at[slot], right_sem.at[slot]),
+                )
+
+            for copy in copies(0, 0):
+                copy.start()
+
+            def one(dp, _, copies=copies):
+                slot = dp % 2
+
+                @pl.when(dp + 1 < dp_count)
+                def _():
+                    for copy in copies(dp + 1, 1 - slot):
+                        copy.start()
+
+                for copy in copies(dp, slot):
+                    copy.wait()
+                left = left_buf[slot].T
+
+                def part_of(part, _):
+                    columns = group_columns(part)
+                    value = jnp.dot(left, out_w[slot, :, columns], preferred_element_type=F32)
+
+                    @pl.when(dp == 0)
+                    def _():
+                        acc[:, columns] = value
+
+                    @pl.when(dp > 0)
+                    def _():
+                        acc[:, columns] += value
+
+                    return 0
+
+                lax.fori_loop(0, groups, part_of, 0)
+                return 0
+
+            lax.fori_loop(0, dp_count, one, 0)
+            term_buf[i] = acc[0:unit_rows, :].astype(BF16)
+            for step in range(1, groups):
+                term_copy(i, step).start()
+
+    pl.run_scoped(weight_terms, pltpu.VMEM((2, piece, padded), BF16), pltpu.VMEM((padded, width), F32))
+
+    def sum_copy(core_out, step):
+        return remote(core_out, core_in.at[step], sum_send, sum_recv.at[step], place.sibling)
+
+    def far_copy(chip_out, step):
+        return remote(
+            chip_out.at[step % 2], chip_in.at[step - 1], far_send.at[step % 2], far_recv.at[step - 1],
+            place.chip_device(place.chip_at(step)),
+        )
+
+    def back_to_input(act_buf, core_out, chip_out, load_buf, branch_buf):
+        def place_of(u):
+            _, which, dp = piece_of(pieces - 2 + u - 4 * (u // 2), False)
+            return chips - 1 - u // 2, which, dp
+
+        def act_copy(u, i):
+            dp = place_of(u)[2]
+            return pltpu.make_async_copy(stored[i].at[dp], act_buf.at[u % 2, i], act_sem.at[u % 2, i])
+
+        def branch_copy(u):
+            dp = place_of(u)[2]
+            return pltpu.make_async_copy(branch_buf.at[u % 2], branch.at[dp], branch_sem.at[u % 2])
+
+        def load_copy(step):
+            return pltpu.make_async_copy(core_in.at[step], load_buf, load_sem)
+
+        for i in range(3):
+            act_copy(0, i).start()
+
+        def one(u, _):
+            step, which, dp = place_of(u)
+            slot = u % 2
+
+            @pl.when(u + 1 < pieces)
+            def _():
+                for i in range(3):
+                    act_copy(u + 1, i).start()
+
+            for i in range(3):
+                act_copy(u, i).wait()
+
+            @pl.when(u >= 2)
+            def _():
+                branch_copy(u - 2).wait()
+
+            def branch_of(part, _):
+                columns = group_columns(part)
+                branch_buf[slot, :, columns] = mxu(act_buf[slot, 0], down_w[:, columns], NN).astype(BF16)
+                return 0
+
+            @pl.when((which == 0) & (u >= 2))
+            def _():
+                sum_copy(core_out, step + 1).wait_send()
+
+            @pl.when(which == 1)
+            def _():
+                lax.fori_loop(0, groups, branch_of, 0)
+                sum_copy(core_out, step).wait_recv()
+                load_copy(step).start()
+
+                @pl.when((step > 0) & (step < chips - 2))
+                def _():
+                    far_copy(chip_out, step + 2).wait_send()
+
+                load_copy(step).wait()
+
+            def columns_of(part, _):
+                columns = group_columns(part)
+                value = mxu(act_buf[slot, 1], gate_w[:, columns], NN) + mxu(act_buf[slot, 2], up_w[:, columns], NN)
+
+                @pl.when(which == 0)
+                def _():
+                    core_out[:, columns] = value.astype(BF16)
+
+                @pl.when((which == 1) & (step > 0))
+                def _():
+                    chip_out[step % 2, :, columns] = (value + load_buf[:, columns].astype(F32)).astype(BF16)
+
+                @pl.when((which == 1) & (step == 0))
+                def _():
+                    own_total[:, columns] = value + load_buf[:, columns].astype(F32)
+
+                return 0
+
+            lax.fori_loop(0, groups, columns_of, 0)
+
+            @pl.when(which == 0)
+            def _():
+                sum_copy(core_out, step).start()
+                lax.fori_loop(0, groups, branch_of, 0)
+
+            @pl.when((which == 1) & (step > 0))
+            def _():
+                far_copy(chip_out, step).start()
+
+            branch_copy(u).start()
+            return 0
+
+        lax.fori_loop(0, pieces, one, 0)
+        for u in range(max(pieces - 2, 0), pieces):
+            branch_copy(u).wait()
+        sum_copy(core_out, 0).wait_send()
+        for step in range(1, min(chips, 3)):
+            far_copy(chip_out, step).wait_send()
+
+    pl.run_scoped(
+        back_to_input,
+        pltpu.VMEM((2, 3, piece, padded), BF16), pltpu.VMEM((piece, width), BF16), pltpu.VMEM((2, piece, width), BF16),
+        pltpu.VMEM((piece, width), BF16), pltpu.VMEM((2, piece, width), BF16),
+    )
+
+    for step in range(1, chips):
+        landed = chip_in.at[step - 1]
+        remote(landed, landed, far_send.at[0], far_recv.at[step - 1], place.sibling).wait_recv()
+    for step in range(1, chips):
+        to_chip(step).wait_send()
+    mid_copy.wait()
+    gain_term[...] = jnp.zeros_like(gain_term)
+
+    def norm_and_heads(rows_buf, mid_buf, heads_buf, sum_buf):
+        def rows_copy(index, step, slot):
+            source = grad_own.at[batch(index), :] if step == 0 else chip_in.at[step - 1, batch(index), :]
+            return pltpu.make_async_copy(source, rows_buf.at[slot, step], rows_sem.at[slot, step])
+
+        def grad_mid_copy(index, slot):
+            return pltpu.make_async_copy(mid_buf.at[slot], grad_mid.at[batch(index), :], gm_sem.at[slot])
+
+        for step in range(chips):
+            rows_copy(0, step, 0).start()
+
+        def norm_back(index, _):
+            slot = index % 2
+
+            @pl.when(index + 1 < batches)
+            def _():
+                for step in range(chips):
+                    rows_copy(index + 1, step, 1 - slot).start()
+
+            for step in range(chips):
+                rows_copy(index, step, slot).wait()
+
+            @pl.when(index >= 2)
+            def _():
+                grad_mid_copy(index - 2, slot).wait()
+
+            rows = batch(index)
+            grad = own_total[rows, :]
+            for step in range(1, chips):
+                grad = grad + rows_buf[slot, step].astype(F32)
+            x = mid[rows, :]
+            rstd = lax.rsqrt(jnp.mean(x * x, axis=-1, keepdims=True) + EPSILON)
+            normed = x * rstd
+            gain_term[0:1, :] += jnp.sum(normed * grad, axis=0, keepdims=True)
+            scaled = grad * gain_rows[1:2, :]
+            shift = jnp.mean(scaled * normed, axis=-1, keepdims=True)
+            total = rows_buf[slot, 0].astype(F32) + rstd * (scaled - normed * shift)
+            mid_buf[slot] = total
+            ffn_in[rows, :] = total.astype(BF16)
+            grad_mid_copy(index, slot).start()
+            return 0
+
+        lax.fori_loop(0, batches, norm_back, 0)
+        grad_branch_copy = pltpu.make_async_copy(ffn_in, grad_branch, gb_sem)
+        grad_branch_copy.start()
+        for index in range(max(batches - 2, 0), batches):
+            grad_mid_copy(index, index % 2).wait()
+
+        def head_copy(step):
+            other = place.line_at(step)
+            return remote(
+                heads_buf.at[other], grad_heads.at[seq], head_send.at[step - 1], head_recv.at[step - 1],
+                place.line_device(other),
+            )
+
+        own_heads = pltpu.make_async_copy(heads_buf.at[seq], grad_heads.at[seq], head_own)
+        order = tuple(range(1, groups)) + (0,)
+        out_copy(place.line_at(order[0]), 0).start()
+        for at, step in enumerate(order):
+            group = place.line_at(step)
+            if at + 1 < groups:
+                out_copy(place.line_at(order[at + 1]), (at + 1) % 2).start()
+            out_copy(group, at % 2).wait()
+            heads_buf[group] = mxu(ffn_in[...], out_w[at % 2], NT).astype(BF16)
+            if step > 0:
+                head_copy(step).start()
+            else:
+                own_heads.start()
+
+        for i, target in enumerate((grad_down, grad_gate, grad_up)):
+            for step in range(1, groups):
+                term_copy(i, step).wait()
+
+                def sum_load(step=step, i=i):
+                    return pltpu.make_async_copy(term_in.at[i, step - 1], sum_buf.at[step - 1], rows_sem.at[0, 0])
+
+                sum_load().start()
+                sum_load().wait()
+            total = term_buf[i, pl.ds(pl.multiple_of(seq * block, block), block), :].astype(F32)
+            for step in range(1, groups):
+                total = total + sum_buf[step - 1].astype(F32)
+            mid[0:block, :] = total
+            store = pltpu.make_async_copy(mid.at[pl.ds(0, block), :], target, gm_sem.at[0])
+            store.start()
+            store.wait()
+        grad_branch_copy.wait()
+        own_heads.wait()
+        for step in range(1, groups):
+            head_copy(step).wait()
+
+    pl.run_scoped(
+        norm_and_heads,
+        pltpu.VMEM((2, chips, some, width), BF16), pltpu.VMEM((2, some, width), F32),
+        pltpu.VMEM((groups, piece, share), BF16), pltpu.VMEM((groups - 1, block, width), BF16),
+    )
     for step in range(1, groups):
-        copy(step).start()
-    own.start()
-    own.wait()
-    for step in range(1, groups):
-        copy(step).wait()
-
-
-def exchange_call(dp_count, groups, piece, width, spread):
+        collect(step).wait_send()
+    for step in range(chips):
+        to_sibling(step).wait_send()
+
+
+def middle_call(dp_count, groups, piece, width, unit_rows):
+    chips = dp_count // 2
     share = width // groups
+    assert share == piece
+    padded = -(-unit_rows // 128) * 128
+    block = unit_rows // groups
+    others = max(chips - 1, 1)
     hbm = pl.BlockSpec(memory_space=pl.ANY)
+    vmem = pl.BlockSpec(memory_space=pltpu.VMEM)
     dma = pltpu.SemaphoreType.DMA
-    shape = (groups, piece, share) if spread else (piece, width)
+    shape = jax.ShapeDtypeStruct
     return pl.pallas_call(
-        functools.partial(exchange_kernel, dp_count, groups, spread),
-        in_specs=[hbm],
-        out_specs=hbm,
-        out_shape=jax.ShapeDtypeStruct(shape, BF16),
-        scratch_shapes=[dma((groups - 1,)), dma((groups - 1,)), dma],
-        compiler_params=pltpu.CompilerParams(collective_id=3 + spread, has_side_effects=True),
-        cost_estimate=pl.CostEstimate(flops=32 * piece * width * width // 8, transcendentals=0, bytes_accessed=4 * piece * width),
-        name="spread_features" if spread else "collect_features",
+        functools.partial(middle_kernel, dp_count, groups),
+        in_specs=[vmem] + [hbm] * 8,
+        out_specs=[vmem, vmem] + [hbm] * 15,
+        out_shape=(
+            shape((piece, width), BF16),
+            shape((8, width), F32),
+            shape((piece, width), F32),
+            shape((piece, width), F32),
+            shape((piece, width), BF16),
+            shape((groups, piece, share), BF16),
+            shape((dp_count, piece, width), BF16),
+            shape((block, width), F32),
+            shape((block, width), F32),
+            shape((block, width), F32),
+            shape((dp_count, piece, width), BF16),
+            shape((dp_count, piece, padded), BF16),
+            shape((dp_count, piece, padded), BF16),
+            shape((dp_count, piece, padded), BF16),
+            shape((chips, piece, width), BF16),
+            shape((others, piece, width), BF16),
+            shape((3, groups - 1, block, width), BF16),
+        ),
+        scratch_shapes=[
+            pltpu.VMEM((padded, width), BF16), pltpu.VMEM((padded, width), BF16), pltpu.VMEM((padded, width), BF16),
+            pltpu.VMEM((2, share, width), BF16),
+            pltpu.VMEM((piece, width), F32),
+            pltpu.VMEM((piece, width), BF16),
+            pltpu.VMEM((piece, width), F32),
+            pltpu.VMEM((3, unit_rows, width), BF16),
+            dma((groups - 1,)), dma((groups - 1,)), dma, dma((3,)), dma((2,)), dma,
+            dma((others,)), dma((others,)), dma((chips,)), dma((chips,)), dma,
+            dma, dma((2,)), dma((2, 3)),
+            dma, dma((chips,)), dma, dma((2,)), dma((others,)), dma((2,)),
+            dma((2,)), dma((2,)), dma((3, groups - 1)), dma((3, groups - 1)),
+            dma((2, chips)), dma((2,)), dma,
+            dma((groups - 1,)), dma((groups - 1,)), dma,
+        ],
+        compiler_params=pltpu.CompilerParams(
+            collective_id=5, has_side_effects=True, vmem_limit_bytes=63 * 1024 * 1024
+        ),
+        cost_estimate=pl.CostEstimate(
+            flops=128 * piece * width * width, transcendentals=0, bytes_accessed=64 * width * width
+        ),
+        name="feed_forward",
     )
 
 
@@ -918,94 +1461,51 @@
     heads = share // HEAD_DIM
     here = w_query.shape[0]
     block = min(512, length)
-    chunks = 2
     tokens = hidden_in.reshape(piece, width)
     mem = memory.reshape(piece, width)
     grad_out = cotangent.reshape(piece, width)
-
-    def gather_dp(value):
-        return lax.all_gather(value, "dp", axis=0, tiled=True)
-
-    def pieces(value):
-        return [value[i * piece // chunks : (i + 1) * piece // chunks] for i in range(chunks)]
 
     attend_forward, attend_backward = attention_calls(length, heads, block)
     start, low, high = document_bounds(segments[0], block)
     flat = (length, share)
     split = (groups, piece, share)
 
-    attn_in, gain_rows, key, value, query, _, key_rows, value_rows, query_rows, out_rows = project_call(
-        dp_count, groups, piece, width, here
-    )(tokens, mem, gain_tile(gain_attn, gain_ffn), w_key, w_value, w_query, w_out)
-    gain_attn32, gain_ffn32 = gain_rows[0], gain_rows[1]
+    units = w_gate.shape[0]
+    padded = -(-units // 16) * 16
+    own_units = [jnp.pad(weight, ((0, padded - units), (0, 0))) for weight in (w_gate, w_up, w_down)]
+    (
+        attn_in, gain_rows, key, value, query, _, key_rows, value_rows, query_rows, out_rows,
+        gate_rows, up_rows, down_rows, dy,
+    ) = project_call(dp_count, groups, piece, width, here, padded, 1)(
+        tokens, mem, gain_tile(gain_attn, gain_ffn), w_key, w_value, w_query, w_out, *own_units, grad_out
+    )
+    gate_rows, up_rows, down_rows = [
+        rows.reshape(groups * padded, width) for rows in (gate_rows, up_rows, down_rows)
+    ]
     key, value, query = [part.reshape(flat) for part in (key, value, query)]
     key_rows, value_rows, query_rows, out_rows = [
         rows.reshape(width, width) for rows in (key_rows, value_rows, query_rows, out_rows)
     ]
-
-    units = w_gate.shape[0]
-    padded = -(-units // 16) * 16
-
-    units_here = jnp.pad(jnp.stack((w_gate, w_up, w_down)), ((0, 0), (0, padded - units), (0, 0)))
-    units_all = lax.all_gather(units_here, "seq", axis=0, tiled=False)
-    gate_rows, up_rows, down_rows = [units_all[:, i].reshape(groups * padded, width) for i in range(3)]
-    dy = [gather_dp(part) for part in pieces(grad_out)]
-
     context_heads, lse = attend_forward(low, start, query, key, value)
-    context = exchange_call(dp_count, groups, piece, width, False)(context_heads.reshape(split))
-
-    hidden32 = tokens.astype(F32)
-    mid = hidden32 + mxu(context, out_rows, NN)
-    rstd_mid = rms_scale(mid)
-    normed_mid = mid * rstd_mid
-    ffn_in = (normed_mid * gain_ffn32).astype(BF16)
-
-    def scatter_dp(value):
-        return lax.psum_scatter(value, "dp", scatter_dimension=0, tiled=True)
-
-    ffn_all = [gather_dp(part) for part in pieces(ffn_in)]
-    acts, grad_gates, grad_ups, scattered = [], [], [], []
-    for part, dy_part in zip(ffn_all, dy):
-        gate = mxu(part, gate_rows, NT)
-        up = mxu(part, up_rows, NT)
-        sig = jax.nn.sigmoid(gate)
-        acts.append((gate * sig * up).astype(BF16))
-        grad_act = mxu(dy_part, down_rows, NT)
-        grad_gates.append((grad_act * up * sig * (1.0 + gate * (1.0 - sig))).astype(BF16))
-        grad_ups.append((grad_act * gate * sig).astype(BF16))
-        scattered.append(
-            scatter_dp((mxu(grad_gates[-1], gate_rows, NN) + mxu(grad_ups[-1], up_rows, NN)).astype(BF16))
-        )
-
-    first, acts, grad_gates, grad_ups = lax.optimization_barrier((scattered[0], acts, grad_gates, grad_ups))
-
-    def unit_terms(lefts, rights):
-        return sum(mxu(left, right, TN) for left, right in zip(lefts, rights)).astype(BF16)
-
-    terms = [unit_terms(acts, dy), unit_terms(grad_gates, ffn_all), unit_terms(grad_ups, ffn_all)]
-    branches = [mxu(act, down_rows, NN).astype(BF16) for act in acts]
-    second, terms, branches = lax.optimization_barrier((scattered[1], terms, branches))
-    grad_ffn_in = jnp.concatenate((first, second)).astype(F32)
-    terms = [lax.psum_scatter(term, "seq", scatter_dimension=0, tiled=True) for term in terms]
-    branches = [scatter_dp(part) for part in branches]
-
-    grad_gain_ffn_all = jnp.sum(normed_mid * grad_ffn_in, axis=0)
-    grad_mid = grad_out.astype(F32) + norm_back(grad_ffn_in, normed_mid, rstd_mid, gain_ffn32)
-    grad_branch = grad_mid.astype(BF16)
-    grad_context = mxu(grad_branch, out_rows, NT).astype(BF16)
-    grad_context_heads = exchange_call(dp_count, groups, piece, width, True)(grad_context).reshape(flat)
+    (
+        context, gain_term, mid, grad_mid, grad_branch, grad_context_heads, branch, grad_w_down, grad_w_gate, grad_w_up, *_
+    ) = middle_call(dp_count, groups, piece, width, groups * padded)(
+        gain_rows, tokens, context_heads.reshape(split), grad_out, out_rows, gate_rows, up_rows, down_rows,
+        dy.reshape(dp_count, piece, width),
+    )
+    branch = lax.psum_scatter(branch.reshape(dp_count * piece, width), "dp", scatter_dimension=0, tiled=True)
+    grad_context_heads = grad_context_heads.reshape(flat)
     dq, dk, dv = attend_backward(high, start, query, key, value, context_heads, grad_context_heads, lse)
 
-    gain_term = jnp.pad(grad_gain_ffn_all[None], ((0, 7), (0, 0)))
     _, _, _, grad_w_out, grad_w_value, grad_w_key, grad_w_query, grad_memory, grad_hidden, gains = reduce_call(
         dp_count, groups, piece, width, here
     )(
         context, mem, attn_in, gain_rows, gain_term, grad_branch, dv.reshape(split), dk.reshape(split),
         dq.reshape(split), value_rows, key_rows, query_rows, tokens, grad_mid,
     )
-    gains, terms, branches, mid = lax.optimization_barrier((gains, terms, branches, mid))
-    grad_w_down, grad_w_gate, grad_w_up = [term[:units].astype(F32) for term in terms]
-    layer_out = (mid + jnp.concatenate(branches).astype(F32)).astype(BF16)
+    gains, branch, mid = lax.optimization_barrier((gains, branch, mid))
+    grad_w_down, grad_w_gate, grad_w_up = [grad[:units] for grad in (grad_w_down, grad_w_gate, grad_w_up)]
+    layer_out = (mid + branch.astype(F32)).astype(BF16)
     grad_gain_attn, grad_gain_ffn = gains[0, :here], gains[1, :here]
     cube = (seqs, piece, width)
     return (

time: 1350 us -> 1190 us (0.88)
  Pallas kernels: 878 us -> 1130 us
  matrix products: 224 us -> 0 us
  waiting for transfers between devices: 164 us -> 0.04 us
  other arithmetic: 28.5 us -> 13.9 us
    pallas_call x3 -> x2, Pallas kernels: 470 us -> 760 us  [the longest x1 403 us: shards(): middle_call(dp_count, groups, piece, width, groups * padded)]
    dot_general x20 -> x0, matrix products: 224 us -> none  [mxu(): return lax.dot_general(left, right, dims, preferred_element_type=F32)]
    all_gather x5 -> x0, waiting for transfers between devices: 101 us -> none  [the longest x4 101 us: gather_dp(): return lax.all_gather(value, 'dp', axis=0, tiled=True)]
    reduce_scatter x7 -> x1, waiting for transfers between devices: 59.6 us -> 0.02 us  [shards(): lax.psum_scatter(branch.reshape(dp_count * piece, width), 'dp', scatter_d...]
    pallas_call x1, Pallas kernels: 336 us -> 294 us  [shards(): reduce_call(dp_count, groups, piece, width, here)]
  transfers between devices with their start and end apart: 12 -> 1, of which waited for: 5 -> 0; matrix products, arithmetic and copies ran while one was open for 19% -> 0% of each run, Pallas kernels for 66% -> 29%
where the time goes in v3:
time: 1190 us; the launch traced here: 1180 us
  Pallas kernels  1130 us (95%)
  local copies, waits for them, and re-layouts  20 us (2%)
  between operations  14.7 us (1%)
  other arithmetic  13.9 us (1%)
    pallas_call x1, Pallas kernels, shards(): middle_call(dp_count, groups, piece, width, groups * padded)  403 us
    pallas_call x1, Pallas kernels, shards(): project_call(dp_count, groups, piece, width, here, padded, 1)  357 us
    pallas_call x1, Pallas kernels, shards(): reduce_call(dp_count, groups, piece, width, here)  294 us
    pallas_call x1, Pallas kernels, shards(): attend_backward(high, start, query, key, value, context_heads, grad_conte...  42.7 us
    pallas_call x1, Pallas kernels, shards(): context_heads, lse = attend_forward(low, start, query, key, value)  29.5 us
  transfers between devices with their start and end apart: 1, of which 0 were waited for; matrix products, arithmetic and copies ran while one was open for 0% of the time, Pallas kernels for 29%

profile of v3, /device:TPU:0, one launch (start us, length us, event | category | flops | bytes accessed | tf_op | source)
XLA Modules:
  0.0 1175.3 jit_solution(8059316226317064227)
XLA Ops:
  7.2 0.0 reduce-scatter.2.cloned.1.call-start
  7.3 7.8 fusion.1
  15.1 0.1 slice.21
  15.2 0.5 and_select_fusion.1.low_ref
  15.7 1.2 pad.18.w_gate
  16.9 1.2 pad.19.w_up
  18.1 1.2 pad.20.w_down
  19.4 356.6 %gather_project.1 = (bf16[512,2048]{1,0:T(8,128)(2,1)S(1)}, f32[8,2048]{1,0:T(8,128)S(1)}, bf16[4,512,512]{2,1,0:T(8,128)(2,1)}, bf16[4,512,512]{2,1,0:T(8,128)(...) custom-call(bf16[512,2048]{1,0:T(8,128)(2,1)} %bitcast.45, ...), custom_call_target="tpu_custom_call" | custom-call | flops 274877906944 | bytes 67108864 | tf_op jit(solution)/shard_map/gather_project/pallas_call | solution.py:1479
  376.0 0.0 copy-start.4
  376.0 1.3 copy-done.4
  377.3 0.6 copy-done.5
  378.0 29.5 %attend_forward.1 = (bf16[2048,512]{1,0:T(8,128)(2,1)}, f32[4,1,2048]{2,1,0:T(1,128)}) custom-call(s32[4]{0:T(128)} %and_select_fusion.1.low_ref, s32[1,2048]{1,0:T(1,128)} %bitcast.70, bf16[2048,512]{1,0:T(8,128)(2,1)} %bitcast.63, bf16[2048,512]{1,0:T(8,128)(2,1)} %bitcast.59, bf16[2048,512]{1,0:T(8,128)(2,1)} %bitcast.61), custom_call_target="tpu_custom_call" | custom-call | flops 34359738368 | bytes 8388608 | tf_op jit(solution)/shard_map/attend_forward/pallas_call | solution.py:1489
  407.5 403.4 %feed_forward.1 = (bf16[512,2048]{1,0:T(8,128)(2,1)}, f32[8,2048]{1,0:T(8,128)}, f32[512,2048]{1,0:T(8,128)}, f32[512,2048]{1,0:T(8,128)}, bf16[512,2048]{1,0:T(...) custom-call(f32[8,2048]{1,0:T(8,128)} %copy-done.5, ...), custom_call_target="tpu_custom_call" | custom-call | flops 274877906944 | bytes 268435456 | tf_op jit(solution)/shard_map/feed_forward/pallas_call | solution.py:1492
  810.9 0.0 reduce-scatter.2.cloned.1.call-update
  811.0 0.8 slice.22
  811.7 0.5 fusion.10.high_ref
  812.3 42.7 %attend_backward.1 = (bf16[2048,512]{1,0:T(8,128)(2,1)}, bf16[2048,512]{1,0:T(8,128)(2,1)}, bf16[2048,512]{1,0:T(8,128)(2,1)}) custom-call(s32[4]{0:T(128)} %fusion.10.high_ref, s32[1,2048]{1,0:T(1,128)} %bitcast.71, bf16[2048,512]{1,0:T(8,128)(2,1)} %bitcast.64, bf16[2048,512]{1,0:T(8,128)(2,1)} %bitcast.60, bf16[2048,512]{1,0:T(8,128)(2,1)} %bitcast.62, ...), custom_call_target="tpu_custom_call" | custom-call | flops 51539607552 | bytes 16777216 | tf_op jit(solution)/shard_map/attend_backward/pallas_call | solution.py:1498
  854.9 294.3 %weight_gradients.1 = (bf16[4,512,512]{2,1,0:T(8,128)(2,1)}, bf16[4,512,512]{2,1,0:T(8,128)(2,1)}, bf16[4,512,512]{2,1,0:T(8,128)(2,1)}, f32[64,2048]{1,0:T(8,12...) custom-call(bf16[512,2048]{1,0:T(8,128)(2,1)} %get-tuple-element.60., ...), custom_call_target="tpu_custom_call" | custom-call | flops 274877906944 | bytes 67108864 | tf_op jit(solution)/shard_map/weight_gradients/pallas_call | solution.py:1500
  1149.3 0.0 reduce-scatter.2.cloned.1.call-done
  1149.3 1.3 slice_bitcast_fusion
  1150.6 5.0 fusion.2
  1155.6 2.1 copy.34
  1157.8 1.6 copy-done.6
  1159.4 2.1 copy.35
  1161.5 0.0 copy-done.14
  1161.5 0.8 copy.36
  1162.3 0.8 copy.37
  1163.1 0.8 copy.38
  1163.9 0.8 copy.39
  1164.7 1.1 copy.40
  1165.8 1.1 copy.41
  1166.9 1.1 copy.42
  (32 shorter events, 0.1 us)
Async XLA Ops:
  7.2 12.1 %copy-start.15 = (bf16[64]{0:T(256)(128)(2,1)S(1)}, bf16[64]{0:T(256)(128)(2,1)}, u32[]{:S(2)}) copy-start(bf16[64]{0:T(256)(128)(2,1)} %param.21) | copy-start | bytes 388
  7.2 12.1 %copy-start.16 = (bf16[64]{0:T(256)(128)(2,1)S(1)}, bf16[64]{0:T(256)(128)(2,1)}, u32[]{:S(2)}) copy-start(bf16[64]{0:T(256)(128)(2,1)} %param.16) | copy-start | bytes 388
  7.2 12.1 %copy-start.3 = (bf16[64,2048]{1,0:T(8,128)(2,1)S(1)}, bf16[64,2048]{1,0:T(8,128)(2,1)}, u32[]{:S(2)}) copy-start(bf16[64,2048]{1,0:T(8,128)(2,1)} %w_out.1) | copy-start | bytes 786436
  7.2 12.1 %copy-start.1 = (bf16[64,2048]{1,0:T(8,128)(2,1)S(1)}, bf16[64,2048]{1,0:T(8,128)(2,1)}, u32[]{:S(2)}) copy-start(bf16[64,2048]{1,0:T(8,128)(2,1)} %w_value.1) | copy-start | bytes 786436
  7.2 12.1 %copy-start = (bf16[64,2048]{1,0:T(8,128)(2,1)S(1)}, bf16[64,2048]{1,0:T(8,128)(2,1)}, u32[]{:S(2)}) copy-start(bf16[64,2048]{1,0:T(8,128)(2,1)} %w_key.1) | copy-start | bytes 786436
  7.2 12.1 %copy-start.2 = (bf16[64,2048]{1,0:T(8,128)(2,1)S(1)}, bf16[64,2048]{1,0:T(8,128)(2,1)}, u32[]{:S(2)}) copy-start(bf16[64,2048]{1,0:T(8,128)(2,1)} %w_query.1) | copy-start | bytes 786436
  7.2 1142.1 %reduce-scatter.2.cloned.1.call-start = ((), (), s32[]{:S(2)}) async-start(), calls=%async_computation.1 | async-start | bytes 18874368 | tf_op jit(solution)/shard_map/reduce_scatter | solution.py:1496
  15.1 360.9 %copy-start.17 = (s32[2048]{0:T(1024)}, s32[2048]{0:T(1024)S(1)}, u32[]{:S(2)}) copy-start(s32[2048]{0:T(1024)S(1)} %get-tuple-element.89) | copy-start | bytes 24580
  376.0 1.3 copy-start.4
  377.3 0.6 copy-start.5
  1150.6 5.0 copy-start.7
  1155.6 3.7 copy-start.6
  1159.3 2.2 copy-start.14
  1159.3 3.0 copy-start.13
  1159.3 3.8 copy-start.12
  1159.3 4.5 copy-start.11
  1159.4 5.3 copy-start.10
  1161.5 4.3 copy-start.9
  1162.3 4.6 copy-start.8
Sparse Core Ops, SparseCore 0:
  811.1 232.9 reduce-scatter.1

commit v4 on v3

--- a/solution.py
+++ b/solution.py
@@ -9,6 +9,7 @@
 from jax.sharding import PartitionSpec as P
 
 HEAD_DIM = 128
+DOCS = 4
 EPSILON = 1e-06
 MASKED = -1e30
 ALL = ("dp", "seq")
@@ -166,11 +167,13 @@
 
 
 def document_bounds(segment_ids, block):
-    length = segment_ids.shape[0]
-    position = jnp.arange(length, dtype=jnp.int32)
-    same = segment_ids[:, None] == segment_ids[None, :]
-    first = jnp.min(jnp.where(same, position[None, :], length), axis=1)
-    last = jnp.max(jnp.where(same, position[None, :], -1), axis=1)
+    first = jnp.zeros_like(segment_ids)
+    last = jnp.zeros_like(segment_ids)
+    for number in range(DOCS):
+        below = jnp.sum((segment_ids < number).astype(jnp.int32))
+        upto = jnp.sum((segment_ids <= number).astype(jnp.int32))
+        first = jnp.where(segment_ids == number, below, first)
+        last = jnp.where(segment_ids == number, upto - 1, last)
     low = first[::block] // block
     high = last[block - 1 :: block] // block + 1
     return first[None, :], low, high
@@ -934,10 +937,10 @@
     dp_count, groups,
     gain_rows, hidden, context_heads, grad_own, out_rows, gate_rows, up_rows, down_rows, all_grad,
     context, gain_term, mid_out, grad_mid, grad_branch, grad_heads, branch, grad_down, grad_gate, grad_up,
-    all_ffn, acts, grad_gates, grad_ups, core_in, chip_in, term_in,
-    gate_w, up_w, down_w, out_w, mid, ffn_in, own_total, term_buf,
+    all_ffn, grad_acts, acts, grad_gates, grad_ups, core_in, chip_in, term_in,
+    gate_w, up_w, down_w, out_w, mid, ffn_in, own_total, chip_out, term_buf,
     col_send, col_recv, col_own, weight_sem, out_sem, mid_sem, chip_send, chip_recv, core_send, core_recv, own_sem,
-    x_sem, dy_sem, act_sem, sum_send, sum_recv, load_sem, far_send, far_recv, branch_sem, left_sem, right_sem,
+    x_sem, dy_sem, act_sem, sum_send, sum_recv, load_sem, far_send, far_recv, left_sem, right_sem, branch_sem,
     term_send, term_recv, rows_sem, gm_sem, gb_sem, head_send, head_recv, head_own,
 ):
     place = Place(dp_count, groups)
@@ -981,6 +984,39 @@
         weight_copy(i).start()
         if padded > unit_rows:
             kept[i][unit_rows:, :] = jnp.zeros((padded - unit_rows, width), BF16)
+
+    def act_gradients(dy_buf, out_buf):
+        def dy_copy(dp, slot):
+            return pltpu.make_async_copy(all_grad.at[dp], dy_buf.at[slot], dy_sem.at[slot])
+
+        def store(dp, slot):
+            return pltpu.make_async_copy(out_buf.at[slot], grad_acts.at[dp], act_sem.at[slot, 0])
+
+        dy_copy(0, 0).start()
+        weight_copy(2).wait()
+
+        def one(dp, _):
+            slot = dp % 2
+
+            @pl.when(dp + 1 < dp_count)
+            def _():
+                dy_copy(dp + 1, 1 - slot).start()
+
+            dy_copy(dp, slot).wait()
+
+            @pl.when(dp >= 2)
+            def _():
+                store(dp - 2, slot).wait()
+
+            out_buf[slot] = mxu(dy_buf[slot], down_w[...], NT)
+            store(dp, slot).start()
+            return 0
+
+        lax.fori_loop(0, dp_count, one, 0)
+        for dp in range(dp_count - 2, dp_count):
+            store(dp, dp % 2).wait()
+
+    pl.run_scoped(act_gradients, pltpu.VMEM((2, piece, width), BF16), pltpu.VMEM((2, piece, padded), F32))
 
     for step in range(groups):
         slot = step % 2
@@ -1037,12 +1073,19 @@
 
     own_ffn = pltpu.make_async_copy(ffn_in, all_ffn.at[place.dp], own_sem)
     own_ffn.start()
-    for step in range(1, chips):
+    square = chips == 4
+    for step in range(1, 3 if square else chips):
         to_chip(step).start()
     own_ffn.wait()
     to_sibling(0).start()
-    for i in range(3):
+    for i in range(2):
         weight_copy(i).wait()
+
+    def hand_on(step):
+        half = piece // 2
+        dp = 2 * place.chip_at(step) + core
+        rows = all_ffn.at[dp, pl.ds((step - 1) * half, half), :]
+        return remote(rows, rows, chip_send.at[2], chip_recv.at[2], place.chip_device(place.chip_at(3 - step)))
 
     pieces = 2 * chips
     stored = (acts, grad_gates, grad_ups)
@@ -1052,51 +1095,82 @@
         mine = 1 - which if own_first else which
         return step, which, 2 * place.chip_at(step) + mine * core + (1 - mine) * (1 - core)
 
-    def hidden_units(x_buf, dy_buf, act_buf):
+    def hidden_units(x_buf, da_buf, act_buf):
         def x_copy(u):
             dp = piece_of(u, True)[2]
-            return pltpu.make_async_copy(all_ffn.at[dp], x_buf, x_sem)
-
-        def dy_copy(u):
+            return pltpu.make_async_copy(all_ffn.at[dp], x_buf.at[u % 2], x_sem.at[u % 2])
+
+        def da_copy(u):
             dp = piece_of(u, True)[2]
-            return pltpu.make_async_copy(all_grad.at[dp], dy_buf.at[u % 2], dy_sem.at[u % 2])
+            return pltpu.make_async_copy(grad_acts.at[dp], da_buf.at[u % 2], dy_sem.at[u % 2])
 
         def act_copy(u, i):
             dp = piece_of(u, True)[2]
             return pltpu.make_async_copy(act_buf.at[u % 2, i], stored[i].at[dp], act_sem.at[u % 2, i])
 
-        dy_copy(0).start()
+        def fetch(u):
+            step, which, _ = piece_of(u, True)
+            if square:
+
+                @pl.when(u == 2)
+                def _():
+                    for near in (1, 2):
+                        to_chip(near).wait_recv()
+                        to_sibling(near).start()
+                        hand_on(near).start()
+
+                @pl.when(u == 6)
+                def _():
+                    to_chip(3).wait_recv()
+                    to_sibling(3).start()
+
+            else:
+
+                @pl.when((which == 0) & (step > 0))
+                def _():
+                    to_chip(step).wait_recv()
+                    to_sibling(step).start()
+
+            @pl.when(which == 1)
+            def _():
+                to_sibling(step).wait_recv()
+
+            x_copy(u).start()
+
+        da_copy(0).start()
 
         def one(u, _):
-            step, which, dp = piece_of(u, True)
             slot = u % 2
-
-            @pl.when((which == 0) & (step > 0))
-            def _():
-                to_chip(step).wait_recv()
-                to_sibling(step).start()
-
-            @pl.when(which == 1)
-            def _():
-                to_sibling(step).wait_recv()
-
-            x_copy(u).start()
+            ahead = u % 2 == 1
+            if square:
+                ahead = ahead | (u == 4)
+            next_ahead = (u + 1 < pieces) & (u % 2 == 0)
+            if square:
+                next_ahead = next_ahead | (u == 3)
+
+            @pl.when(jnp.logical_not(ahead))
+            def _():
+                fetch(u)
+
+            @pl.when(next_ahead)
+            def _():
+                fetch(u + 1)
 
             @pl.when(u + 1 < pieces)
             def _():
-                dy_copy(u + 1).start()
+                da_copy(u + 1).start()
 
             @pl.when(u >= 2)
             def _():
                 for i in range(3):
                     act_copy(u - 2, i).wait()
 
-            dy_copy(u).wait()
-            grad_act = mxu(dy_buf[slot], down_w[...], NT)
             x_copy(u).wait()
-            gate = mxu(x_buf[...], gate_w[...], NT)
-            up = mxu(x_buf[...], up_w[...], NT)
+            gate = mxu(x_buf[slot], gate_w[...], NT)
+            up = mxu(x_buf[slot], up_w[...], NT)
             sig = 1.0 / (1.0 + jnp.exp(-gate))
+            da_copy(u).wait()
+            grad_act = da_buf[slot]
             act_buf[slot, 0] = (gate * sig * up).astype(BF16)
             act_buf[slot, 1] = (grad_act * up * sig * (1.0 + gate * (1.0 - sig))).astype(BF16)
             act_buf[slot, 2] = (grad_act * gate * sig).astype(BF16)
@@ -1111,17 +1185,171 @@
 
     pl.run_scoped(
         hidden_units,
-        pltpu.VMEM((piece, width), BF16), pltpu.VMEM((2, piece, width), BF16), pltpu.VMEM((2, 3, piece, padded), BF16),
+        pltpu.VMEM((2, piece, width), BF16), pltpu.VMEM((2, piece, padded), F32),
+        pltpu.VMEM((2, 3, piece, padded), BF16),
     )
 
+    def far_copy(step):
+        return remote(
+            chip_out.at[step - 1], chip_in.at[step - 1], far_send.at[step - 1],
+            far_recv.at[step - 1], place.chip_device(place.chip_at(step)),
+        )
+
+    def input_sum(act_buf, core_out, load_buf):
+        sources, rights, own = (grad_gates, grad_ups), (gate_w, up_w), own_total
+        used = len(sources)
+
+        def place_of(u):
+            _, which, dp = piece_of(pieces - 2 + u - 4 * (u // 2), False)
+            return chips - 1 - u // 2, which, dp
+
+        def act_copy(u, i):
+            dp = place_of(u)[2]
+            return pltpu.make_async_copy(sources[i].at[dp], act_buf.at[u % 2, i], act_sem.at[u % 2, i])
+
+        def sum_copy(step):
+            return remote(
+                core_out, core_in.at[step], sum_send, sum_recv.at[step], place.sibling
+            )
+
+        def load_copy(step):
+            return pltpu.make_async_copy(core_in.at[step], load_buf, load_sem)
+
+        for i in range(used):
+            act_copy(0, i).start()
+
+        def one(u, _):
+            step, which, dp = place_of(u)
+            slot = u % 2
+
+            @pl.when(u + 1 < pieces)
+            def _():
+                for i in range(used):
+                    act_copy(u + 1, i).start()
+
+            for i in range(used):
+                act_copy(u, i).wait()
+
+            @pl.when((which == 0) & (u >= 2))
+            def _():
+                sum_copy(step + 1).wait_send()
+
+            @pl.when(which == 1)
+            def _():
+                sum_copy(step).wait_recv()
+                load_copy(step).start()
+                load_copy(step).wait()
+
+            def columns_of(part, _):
+                columns = group_columns(part)
+                value = mxu(act_buf[slot, 0], rights[0][:, columns], NN)
+                for i in range(1, used):
+                    value = value + mxu(act_buf[slot, i], rights[i][:, columns], NN)
+
+                @pl.when(which == 0)
+                def _():
+                    core_out[:, columns] = value.astype(BF16)
+
+                @pl.when((which == 1) & (step > 0))
+                def _():
+                    chip_out[step - 1, :, columns] = (value + load_buf[:, columns].astype(F32)).astype(BF16)
+
+                @pl.when((which == 1) & (step == 0))
+                def _():
+                    own[:, columns] = value + load_buf[:, columns].astype(F32)
+
+                return 0
+
+            lax.fori_loop(0, groups, columns_of, 0)
+
+            @pl.when(which == 0)
+            def _():
+                sum_copy(step).start()
+
+            @pl.when((which == 1) & (step > 0))
+            def _():
+                far_copy(step).start()
+
+            return 0
+
+        lax.fori_loop(0, pieces, one, 0)
+        sum_copy(0).wait_send()
+
     block = unit_rows // groups
+
+    paired = groups == 4
+    side = seq // 2
+    inner = (seq == 1) | (seq == 2)
+    partner = seq + 1 - 2 * (seq % 2)
+
+    def across(j):
+        return 2 * (1 - side) + j
+
+    def term_rows(i, owner):
+        return term_buf.at[i, pl.ds(pl.multiple_of(owner * block, block), block), :]
 
     def term_copy(i, step):
         other = place.line_at(step)
         return remote(
-            term_buf.at[i, pl.ds(other * block, block), :], term_in.at[i, step - 1], term_send.at[i, step - 1],
-            term_recv.at[i, step - 1], place.line_device(other),
-        )
+            term_rows(i, other), term_in.at[i, step - 1], term_send.at[i, step - 1], term_recv.at[i, step - 1],
+            place.line_device(other),
+        )
+
+    def near_copy(i):
+        return remote(
+            term_rows(i, partner), term_in.at[i, 0], term_send.at[i, 0], term_recv.at[i, 0], place.line_device(partner)
+        )
+
+    def relay_copy(i, j):
+        return remote(
+            term_rows(i, across(j)), term_in.at[i, 2 + j], term_send.at[i, 1 + j], term_recv.at[i, 2 + j],
+            place.line_device(partner),
+        )
+
+    def across_copy(i, j):
+        return remote(
+            term_rows(i, across(j)), term_in.at[i, 1], term_send.at[i, 1 + j], term_recv.at[i, 1],
+            place.line_device(across(j)),
+        )
+
+    def send_term(i):
+        if paired:
+            near_copy(i).start()
+
+            @pl.when(jnp.logical_not(inner))
+            def _():
+                for j in range(2):
+                    relay_copy(i, j).start()
+
+        else:
+            for step in range(1, groups):
+                term_copy(i, step).start()
+
+    def relay_term(i, buf):
+        if not paired:
+            return
+
+        @pl.when(inner)
+        def _():
+            for j in range(2):
+                relay_copy(i, j).wait_recv()
+                load = pltpu.make_async_copy(term_in.at[i, 2 + j], buf, left_sem.at[0])
+                load.start()
+                load.wait()
+                rows = pl.ds(pl.multiple_of(across(j) * block, block), block)
+                term_buf[i, rows, :] = (term_buf[i, rows, :].astype(F32) + buf[...].astype(F32)).astype(BF16)
+                across_copy(i, j).start()
+
+    def arrived_terms(i):
+        if not paired:
+            for step in range(1, groups):
+                term_copy(i, step).wait()
+            return range(groups - 1)
+        near_copy(i).wait()
+        across_copy(i, 0).wait_recv()
+        for j in range(2):
+            across_copy(i, j).wait_send()
+        return range(2)
 
     def weight_terms(left_buf, acc):
         for i, (lefts, rights) in enumerate(((acts, all_grad), (grad_gates, all_ffn), (grad_ups, all_ffn))):
@@ -1147,143 +1375,71 @@
                     copy.wait()
                 left = left_buf[slot].T
 
-                def part_of(part, _):
-                    columns = group_columns(part)
-                    value = jnp.dot(left, out_w[slot, :, columns], preferred_element_type=F32)
-
-                    @pl.when(dp == 0)
-                    def _():
-                        acc[:, columns] = value
-
-                    @pl.when(dp > 0)
-                    def _():
-                        acc[:, columns] += value
-
-                    return 0
-
-                lax.fori_loop(0, groups, part_of, 0)
+
+                @pl.when(dp == 0)
+                def _():
+                    acc[...] = jnp.zeros_like(acc)
+
+                acc[...] += jnp.dot(left, out_w[slot], preferred_element_type=F32)
                 return 0
 
             lax.fori_loop(0, dp_count, one, 0)
             term_buf[i] = acc[0:unit_rows, :].astype(BF16)
-            for step in range(1, groups):
-                term_copy(i, step).start()
+            send_term(i)
 
     pl.run_scoped(weight_terms, pltpu.VMEM((2, piece, padded), BF16), pltpu.VMEM((padded, width), F32))
 
-    def sum_copy(core_out, step):
-        return remote(core_out, core_in.at[step], sum_send, sum_recv.at[step], place.sibling)
-
-    def far_copy(chip_out, step):
-        return remote(
-            chip_out.at[step % 2], chip_in.at[step - 1], far_send.at[step % 2], far_recv.at[step - 1],
-            place.chip_device(place.chip_at(step)),
-        )
-
-    def back_to_input(act_buf, core_out, chip_out, load_buf, branch_buf):
-        def place_of(u):
-            _, which, dp = piece_of(pieces - 2 + u - 4 * (u // 2), False)
-            return chips - 1 - u // 2, which, dp
-
-        def act_copy(u, i):
-            dp = place_of(u)[2]
-            return pltpu.make_async_copy(stored[i].at[dp], act_buf.at[u % 2, i], act_sem.at[u % 2, i])
-
-        def branch_copy(u):
-            dp = place_of(u)[2]
-            return pltpu.make_async_copy(branch_buf.at[u % 2], branch.at[dp], branch_sem.at[u % 2])
-
-        def load_copy(step):
-            return pltpu.make_async_copy(core_in.at[step], load_buf, load_sem)
-
-        for i in range(3):
-            act_copy(0, i).start()
-
-        def one(u, _):
-            step, which, dp = place_of(u)
-            slot = u % 2
-
-            @pl.when(u + 1 < pieces)
-            def _():
-                for i in range(3):
-                    act_copy(u + 1, i).start()
-
-            for i in range(3):
-                act_copy(u, i).wait()
-
-            @pl.when(u >= 2)
-            def _():
-                branch_copy(u - 2).wait()
-
-            def branch_of(part, _):
+    pl.run_scoped(
+        input_sum,
+        pltpu.VMEM((2, 2, piece, padded), BF16), pltpu.VMEM((piece, width), BF16), pltpu.VMEM((piece, width), BF16),
+    )
+
+    def branch_parts(relay_buf, act_buf, branch_buf):
+        relay_term(0, relay_buf)
+
+        def act_copy(dp, slot):
+            return pltpu.make_async_copy(acts.at[dp], act_buf.at[slot], act_sem.at[slot, 0])
+
+        def branch_copy(dp, slot):
+            return pltpu.make_async_copy(branch_buf.at[slot], branch.at[dp], branch_sem.at[slot])
+
+        act_copy(0, 0).start()
+
+        def one(dp, _):
+            slot = dp % 2
+
+            @pl.when(dp + 1 < dp_count)
+            def _():
+                act_copy(dp + 1, 1 - slot).start()
+
+            act_copy(dp, slot).wait()
+
+            @pl.when(dp >= 2)
+            def _():
+                branch_copy(dp - 2, slot).wait()
+
+            def part_of(part, _):
                 columns = group_columns(part)
-                branch_buf[slot, :, columns] = mxu(act_buf[slot, 0], down_w[:, columns], NN).astype(BF16)
+                branch_buf[slot, :, columns] = mxu(act_buf[slot], down_w[:, columns], NN).astype(BF16)
                 return 0
 
-            @pl.when((which == 0) & (u >= 2))
-            def _():
-                sum_copy(core_out, step + 1).wait_send()
-
-            @pl.when(which == 1)
-            def _():
-                lax.fori_loop(0, groups, branch_of, 0)
-                sum_copy(core_out, step).wait_recv()
-                load_copy(step).start()
-
-                @pl.when((step > 0) & (step < chips - 2))
-                def _():
-                    far_copy(chip_out, step + 2).wait_send()
-
-                load_copy(step).wait()
-
-            def columns_of(part, _):
-                columns = group_columns(part)
-                value = mxu(act_buf[slot, 1], gate_w[:, columns], NN) + mxu(act_buf[slot, 2], up_w[:, columns], NN)
-
-                @pl.when(which == 0)
-                def _():
-                    core_out[:, columns] = value.astype(BF16)
-
-                @pl.when((which == 1) & (step > 0))
-                def _():
-                    chip_out[step % 2, :, columns] = (value + load_buf[:, columns].astype(F32)).astype(BF16)
-
-                @pl.when((which == 1) & (step == 0))
-                def _():
-                    own_total[:, columns] = value + load_buf[:, columns].astype(F32)
-
-                return 0
-
-            lax.fori_loop(0, groups, columns_of, 0)
-
-            @pl.when(which == 0)
-            def _():
-                sum_copy(core_out, step).start()
-                lax.fori_loop(0, groups, branch_of, 0)
-
-            @pl.when((which == 1) & (step > 0))
-            def _():
-                far_copy(chip_out, step).start()
-
-            branch_copy(u).start()
+            lax.fori_loop(0, groups, part_of, 0)
+            branch_copy(dp, slot).start()
             return 0
 
-        lax.fori_loop(0, pieces, one, 0)
-        for u in range(max(pieces - 2, 0), pieces):
-            branch_copy(u).wait()
-        sum_copy(core_out, 0).wait_send()
-        for step in range(1, min(chips, 3)):
-            far_copy(chip_out, step).wait_send()
+        lax.fori_loop(0, dp_count, one, 0)
+        for dp in range(dp_count - 2, dp_count):
+            branch_copy(dp, dp % 2).wait()
+        relay_term(1, relay_buf)
 
     pl.run_scoped(
-        back_to_input,
-        pltpu.VMEM((2, 3, piece, padded), BF16), pltpu.VMEM((piece, width), BF16), pltpu.VMEM((2, piece, width), BF16),
-        pltpu.VMEM((piece, width), BF16), pltpu.VMEM((2, piece, width), BF16),
+        branch_parts,
+        pltpu.VMEM((block, width), BF16), pltpu.VMEM((2, piece, padded), BF16), pltpu.VMEM((2, piece, width), BF16),
     )
 
     for step in range(1, chips):
         landed = chip_in.at[step - 1]
-        remote(landed, landed, far_send.at[0], far_recv.at[step - 1], place.sibling).wait_recv()
+        remote(landed, landed, far_send.at[step - 1], far_recv.at[step - 1], place.sibling).wait_recv()
     for step in range(1, chips):
         to_chip(step).wait_send()
     mid_copy.wait()
@@ -1358,18 +1514,17 @@
             else:
                 own_heads.start()
 
+        relay_term(2, sum_buf.at[0])
+
         for i, target in enumerate((grad_down, grad_gate, grad_up)):
-            for step in range(1, groups):
-                term_copy(i, step).wait()
-
-                def sum_load(step=step, i=i):
-                    return pltpu.make_async_copy(term_in.at[i, step - 1], sum_buf.at[step - 1], rows_sem.at[0, 0])
-
-                sum_load().start()
-                sum_load().wait()
+            landed = arrived_terms(i)
+            for j in landed:
+                load = pltpu.make_async_copy(term_in.at[i, j], sum_buf.at[j], rows_sem.at[0, 0])
+                load.start()
+                load.wait()
             total = term_buf[i, pl.ds(pl.multiple_of(seq * block, block), block), :].astype(F32)
-            for step in range(1, groups):
-                total = total + sum_buf[step - 1].astype(F32)
+            for j in landed:
+                total = total + sum_buf[j].astype(F32)
             mid[0:block, :] = total
             store = pltpu.make_async_copy(mid.at[pl.ds(0, block), :], target, gm_sem.at[0])
             store.start()
@@ -1388,6 +1543,8 @@
         collect(step).wait_send()
     for step in range(chips):
         to_sibling(step).wait_send()
+    for step in range(1, chips):
+        far_copy(step).wait_send()
 
 
 def middle_call(dp_count, groups, piece, width, unit_rows):
@@ -1404,7 +1561,7 @@
     return pl.pallas_call(
         functools.partial(middle_kernel, dp_count, groups),
         in_specs=[vmem] + [hbm] * 8,
-        out_specs=[vmem, vmem] + [hbm] * 15,
+        out_specs=[vmem, vmem] + [hbm] * 16,
         out_shape=(
             shape((piece, width), BF16),
             shape((8, width), F32),
@@ -1417,12 +1574,13 @@
             shape((block, width), F32),
             shape((block, width), F32),
             shape((dp_count, piece, width), BF16),
+            shape((dp_count, piece, padded), F32),
             shape((dp_count, piece, padded), BF16),
             shape((dp_count, piece, padded), BF16),
             shape((dp_count, piece, padded), BF16),
             shape((chips, piece, width), BF16),
             shape((others, piece, width), BF16),
-            shape((3, groups - 1, block, width), BF16),
+            shape((3, max(groups - 1, 4), block, width), BF16),
         ),
         scratch_shapes=[
             pltpu.VMEM((padded, width), BF16), pltpu.VMEM((padded, width), BF16), pltpu.VMEM((padded, width), BF16),
@@ -1430,12 +1588,13 @@
             pltpu.VMEM((piece, width), F32),
             pltpu.VMEM((piece, width), BF16),
             pltpu.VMEM((piece, width), F32),
+            pltpu.VMEM((others, piece, width), BF16),
             pltpu.VMEM((3, unit_rows, width), BF16),
             dma((groups - 1,)), dma((groups - 1,)), dma, dma((3,)), dma((2,)), dma,
             dma((others,)), dma((others,)), dma((chips,)), dma((chips,)), dma,
-            dma, dma((2,)), dma((2, 3)),
-            dma, dma((chips,)), dma, dma((2,)), dma((others,)), dma((2,)),
-            dma((2,)), dma((2,)), dma((3, groups - 1)), dma((3, groups - 1)),
+            dma((2,)), dma((2,)), dma((2, 3)),
+            dma, dma((chips,)), dma, dma((others,)), dma((others,)),
+            dma((2,)), dma((2,)), dma((2,)), dma((3, max(groups - 1, 4))), dma((3, max(groups - 1, 4))),
             dma((2, chips)), dma((2,)), dma,
             dma((groups - 1,)), dma((groups - 1,)), dma,
         ],

time: 1190 us -> 1160 us (0.975)
  Pallas kernels: 1130 us -> 1100 us
    pallas_call x1, Pallas kernels: 403 us -> 384 us  [shards(): middle_call(dp_count, groups, piece, width, groups * padded)]
  transfers between devices with their start and end apart: 1 -> 1, of which waited for: 0 -> 0; matrix products, arithmetic and copies ran while one was open for 0% -> 0% of each run, Pallas kernels for 29% -> 28%
where the time goes in v4:
time: 1160 us; the launch traced here: 1140 us
  Pallas kernels  1100 us (95%)
  local copies, waits for them, and re-layouts  19.6 us (2%)
  between operations  17 us (1%)
  other arithmetic  11.6 us (1%)
    pallas_call x1, Pallas kernels, shards(): middle_call(dp_count, groups, piece, width, groups * padded)  384 us
    pallas_call x1, Pallas kernels, shards(): project_call(dp_count, groups, piece, width, here, padded, 1)  357 us
    pallas_call x1, Pallas kernels, shards(): reduce_call(dp_count, groups, piece, width, here)  283 us
    pallas_call x1, Pallas kernels, shards(): attend_backward(high, start, query, key, value, context_heads, grad_conte...  42.8 us
    pallas_call x1, Pallas kernels, shards(): context_heads, lse = attend_forward(low, start, query, key, value)  29.5 us
  transfers between devices with their start and end apart: 1, of which 0 were waited for; matrix products, arithmetic and copies ran while one was open for 0% of the time, Pallas kernels for 28%

profile of v4, /device:TPU:0, one launch (start us, length us, event | category | flops | bytes accessed | tf_op | source)
XLA Modules:
  0.0 1143.9 jit_solution(11571219668759021670)
XLA Ops:
  7.2 0.0 reduce-scatter.2.cloned.1.call-start
  7.2 1.6 fusion.6
  11.4 3.9 compare_select_fusion.7
  15.3 0.1 slice.21
  15.4 0.5 and_select_fusion.1.low_ref
  16.0 1.3 pad.18.w_gate
  17.2 1.2 pad.19.w_up
  18.4 0.1 pad.20.w_down
  18.6 356.6 %gather_project.1 = (bf16[512,2048]{1,0:T(8,128)(2,1)S(1)}, f32[8,2048]{1,0:T(8,128)S(1)}, bf16[4,512,512]{2,1,0:T(8,128)(2,1)}, bf16[4,512,512]{2,1,0:T(8,128)(...) custom-call(bf16[512,2048]{1,0:T(8,128)(2,1)} %bitcast.47, ...), custom_call_target="tpu_custom_call" | custom-call | flops 274877906944 | bytes 67108864 | tf_op jit(solution)/shard_map/gather_project/pallas_call | solution.py:1638
  375.2 1.3 copy-done.4
  376.5 0.6 copy-done.5
  377.2 29.5 %attend_forward.1 = (bf16[2048,512]{1,0:T(8,128)(2,1)}, f32[4,1,2048]{2,1,0:T(1,128)}) custom-call(s32[4]{0:T(128)} %and_select_fusion.1.low_ref, s32[1,2048]{1,0:T(1,128)} %copy-done.16, bf16[2048,512]{1,0:T(8,128)(2,1)} %bitcast.64, bf16[2048,512]{1,0:T(8,128)(2,1)} %bitcast.60, bf16[2048,512]{1,0:T(8,128)(2,1)} %bitcast.62), custom_call_target="tpu_custom_call" | custom-call | flops 34359738368 | bytes 8388608 | tf_op jit(solution)/shard_map/attend_forward/pallas_call | solution.py:1648
  406.7 383.7 %feed_forward.1 = (bf16[512,2048]{1,0:T(8,128)(2,1)}, f32[8,2048]{1,0:T(8,128)}, f32[512,2048]{1,0:T(8,128)}, f32[512,2048]{1,0:T(8,128)}, bf16[512,2048]{1,0:T(...) custom-call(f32[8,2048]{1,0:T(8,128)} %copy-done.5, ...), custom_call_target="tpu_custom_call" | custom-call | flops 274877906944 | bytes 268435456 | tf_op jit(solution)/shard_map/feed_forward/pallas_call | solution.py:1651
  790.5 0.0 reduce-scatter.2.cloned.1.call-update
  790.5 0.8 slice.22
  791.3 0.5 fusion.16.high_ref
  791.8 42.8 %attend_backward.1 = (bf16[2048,512]{1,0:T(8,128)(2,1)}, bf16[2048,512]{1,0:T(8,128)(2,1)}, bf16[2048,512]{1,0:T(8,128)(2,1)}) custom-call(s32[4]{0:T(128)} %fusion.16.high_ref, s32[1,2048]{1,0:T(1,128)} %copy-done.16, bf16[2048,512]{1,0:T(8,128)(2,1)} %bitcast.65, bf16[2048,512]{1,0:T(8,128)(2,1)} %bitcast.61, bf16[2048,512]{1,0:T(8,128)(2,1)} %bitcast.63, ...), custom_call_target="tpu_custom_call" | custom-call | flops 51539607552 | bytes 16777216 | tf_op jit(solution)/shard_map/attend_backward/pallas_call | solution.py:1657
  834.6 282.9 %weight_gradients.1 = (bf16[4,512,512]{2,1,0:T(8,128)(2,1)}, bf16[4,512,512]{2,1,0:T(8,128)(2,1)}, bf16[4,512,512]{2,1,0:T(8,128)(2,1)}, f32[64,2048]{1,0:T(8,12...) custom-call(bf16[512,2048]{1,0:T(8,128)(2,1)} %get-tuple-element.60., ...), custom_call_target="tpu_custom_call" | custom-call | flops 274877906944 | bytes 67108864 | tf_op jit(solution)/shard_map/weight_gradients/pallas_call | solution.py:1659
  1117.5 0.0 reduce-scatter.2.cloned.1.call-done
  1117.5 1.3 slice_bitcast_fusion
  1118.8 5.0 fusion
  1123.8 2.1 copy.34
  1126.0 1.6 copy-done.6
  1127.5 2.0 copy.35
  1129.6 0.8 copy.36
  1130.4 0.8 copy.37
  1131.2 0.8 copy.38
  1131.9 0.8 copy.39
  1132.7 1.1 copy.40
  1133.8 1.1 copy.41
  1135.0 0.8 copy-done.8
  1135.7 1.1 copy.42
  (35 shorter events, 0.1 us)
Async XLA Ops:
  7.2 11.3 copy-start.11
  7.2 1110.3 %reduce-scatter.2.cloned.1.call-start = ((), (), s32[]{:S(2)}) async-start(), calls=%async_computation.1 | async-start | bytes 18874368 | tf_op jit(solution)/shard_map/reduce_scatter | solution.py:1655
  15.3 3.2 copy-start.16
  15.9 2.6 copy-start.17
  15.9 2.6 copy-start.18
  15.9 2.6 copy-start
  15.9 2.6 copy-start.1
  15.9 2.6 copy-start.2
  15.9 2.6 copy-start.3
  375.2 1.3 copy-start.4
  376.5 0.6 copy-start.5
  1118.8 5.0 copy-start.7
  1123.8 3.7 copy-start.6
  1127.5 2.0 copy-start.15
  1127.5 2.8 copy-start.14
  1127.5 3.6 copy-start.13
  1129.6 2.4 copy-start.12
  1129.6 3.2 copy-start.10
  1131.9 1.9 copy-start.9
  1133.8 1.9 copy-start.8
Sparse Core Ops, SparseCore 0:
  790.6 191.4 reduce-scatter.1

commit v5 on v4

--- a/solution.py
+++ b/solution.py
@@ -534,7 +534,7 @@
 def reduce_kernel(
     dp_count, groups, here, context, memory, attn_in, gain_rows, gain_ffn_term, grad_branch, dv, dk, dq,
     all_value, all_key, all_query, hidden, grad_mid,
-    out_v, out_k, out_q, grad_out, grad_value, grad_key, grad_query, grad_memory, grad_hidden, grad_gains,
+    grad_out, grad_value, grad_key, grad_query, grad_memory, grad_hidden, grad_gains,
     right, core_buf, core_in, chip_buf, chip_in, kept, line_buf, line_in, line_own,
     part_send, part_recv, part_own, load_sem, core_send, core_recv, chip_send, chip_recv,
     line_send, line_recv, store_sem, core_free, chip_free,
@@ -547,53 +547,53 @@
     share = right.shape[3]
     lefts = (context, memory, memory, attn_in)
     parts = (None, dv, dk, dq)
-    wholes = (None, out_v, out_k, out_q)
     grads = (grad_out, grad_value, grad_key, grad_query)
-    count = 4
-
-    def part_copy(m, step):
+    half = share // 2
+    count = 8
+
+    def half_columns(job, group=0):
+        return pl.ds(group * share + job % 2 * half, half)
+
+    def part_copy(job, step):
         other = place.line_at(step)
         return remote(
-            parts[m].at[other], wholes[m].at[seq], part_send.at[m, step - 1], part_recv.at[m, step - 1],
-            place.line_device(other),
-        )
-
-    def own_part(m):
-        return pltpu.make_async_copy(parts[m].at[seq], wholes[m].at[seq], part_own.at[m])
-
-    def send_parts(m):
-        own_part(m).start()
+            parts[job // 2].at[other, :, half_columns(job)], right.at[job // 2, seq, :, half_columns(job)],
+            part_send.at[job, step - 1], part_recv.at[job, step - 1], place.line_device(other),
+        )
+
+    def own_part(job):
+        return pltpu.make_async_copy(
+            parts[job // 2].at[seq, :, half_columns(job)], right.at[job // 2, seq, :, half_columns(job)],
+            part_own.at[job],
+        )
+
+    def send_parts(job):
+        own_part(job).start()
         for step in range(1, groups):
-            part_copy(m, step).start()
-
-    def sent_parts(m):
+            part_copy(job, step).start()
+
+    def sent_parts(job):
         for step in range(1, groups):
-            part_copy(m, step).wait_send()
-
-    def load_copy(m, group):
-        source = grad_branch.at[:, pl.ds(group * share, share)] if m == 0 else wholes[m].at[group]
-        return pltpu.make_async_copy(source, right.at[m % 2, group], load_sem.at[group])
-
-    def load_right(m):
-        if m > 0:
-            own_part(m).wait()
-            for step in range(1, groups):
-                part_copy(m, step).wait_recv()
+            part_copy(job, step).wait_send()
+
+    def arrived_parts(job):
+        own_part(job).wait()
+        for step in range(1, groups):
+            part_copy(job, step).wait_recv()
+
+    def branch_copy(group):
+        return pltpu.make_async_copy(
+            grad_branch.at[:, pl.ds(group * share, share)], right.at[0, group], load_sem.at[group]
+        )
+
+    def product(job, dp, store):
+        rows = pl.ds(pl.multiple_of(dp * panel, panel), panel)
+        left = lefts[job // 2][:, rows].T
         for group in range(groups):
-            load_copy(m, group).start()
-        for group in range(groups):
-            load_copy(m, group).wait()
-
-    def product(m, dp, store):
-        rows = pl.ds(pl.multiple_of(dp * panel, panel), panel)
-        left = lefts[m][:, rows].T
-
-        def one(group, _):
-            columns = pl.ds(pl.multiple_of(group * share, share), share)
-            store(columns, jnp.dot(left, right[m % 2, group], preferred_element_type=F32))
-            return 0
-
-        lax.fori_loop(0, groups, one, 0)
+            store(
+                slice(group * half, (group + 1) * half),
+                jnp.dot(left, right[job // 2, group, :, half_columns(job)], preferred_element_type=F32),
+            )
 
     def core_copy(m, step):
         return remote(
@@ -610,6 +610,30 @@
         return remote(
             line_buf.at[m, step - 1], line_in.at[m, step - 1], line_send.at[m, step - 1], line_recv.at[m, step - 1],
             place.line_device(place.line_at(step)),
+        )
+
+    paired = groups == 4
+    inner = (seq == 1) | (seq == 2)
+    mate = seq + 1 - 2 * (seq % 2)
+
+    def across(j):
+        return 2 * (1 - seq // 2) + j
+
+    def near_copy(m):
+        return remote(
+            line_buf.at[m, 0], line_in.at[m, 0], line_send.at[m, 0], line_recv.at[m, 0], place.line_device(mate)
+        )
+
+    def relay_copy(m, j):
+        return remote(
+            line_buf.at[m, 1 + j], line_in.at[m, 2 + j], line_send.at[m, 1 + j], line_recv.at[m, 2 + j],
+            place.line_device(mate),
+        )
+
+    def across_copy(m, j):
+        return remote(
+            line_buf.at[m, 1 + j], line_in.at[m, 1], line_send.at[m, 1 + j], line_recv.at[m, 1],
+            place.line_device(across(j)),
         )
 
     order = tuple(range(1, chips)) + (0,)
@@ -652,37 +676,75 @@
         if m + 2 < count:
             pl.semaphore_signal(core_free, inc=1, device_id=place.sibling, device_id_type=BY_MESH)
 
-    def to_line(m):
+    def sum_chips(m):
         for step in range(1, chips):
             chip_copy(m, step).wait_recv()
-        for step in tuple(range(1, groups)) + (0,):
-            block = place.line_at(step)
+
+        def block_sum(block):
             rows = pl.ds(pl.multiple_of(block * here, here), here)
             total = kept[m % 2, rows, :]
             for other in range(1, chips):
                 total = total + chip_in[m % 2, other - 1, rows, :].astype(F32)
-            if step > 0:
-                line_buf[m, step - 1] = total.astype(BF16)
-                line_copy(m, step).start()
-            else:
-                line_own[m] = total
+            return total
+
+        if paired:
+            line_buf[m, 0] = block_sum(mate).astype(BF16)
+            for j in range(2):
+                line_buf[m, 1 + j] = block_sum(across(j)).astype(BF16)
+        else:
+            for step in range(1, groups):
+                line_buf[m, step - 1] = block_sum(place.line_at(step)).astype(BF16)
+        line_own[m] = block_sum(seq)
         if m + 2 < count:
             for step in range(1, chips):
-                partner = place.chip_at(step)
                 pl.semaphore_signal(
-                    chip_free.at[step - 1], inc=1, device_id=place.chip_device(partner), device_id_type=BY_MESH
+                    chip_free.at[step - 1], inc=1, device_id=place.chip_device(place.chip_at(step)),
+                    device_id_type=BY_MESH,
                 )
 
-    def store_grad(m):
-        return pltpu.make_async_copy(line_own.at[m], grads[m], store_sem.at[m])
+    def send_line(m):
+        if paired:
+            near_copy(m).start()
+
+            @pl.when(jnp.logical_not(inner))
+            def _():
+                for j in range(2):
+                    relay_copy(m, j).start()
+
+        else:
+            for step in range(1, groups):
+                line_copy(m, step).start()
+
+    def relay(m):
+        if not paired:
+            return
+
+        @pl.when(inner)
+        def _():
+            for j in range(2):
+                relay_copy(m, j).wait_recv()
+                line_buf[m, 1 + j] = (line_buf[m, 1 + j].astype(F32) + line_in[m, 2 + j].astype(F32)).astype(BF16)
+                across_copy(m, j).start()
+
+    def store_grad(m, group):
+        return pltpu.make_async_copy(
+            line_own.at[m, :, pl.ds(group * half, half)], grads[m // 2].at[:, half_columns(m, group)],
+            store_sem.at[m, group],
+        )
 
     def settle(m):
         total = line_own[m]
-        for step in range(1, groups):
-            line_copy(m, step).wait_recv()
-            total = total + line_in[m, step - 1].astype(F32)
+        if paired:
+            near_copy(m).wait_recv()
+            across_copy(m, 0).wait_recv()
+            total = total + line_in[m, 0].astype(F32) + line_in[m, 1].astype(F32)
+        else:
+            for step in range(1, groups):
+                line_copy(m, step).wait_recv()
+                total = total + line_in[m, step - 1].astype(F32)
         line_own[m] = total
-        store_grad(m).start()
+        for group in range(groups):
+            store_grad(m, group).start()
 
     width = memory.shape[1]
     panels = width // panel
@@ -701,7 +763,7 @@
         for group in range(groups):
             columns = slice(group * share, (group + 1) * share)
             total = total + lax.dot_general(
-                right[m % 2, group], weight[slot, which, :, columns], NT, preferred_element_type=F32
+                right[m, group], weight[slot, which, :, columns], NT, preferred_element_type=F32
             )
         return total
 
@@ -837,47 +899,66 @@
 
     lax.fori_loop(1, devices, greet, 0)
     pl.semaphore_wait(everyone, devices - 1)
-    send_parts(1)
-    load_right(0)
-    to_sibling(0)
-    to_chips(0)
-    sent_parts(1)
     send_parts(2)
-    load_right(1)
-    to_sibling(1)
-    to_chips(1)
-    to_line(0)
-    sent_parts(2)
     send_parts(3)
-    load_right(2)
-    to_sibling(2)
-    to_chips(2)
-    to_line(1)
-    settle(0)
-    memory_gradient()
-    sent_parts(3)
-    load_right(3)
-    to_sibling(3)
-    to_chips(3)
-    to_line(2)
-    settle(1)
+    for group in range(groups):
+        branch_copy(group).start()
+    for group in range(groups):
+        branch_copy(group).wait()
+    for job in range(2):
+        to_sibling(job)
+        to_chips(job)
+    for job in range(2, count):
+        sent_parts(job)
+        if job + 2 < count:
+            send_parts(job + 2)
+        if job == count - 1:
+            for earlier in range(job - 2):
+                send_line(earlier)
+        arrived_parts(job)
+        to_sibling(job)
+        sum_chips(job - 2)
+        if job == count - 1:
+            send_line(job - 2)
+        to_chips(job)
+        if job == 5:
+            memory_gradient()
+    sum_chips(6)
+    send_line(6)
     query_gradient()
+    relay(0)
+    relay(1)
+    relay(2)
     hidden_gradient()
+    relay(3)
+    relay(4)
+    relay(5)
     send_gains()
-    to_line(3)
-    settle(2)
-    settle(3)
+    sum_chips(7)
+    send_line(7)
+    for job in range(6):
+        settle(job)
+    relay(6)
+    settle(6)
+    relay(7)
+    settle(7)
     sum_gains()
     pltpu.make_async_copy(grad_attn_in, grad_hidden, panel_sem.at[0]).wait()
     for step in range(chips):
-        core_copy(3, step).wait_send()
-    for m in (2, 3):
-        for step in range(1, chips):
-            chip_copy(m, step).wait_send()
-    for m in range(count):
-        for step in range(1, groups):
-            line_copy(m, step).wait_send()
-        store_grad(m).wait()
+        core_copy(count - 1, step).wait_send()
+    for job in range(count):
+        if job >= count - 2:
+            for step in range(1, chips):
+                chip_copy(job, step).wait_send()
+        if paired:
+            near_copy(job).wait_send()
+            for j in range(2):
+                across_copy(job, j).wait_send()
+        else:
+            for step in range(1, groups):
+                line_copy(job, step).wait_send()
+        for group in range(groups):
+            store_grad(job, group).wait()
 
 
 def reduce_call(dp_count, groups, piece, width, here):
@@ -886,7 +967,6 @@
     panel = groups * here
     hbm = pl.BlockSpec(memory_space=pl.ANY)
     vmem = pl.BlockSpec(memory_space=pltpu.VMEM)
-    part = jax.ShapeDtypeStruct((groups, piece, share), BF16)
     grad = jax.ShapeDtypeStruct((here, width), F32)
     tokens = jax.ShapeDtypeStruct((piece, width), F32)
     some = min(64, piece)
@@ -896,22 +976,22 @@
     return pl.pallas_call(
         functools.partial(reduce_kernel, dp_count, groups, here),
         in_specs=[vmem] * 5 + [hbm] * 9,
-        out_specs=[hbm] * 9 + [vmem],
-        out_shape=(part, part, part, grad, grad, grad, grad, tokens, tokens, jax.ShapeDtypeStruct((8, 128), F32)),
+        out_specs=[hbm] * 6 + [vmem],
+        out_shape=(grad, grad, grad, grad, tokens, tokens, jax.ShapeDtypeStruct((8, 128), F32)),
         scratch_shapes=[
-            pltpu.VMEM((2, groups, piece, share), BF16),
-            pltpu.VMEM((chips, panel, width), BF16),
-            pltpu.VMEM((2, chips, panel, width), BF16),
-            pltpu.VMEM((2, others, panel, width), BF16),
-            pltpu.VMEM((2, others, panel, width), BF16),
-            pltpu.VMEM((2, panel, width), F32),
-            pltpu.VMEM((4, groups - 1, here, width), BF16),
-            pltpu.VMEM((4, groups - 1, here, width), BF16),
-            pltpu.VMEM((4, here, width), F32),
-            dma((4, groups - 1)), dma((4, groups - 1)), dma((4,)), dma((groups,)),
+            pltpu.VMEM((4, groups, piece, share), BF16),
+            pltpu.VMEM((chips, panel, width // 2), BF16),
+            pltpu.VMEM((2, chips, panel, width // 2), BF16),
+            pltpu.VMEM((2, others, panel, width // 2), BF16),
+            pltpu.VMEM((2, others, panel, width // 2), BF16),
+            pltpu.VMEM((2, panel, width // 2), F32),
+            pltpu.VMEM((8, max(groups - 1, 3), here, width // 2), BF16),
+            pltpu.VMEM((8, max(groups - 1, 4), here, width // 2), BF16),
+            pltpu.VMEM((8, here, width // 2), F32),
+            dma((8, groups - 1)), dma((8, groups - 1)), dma((8,)), dma((groups,)),
             dma((chips,)), dma((2, chips)),
             dma((2, others)), dma((2, others)),
-            dma((4, groups - 1)), dma((4, groups - 1)), dma((4,)),
+            dma((8, max(groups - 1, 3))), dma((8, max(groups - 1, 4))), dma((8, groups)),
             pltpu.SemaphoreType.REGULAR, pltpu.SemaphoreType.REGULAR((others,)),
             pltpu.VMEM((2, 2, panel, width), BF16),
             pltpu.VMEM((2, piece, panel), F32),
@@ -936,11 +1016,12 @@
 def middle_kernel(
     dp_count, groups,
     gain_rows, hidden, context_heads, grad_own, out_rows, gate_rows, up_rows, down_rows, all_grad,
-    context, gain_term, mid_out, grad_mid, grad_branch, grad_heads, branch, grad_down, grad_gate, grad_up,
-    all_ffn, grad_acts, acts, grad_gates, grad_ups, core_in, chip_in, term_in,
+    context, gain_term, layer_out, grad_mid, grad_branch, grad_heads, grad_down, grad_gate, grad_up,
+    all_ffn, grad_acts, acts, grad_gates, grad_ups, core_in, chip_in, branch_core, branch_out, branch_in, term_in,
     gate_w, up_w, down_w, out_w, mid, ffn_in, own_total, chip_out, term_buf,
-    col_send, col_recv, col_own, weight_sem, out_sem, mid_sem, chip_send, chip_recv, core_send, core_recv, own_sem,
+    col_send, col_recv, col_own, weight_sem, out_sem, chip_send, chip_recv, core_send, core_recv, own_sem,
     x_sem, dy_sem, act_sem, sum_send, sum_recv, load_sem, far_send, far_recv, left_sem, right_sem, branch_sem,
+    part_send, part_recv, plane_send, plane_recv,
     term_send, term_recv, rows_sem, gm_sem, gb_sem, head_send, head_recv, head_own,
 ):
     place = Place(dp_count, groups)
@@ -1058,8 +1139,6 @@
         return 0
 
     lax.fori_loop(0, batches, normalize, 0)
-    mid_copy = pltpu.make_async_copy(mid, mid_out, mid_sem)
-    mid_copy.start()
 
     def to_chip(step):
         return remote(
@@ -1394,61 +1473,114 @@
         pltpu.VMEM((2, 2, piece, padded), BF16), pltpu.VMEM((piece, width), BF16), pltpu.VMEM((piece, width), BF16),
     )
 
-    def branch_parts(relay_buf, act_buf, branch_buf):
+    def plane_copy(step):
+        return remote(
+            branch_out.at[step], branch_in.at[step - 1], plane_send.at[step - 1], plane_recv.at[step - 1],
+            place.chip_device(place.chip_at(step)),
+        )
+
+    def branch_parts(relay_buf, act_buf, branch_buf, core_out, load_buf):
         relay_term(0, relay_buf)
 
-        def act_copy(dp, slot):
-            return pltpu.make_async_copy(acts.at[dp], act_buf.at[slot], act_sem.at[slot, 0])
-
-        def branch_copy(dp, slot):
-            return pltpu.make_async_copy(branch_buf.at[slot], branch.at[dp], branch_sem.at[slot])
-
-        act_copy(0, 0).start()
-
-        def one(dp, _):
-            slot = dp % 2
-
-            @pl.when(dp + 1 < dp_count)
-            def _():
-                act_copy(dp + 1, 1 - slot).start()
-
-            act_copy(dp, slot).wait()
-
-            @pl.when(dp >= 2)
-            def _():
-                branch_copy(dp - 2, slot).wait()
+        def act_copy(u):
+            return pltpu.make_async_copy(acts.at[piece_of(u, False)[2]], act_buf.at[u % 2], act_sem.at[u % 2, 0])
+
+        def part_copy(step):
+            return remote(core_out, branch_core.at[step], part_send, part_recv.at[step], place.sibling)
+
+        def load_copy(step):
+            return pltpu.make_async_copy(branch_core.at[step], load_buf, load_sem)
+
+        def store(step):
+            return pltpu.make_async_copy(branch_buf.at[step % 2], branch_out.at[step], branch_sem.at[step % 2])
+
+        act_copy(0).start()
+
+        def one(u, _):
+            step, which, dp = piece_of(u, False)
+            slot = u % 2
+
+            @pl.when(u + 1 < pieces)
+            def _():
+                act_copy(u + 1).start()
+
+            act_copy(u).wait()
+
+            @pl.when((which == 0) & (step > 0))
+            def _():
+                part_copy(step - 1).wait_send()
+
+            @pl.when(which == 1)
+            def _():
+                part_copy(step).wait_recv()
+                load_copy(step).start()
+
+                @pl.when(step > 1)
+                def _():
+                    store(step - 2).wait()
+
+                load_copy(step).wait()
 
             def part_of(part, _):
                 columns = group_columns(part)
-                branch_buf[slot, :, columns] = mxu(act_buf[slot], down_w[:, columns], NN).astype(BF16)
+                value = mxu(act_buf[slot], down_w[:, columns], NN)
+
+                @pl.when(which == 0)
+                def _():
+                    core_out[:, columns] = value.astype(BF16)
+
+                @pl.when(which == 1)
+                def _():
+                    branch_buf[step % 2, :, columns] = (value + load_buf[:, columns].astype(F32)).astype(BF16)
+
                 return 0
 
             lax.fori_loop(0, groups, part_of, 0)
-            branch_copy(dp, slot).start()
+
+            @pl.when(which == 0)
+            def _():
+                part_copy(step).start()
+
+            @pl.when(which == 1)
+            def _():
+                store(step).start()
+
             return 0
 
-        lax.fori_loop(0, dp_count, one, 0)
-        for dp in range(dp_count - 2, dp_count):
-            branch_copy(dp, dp % 2).wait()
+        lax.fori_loop(0, pieces, one, 0)
+        part_copy(chips - 1).wait_send()
+        for step in range(max(chips - 2, 0), chips):
+            store(step).wait()
         relay_term(1, relay_buf)
 
     pl.run_scoped(
         branch_parts,
         pltpu.VMEM((block, width), BF16), pltpu.VMEM((2, piece, padded), BF16), pltpu.VMEM((2, piece, width), BF16),
+        pltpu.VMEM((piece, width), BF16), pltpu.VMEM((piece, width), BF16),
     )
 
     for step in range(1, chips):
         landed = chip_in.at[step - 1]
         remote(landed, landed, far_send.at[step - 1], far_recv.at[step - 1], place.sibling).wait_recv()
     for step in range(1, chips):
+        plane_copy(step).start()
+    for step in range(1, chips):
         to_chip(step).wait_send()
-    mid_copy.wait()
     gain_term[...] = jnp.zeros_like(gain_term)
 
-    def norm_and_heads(rows_buf, mid_buf, heads_buf, sum_buf):
+    def norm_and_heads(rows_buf, mid_buf, layer_buf, heads_buf, sum_buf):
         def rows_copy(index, step, slot):
             source = grad_own.at[batch(index), :] if step == 0 else chip_in.at[step - 1, batch(index), :]
             return pltpu.make_async_copy(source, rows_buf.at[slot, step], rows_sem.at[slot, step])
+
+        def layer_rows(index, step, slot):
+            source = branch_out.at[0] if step == 0 else branch_in.at[step - 1]
+            return pltpu.make_async_copy(
+                source.at[batch(index), :], rows_buf.at[slot, step], rows_sem.at[slot, step]
+            )
+
+        def layer_copy(index, slot):
+            return pltpu.make_async_copy(layer_buf.at[slot], layer_out.at[batch(index), :], gm_sem.at[slot])
 
         def grad_mid_copy(index, slot):
             return pltpu.make_async_copy(mid_buf.at[slot], grad_mid.at[batch(index), :], gm_sem.at[slot])
@@ -1525,10 +1657,40 @@
             total = term_buf[i, pl.ds(pl.multiple_of(seq * block, block), block), :].astype(F32)
             for j in landed:
                 total = total + sum_buf[j].astype(F32)
-            mid[0:block, :] = total
-            store = pltpu.make_async_copy(mid.at[pl.ds(0, block), :], target, gm_sem.at[0])
+            own_total[0:block, :] = total
+            store = pltpu.make_async_copy(own_total.at[pl.ds(0, block), :], target, gm_sem.at[0])
             store.start()
             store.wait()
+        for step in range(1, chips):
+            plane_copy(step).wait()
+        for step in range(chips):
+            layer_rows(0, step, 0).start()
+
+        def layer(index, _):
+            slot = index % 2
+
+            @pl.when(index + 1 < batches)
+            def _():
+                for step in range(chips):
+                    layer_rows(index + 1, step, 1 - slot).start()
+
+            for step in range(chips):
+                layer_rows(index, step, slot).wait()
+
+            @pl.when(index >= 2)
+            def _():
+                layer_copy(index - 2, slot).wait()
+
+            total = mid[batch(index), :]
+            for step in range(chips):
+                total = total + rows_buf[slot, step].astype(F32)
+            layer_buf[slot] = total.astype(BF16)
+            layer_copy(index, slot).start()
+            return 0
+
+        lax.fori_loop(0, batches, layer, 0)
+        for index in range(max(batches - 2, 0), batches):
+            layer_copy(index, index % 2).wait()
         grad_branch_copy.wait()
         own_heads.wait()
         for step in range(1, groups):
@@ -1537,7 +1699,7 @@
     pl.run_scoped(
         norm_and_heads,
         pltpu.VMEM((2, chips, some, width), BF16), pltpu.VMEM((2, some, width), F32),
-        pltpu.VMEM((groups, piece, share), BF16), pltpu.VMEM((groups - 1, block, width), BF16),
+        pltpu.VMEM((2, some, width), BF16), pltpu.VMEM((groups, piece, share), BF16), pltpu.VMEM((groups - 1, block, width), BF16),
     )
     for step in range(1, groups):
         collect(step).wait_send()
@@ -1561,15 +1723,14 @@
     return pl.pallas_call(
         functools.partial(middle_kernel, dp_count, groups),
         in_specs=[vmem] + [hbm] * 8,
-        out_specs=[vmem, vmem] + [hbm] * 16,
+        out_specs=[vmem, vmem] + [hbm] * 18,
         out_shape=(
             shape((piece, width), BF16),
             shape((8, width), F32),
-            shape((piece, width), F32),
+            shape((piece, width), BF16),
             shape((piece, width), F32),
             shape((piece, width), BF16),
             shape((groups, piece, share), BF16),
-            shape((dp_count, piece, width), BF16),
             shape((block, width), F32),
             shape((block, width), F32),
             shape((block, width), F32),
@@ -1578,6 +1739,9 @@
             shape((dp_count, piece, padded), BF16),
             shape((dp_count, piece, padded), BF16),
             shape((dp_count, piece, padded), BF16),
+            shape((chips, piece, width), BF16),
+            shape((others, piece, width), BF16),
+            shape((chips, piece, width), BF16),
             shape((chips, piece, width), BF16),
             shape((others, piece, width), BF16),
             shape((3, max(groups - 1, 4), block, width), BF16),
@@ -1590,11 +1754,12 @@
             pltpu.VMEM((piece, width), F32),
             pltpu.VMEM((others, piece, width), BF16),
             pltpu.VMEM((3, unit_rows, width), BF16),
-            dma((groups - 1,)), dma((groups - 1,)), dma, dma((3,)), dma((2,)), dma,
+            dma((groups - 1,)), dma((groups - 1,)), dma, dma((3,)), dma((2,)),
             dma((others,)), dma((others,)), dma((chips,)), dma((chips,)), dma,
             dma((2,)), dma((2,)), dma((2, 3)),
             dma, dma((chips,)), dma, dma((others,)), dma((others,)),
-            dma((2,)), dma((2,)), dma((2,)), dma((3, max(groups - 1, 4))), dma((3, max(groups - 1, 4))),
+            dma((2,)), dma((2,)), dma((2,)),
+            dma, dma((chips,)), dma((others,)), dma((others,)), dma((3, max(groups - 1, 4))), dma((3, max(groups - 1, 4))),
             dma((2, chips)), dma((2,)), dma,
             dma((groups - 1,)), dma((groups - 1,)), dma,
         ],
@@ -1647,24 +1812,21 @@
     ]
     context_heads, lse = attend_forward(low, start, query, key, value)
     (
-        context, gain_term, mid, grad_mid, grad_branch, grad_context_heads, branch, grad_w_down, grad_w_gate, grad_w_up, *_
+        context, gain_term, layer_out, grad_mid, grad_branch, grad_context_heads, grad_w_down, grad_w_gate, grad_w_up, *_
     ) = middle_call(dp_count, groups, piece, width, groups * padded)(
         gain_rows, tokens, context_heads.reshape(split), grad_out, out_rows, gate_rows, up_rows, down_rows,
         dy.reshape(dp_count, piece, width),
     )
-    branch = lax.psum_scatter(branch.reshape(dp_count * piece, width), "dp", scatter_dimension=0, tiled=True)
     grad_context_heads = grad_context_heads.reshape(flat)
     dq, dk, dv = attend_backward(high, start, query, key, value, context_heads, grad_context_heads, lse)
 
-    _, _, _, grad_w_out, grad_w_value, grad_w_key, grad_w_query, grad_memory, grad_hidden, gains = reduce_call(
+    grad_w_out, grad_w_value, grad_w_key, grad_w_query, grad_memory, grad_hidden, gains = reduce_call(
         dp_count, groups, piece, width, here
     )(
         context, mem, attn_in, gain_rows, gain_term, grad_branch, dv.reshape(split), dk.reshape(split),
         dq.reshape(split), value_rows, key_rows, query_rows, tokens, grad_mid,
     )
-    gains, branch, mid = lax.optimization_barrier((gains, branch, mid))
     grad_w_down, grad_w_gate, grad_w_up = [grad[:units] for grad in (grad_w_down, grad_w_gate, grad_w_up)]
-    layer_out = (mid + branch.astype(F32)).astype(BF16)
     grad_gain_attn, grad_gain_ffn = gains[0, :here], gains[1, :here]
     cube = (seqs, piece, width)
     return (

time: 1160 us -> 1130 us (0.974)
  Pallas kernels: 1100 us -> 1080 us
  between operations: 17 us -> 3.8 us
    pallas_call x1, Pallas kernels: 283 us -> 259 us  [shards(): reduce_call(dp_count, groups, piece, width, here)]
    pallas_call x1, Pallas kernels: 384 us -> 397 us  [shards(): middle_call(dp_count, groups, piece, width, groups * padded)]
  transfers between devices with their start and end apart: 1 -> 0, of which waited for: 0 -> 0; matrix products, arithmetic and copies ran while one was open for 0% -> 0% of each run, Pallas kernels for 28% -> 0%
where the time goes in v5:
time: 1130 us; the launch traced here: 1120 us
  Pallas kernels  1080 us (96%)
  local copies, waits for them, and re-layouts  21.3 us (2%)
    pallas_call x1, Pallas kernels, shards(): middle_call(dp_count, groups, piece, width, groups * padded)  397 us
    pallas_call x1, Pallas kernels, shards(): project_call(dp_count, groups, piece, width, here, padded, 1)  357 us
    pallas_call x1, Pallas kernels, shards(): reduce_call(dp_count, groups, piece, width, here)  259 us
    pallas_call x1, Pallas kernels, shards(): attend_backward(high, start, query, key, value, context_heads, grad_conte...  42.6 us
    pallas_call x1, Pallas kernels, shards(): context_heads, lse = attend_forward(low, start, query, key, value)  29.5 us

profile of v5, /device:TPU:0, one launch (start us, length us, event | category | flops | bytes accessed | tf_op | source)
XLA Modules:
  0.0 1116.4 jit_solution(9991552164626469413)
XLA Ops:
  0.7 0.8 fusion.14.gains
  1.5 1.5 fusion.5
  5.6 3.3 compare_select_fusion.7
  8.9 0.0 copy-start.16
  8.9 0.1 slice.22
  9.0 0.5 fusion.15.high_ref
  9.5 0.1 slice.21
  9.6 0.5 and_select_fusion.1.low_ref
  10.2 1.2 pad.18.w_gate
  11.3 1.2 pad.19.w_up
  12.5 0.1 pad.20.w_down
  12.6 356.6 %gather_project.1 = (bf16[512,2048]{1,0:T(8,128)(2,1)S(1)}, f32[8,2048]{1,0:T(8,128)S(1)}, bf16[4,512,512]{2,1,0:T(8,128)(2,1)}, bf16[4,512,512]{2,1,0:T(8,128)(...) custom-call(bf16[512,2048]{1,0:T(8,128)(2,1)} %bitcast.45, ...), custom_call_target="tpu_custom_call" | custom-call | flops 274877906944 | bytes 67108864 | tf_op jit(solution)/shard_map/gather_project/pallas_call | solution.py:1803
  369.3 0.0 copy-start.4
  369.3 1.3 copy-done.4
  370.6 0.6 copy-done.5
  371.2 29.5 %attend_forward.1 = (bf16[2048,512]{1,0:T(8,128)(2,1)}, f32[4,1,2048]{2,1,0:T(1,128)}) custom-call(s32[4]{0:T(128)} %and_select_fusion.1.low_ref, s32[1,2048]{1,0:T(1,128)} %copy-done.16, bf16[2048,512]{1,0:T(8,128)(2,1)} %bitcast.62, bf16[2048,512]{1,0:T(8,128)(2,1)} %bitcast.58, bf16[2048,512]{1,0:T(8,128)(2,1)} %bitcast.60), custom_call_target="tpu_custom_call" | custom-call | flops 34359738368 | bytes 8388608 | tf_op jit(solution)/shard_map/attend_forward/pallas_call | solution.py:1813
  400.8 397.2 %feed_forward.1 = (bf16[512,2048]{1,0:T(8,128)(2,1)}, f32[8,2048]{1,0:T(8,128)}, bf16[512,2048]{1,0:T(8,128)(2,1)}, f32[512,2048]{1,0:T(8,128)}, bf16[512,2048]{...) custom-call(f32[8,2048]{1,0:T(8,128)} %copy-done.5, ...), custom_call_target="tpu_custom_call" | custom-call | flops 274877906944 | bytes 268435456 | tf_op jit(solution)/shard_map/feed_forward/pallas_call | solution.py:1816
  797.9 42.6 %attend_backward.1 = (bf16[2048,512]{1,0:T(8,128)(2,1)}, bf16[2048,512]{1,0:T(8,128)(2,1)}, bf16[2048,512]{1,0:T(8,128)(2,1)}) custom-call(s32[4]{0:T(128)} %fusion.15.high_ref, s32[1,2048]{1,0:T(1,128)} %copy-done.16, bf16[2048,512]{1,0:T(8,128)(2,1)} %bitcast.63, bf16[2048,512]{1,0:T(8,128)(2,1)} %bitcast.59, bf16[2048,512]{1,0:T(8,128)(2,1)} %bitcast.61, ...), custom_call_target="tpu_custom_call" | custom-call | flops 51539607552 | bytes 16777216 | tf_op jit(solution)/shard_map/attend_backward/pallas_call | solution.py:1821
  840.6 258.7 %weight_gradients.1 = (f32[64,2048]{1,0:T(8,128)}, f32[64,2048]{1,0:T(8,128)}, f32[64,2048]{1,0:T(8,128)}, f32[64,2048]{1,0:T(8,128)}, f32[512,2048]{1,0:T(8,128...) custom-call(bf16[512,2048]{1,0:T(8,128)(2,1)} %get-tuple-element.57.context, bf16[512,2048]{1,0:T(8,128)(2,1)} %bitcast.49, ...), custom_call_target="tpu_custom_call" | custom-call | flops 274877906944 | bytes 67108864 | tf_op jit(solution)/shard_map/weight_gradients/pallas_call | solution.py:1823
  1099.3 1.3 slice_bitcast_fusion
  1100.6 3.2 copy.35
  1103.8 2.1 copy.36
  1105.9 1.6 copy-done.6
  1107.5 2.0 copy.37
  1109.5 0.8 copy.38
  1110.3 0.0 copy-done.14
  1110.3 0.8 copy.39
  1111.1 0.8 copy.40
  1111.9 0.8 copy.41
  1112.7 1.1 copy.42
  1113.8 1.1 copy.43
  1114.9 1.1 copy.44
  (28 shorter events, 0.1 us)
Async XLA Ops:
  0.6 11.9 %copy-start.11 = (bf16[172,2048]{1,0:T(8,128)(2,1)S(1)}, bf16[172,2048]{1,0:T(8,128)(2,1)}, u32[]{:S(2)}) copy-start(bf16[172,2048]{1,0:T(8,128)(2,1)} %param.24) | copy-start | bytes 2113540
  0.7 11.9 %copy-start.3 = (bf16[64,2048]{1,0:T(8,128)(2,1)S(1)}, bf16[64,2048]{1,0:T(8,128)(2,1)}, u32[]{:S(2)}) copy-start(bf16[64,2048]{1,0:T(8,128)(2,1)} %w_out.1) | copy-start | bytes 786436
  0.7 11.9 %copy-start.1 = (bf16[64,2048]{1,0:T(8,128)(2,1)S(1)}, bf16[64,2048]{1,0:T(8,128)(2,1)}, u32[]{:S(2)}) copy-start(bf16[64,2048]{1,0:T(8,128)(2,1)} %w_value.1) | copy-start | bytes 786436
  0.7 11.9 %copy-start = (bf16[64,2048]{1,0:T(8,128)(2,1)S(1)}, bf16[64,2048]{1,0:T(8,128)(2,1)}, u32[]{:S(2)}) copy-start(bf16[64,2048]{1,0:T(8,128)(2,1)} %w_key.1) | copy-start | bytes 786436
  0.7 11.9 %copy-start.2 = (bf16[64,2048]{1,0:T(8,128)(2,1)S(1)}, bf16[64,2048]{1,0:T(8,128)(2,1)}, u32[]{:S(2)}) copy-start(bf16[64,2048]{1,0:T(8,128)(2,1)} %w_query.1) | copy-start | bytes 786436
  8.9 360.4 %copy-start.16 = (s32[1,2048]{1,0:T(1,128)}, s32[1,2048]{1,0:T(1,128)S(1)}, u32[]{:S(2)}) copy-start(s32[1,2048]{1,0:T(1,128)S(1)} %get-tuple-element.89.start_ref) | copy-start | bytes 24580
  369.3 1.3 copy-start.4
  370.6 0.6 copy-start.5
  1099.3 4.5 copy-start.7
  1103.8 3.7 copy-start.6
  1107.5 2.0 copy-start.15
  1107.5 2.8 copy-start.14
  1107.5 3.6 copy-start.13
  1109.5 2.4 copy-start.12
  1109.5 3.2 copy-start.10
  1110.3 3.5 copy-start.9
  1112.7 2.2 copy-start.8

commit v6 on v5

--- a/solution.py
+++ b/solution.py
@@ -36,41 +36,44 @@
 
 
 def forward_kernel(block, low_ref, start_ref, q_ref, k_ref, v_ref, out_ref, lse_ref):
-    length = q_ref.shape[0]
+    length, width = q_ref.shape
+    heads = range(width // HEAD_DIM)
+    columns = [slice(h * HEAD_DIM, (h + 1) * HEAD_DIM) for h in heads]
 
     def one_query_block(qb, _):
         q0 = pl.multiple_of(qb * block, block)
         rows = pl.ds(q0, block)
-        query = q_ref[rows, :]
         start = start_ref[:, rows]
         query_pos = q0 + lax.broadcasted_iota(jnp.int32, (block, block), 1)
 
         def one_key_block(kb, carry):
-            top, total, acc = carry
             k0 = pl.multiple_of(kb * block, block)
             keys = pl.ds(k0, block)
-            score = mxu(k_ref[keys, :], query, NT)
             key_pos = k0 + lax.broadcasted_iota(jnp.int32, (block, block), 0)
-            score = jnp.where((key_pos >= start) & (key_pos <= query_pos), score, MASKED)
-            new_top = jnp.maximum(top, jnp.max(score, axis=0, keepdims=True))
-            shrink = jnp.exp2((top - new_top) * EXP2_SCALE)
-            raised = jnp.exp2((score - new_top) * EXP2_SCALE)
-            total = total * shrink + jnp.sum(raised, axis=0, keepdims=True)
-            acc = acc * shrink + mxu(v_ref[keys, :], raised.astype(BF16), TN)
-            return new_top, total, acc
-
-        top, total, acc = lax.fori_loop(
-            low_ref[qb],
-            qb + 1,
-            one_key_block,
-            (
-                jnp.full((1, block), MASKED, F32),
-                jnp.zeros((1, block), F32),
-                jnp.zeros((HEAD_DIM, block), F32),
-            ),
-        )
-        out_ref[rows, :] = (acc / total).T.astype(BF16)
-        lse_ref[0, :, rows] = top * EXP2_SCALE + jnp.log2(total)
+            seen = (key_pos >= start) & (key_pos <= query_pos)
+            scores = [mxu(k_ref[keys, columns[h]], q_ref[rows, columns[h]], NT) for h in heads]
+            after = []
+            for h in heads:
+                top, total, acc = carry[h]
+                score = jnp.where(seen, scores[h], MASKED)
+                new_top = jnp.maximum(top, jnp.max(score, axis=0, keepdims=True))
+                shrink = jnp.exp2((top - new_top) * EXP2_SCALE)
+                raised = jnp.exp2((score - new_top) * EXP2_SCALE)
+                total = total * shrink + jnp.sum(raised, axis=0, keepdims=True)
+                acc = acc * shrink + mxu(v_ref[keys, columns[h]], raised.astype(BF16), TN)
+                after.append((new_top, total, acc))
+            return tuple(after)
+
+        first = (
+            jnp.full((1, block), MASKED, F32),
+            jnp.zeros((1, block), F32),
+            jnp.zeros((HEAD_DIM, block), F32),
+        )
+        done = lax.fori_loop(low_ref[qb], qb + 1, one_key_block, tuple(first for _ in heads))
+        for h in heads:
+            top, total, acc = done[h]
+            out_ref[rows, columns[h]] = (acc / total).T.astype(BF16)
+            lse_ref[h, :, rows] = top * EXP2_SCALE + jnp.log2(total)
         return 0
 
     lax.fori_loop(0, length // block, one_query_block, 0)
@@ -80,15 +83,18 @@
     block, high_ref, start_ref, q_ref, k_ref, v_ref, ctx_ref, grad_ref, lse_ref,
     dq_ref, dk_ref, dv_ref, dq_acc, delta_acc,
 ):
-    length = q_ref.shape[0]
+    length, width = q_ref.shape
+    heads = range(width // HEAD_DIM)
+    columns = [slice(h * HEAD_DIM, (h + 1) * HEAD_DIM) for h in heads]
     blocks = length // block
     scale = HEAD_DIM ** (-0.5)
     dq_acc[...] = jnp.zeros_like(dq_acc)
 
     def one_delta(qb, _):
         rows = pl.ds(pl.multiple_of(qb * block, block), block)
-        both = ctx_ref[rows, :].astype(F32) * grad_ref[rows, :].astype(F32)
-        delta_acc[:, rows] = jnp.sum(both.T, axis=0, keepdims=True)
+        for h in heads:
+            both = ctx_ref[rows, columns[h]].astype(F32) * grad_ref[rows, columns[h]].astype(F32)
+            delta_acc[h, :, rows] = jnp.sum(both.T, axis=0, keepdims=True)
         return 0
 
     lax.fori_loop(0, blocks, one_delta, 0)
@@ -96,32 +102,33 @@
     def one_key_block(kb, _):
         k0 = pl.multiple_of(kb * block, block)
         keys = pl.ds(k0, block)
-        key = k_ref[keys, :]
-        value = v_ref[keys, :]
         key_pos = k0 + lax.broadcasted_iota(jnp.int32, (block, block), 0)
 
         def one_query_block(qb, carry):
-            dk, dv = carry
             q0 = pl.multiple_of(qb * block, block)
             rows = pl.ds(q0, block)
-            query = q_ref[rows, :]
-            grad = grad_ref[rows, :]
             start = start_ref[:, rows]
             query_pos = q0 + lax.broadcasted_iota(jnp.int32, (block, block), 1)
-            score = mxu(key, query, NT)
-            prob = jnp.exp2(score * EXP2_SCALE - lse_ref[0, :, rows])
-            prob = jnp.where((key_pos >= start) & (key_pos <= query_pos), prob, 0.0)
-            grad_prob = mxu(value, grad, NT)
-            grad_score = (prob * (grad_prob - delta_acc[:, rows])).astype(BF16)
-            dv = dv + mxu(prob.astype(BF16), grad, NN)
-            dk = dk + mxu(grad_score, query, NN)
-            dq_acc[rows, :] += mxu(grad_score, key, TN)
-            return dk, dv
+            seen = (key_pos >= start) & (key_pos <= query_pos)
+            scores = [mxu(k_ref[keys, columns[h]], q_ref[rows, columns[h]], NT) for h in heads]
+            grad_probs = [mxu(v_ref[keys, columns[h]], grad_ref[rows, columns[h]], NT) for h in heads]
+            after = []
+            for h in heads:
+                dk, dv = carry[h]
+                prob = jnp.exp2(scores[h] * EXP2_SCALE - lse_ref[h, :, rows])
+                prob = jnp.where(seen, prob, 0.0)
+                grad_score = (prob * (grad_probs[h] - delta_acc[h, :, rows])).astype(BF16)
+                dv = dv + mxu(prob.astype(BF16), grad_ref[rows, columns[h]], NN)
+                dk = dk + mxu(grad_score, q_ref[rows, columns[h]], NN)
+                dq_acc[rows, columns[h]] += mxu(grad_score, k_ref[keys, columns[h]], TN)
+                after.append((dk, dv))
+            return tuple(after)
 
         zeros = jnp.zeros((block, HEAD_DIM), F32)
-        dk, dv = lax.fori_loop(kb, high_ref[kb], one_query_block, (zeros, zeros))
-        dk_ref[keys, :] = (dk * scale).astype(BF16)
-        dv_ref[keys, :] = dv.astype(BF16)
+        done = lax.fori_loop(kb, high_ref[kb], one_query_block, tuple((zeros, zeros) for _ in heads))
+        for h in heads:
+            dk_ref[keys, columns[h]] = (done[h][0] * scale).astype(BF16)
+            dv_ref[keys, columns[h]] = done[h][1].astype(BF16)
         return 0
 
     lax.fori_loop(0, blocks, one_key_block, 0)
@@ -129,20 +136,24 @@
 
 
 def attention_calls(length, heads, block):
-    column = pl.BlockSpec((length, HEAD_DIM), lambda h, *_: (0, h))
+    together = math.gcd(heads, 4)
+    wide = together * HEAD_DIM
+    column = pl.BlockSpec((length, wide), lambda h, *_: (0, h))
     row = pl.BlockSpec((1, length), lambda h, *_: (0, 0))
-    stat = pl.BlockSpec((1, 1, length), lambda h, *_: (h, 0, 0))
+    stat = pl.BlockSpec((together, 1, length), lambda h, *_: (h, 0, 0))
     flat = jax.ShapeDtypeStruct((length, heads * HEAD_DIM), BF16)
     pairs = heads * length * length // 4
+    params = pltpu.CompilerParams(vmem_limit_bytes=56 * 1024 * 1024)
     forward = pl.pallas_call(
         functools.partial(forward_kernel, block),
         grid_spec=pltpu.PrefetchScalarGridSpec(
             num_scalar_prefetch=1,
-            grid=(heads,),
+            grid=(heads // together,),
             in_specs=[row, column, column, column],
             out_specs=[column, stat],
         ),
         out_shape=(flat, jax.ShapeDtypeStruct((heads, 1, length), F32)),
+        compiler_params=params,
         cost_estimate=pl.CostEstimate(
             flops=64 * pairs * HEAD_DIM, transcendentals=pairs, bytes_accessed=8 * length * heads * HEAD_DIM
         ),
@@ -152,12 +163,13 @@
         functools.partial(backward_kernel, block),
         grid_spec=pltpu.PrefetchScalarGridSpec(
             num_scalar_prefetch=1,
-            grid=(heads,),
+            grid=(heads // together,),
             in_specs=[row, column, column, column, column, column, stat],
             out_specs=[column, column, column],
-            scratch_shapes=[pltpu.VMEM((length, HEAD_DIM), F32), pltpu.VMEM((1, length), F32)],
+            scratch_shapes=[pltpu.VMEM((length, wide), F32), pltpu.VMEM((together, 1, length), F32)],
         ),
         out_shape=(flat, flat, flat),
+        compiler_params=params,
         cost_estimate=pl.CostEstimate(
             flops=96 * pairs * HEAD_DIM, transcendentals=pairs, bytes_accessed=16 * length * heads * HEAD_DIM
         ),
@@ -1784,7 +1796,7 @@
     share = width // groups
     heads = share // HEAD_DIM
     here = w_query.shape[0]
-    block = min(512, length)
+    block = min(256, length)
     tokens = hidden_in.reshape(piece, width)
     mem = memory.reshape(piece, width)
     grad_out = cotangent.reshape(piece, width)

time: 1130 us -> 1120 us (level)
  no operation moved by 1% of the time
where the time goes in v6:
time: 1120 us; the launch traced here: 1110 us
  Pallas kernels  1080 us (96%)
  local copies, waits for them, and re-layouts  21.3 us (2%)
    pallas_call x1, Pallas kernels, shards(): middle_call(dp_count, groups, piece, width, groups * padded)  399 us
    pallas_call x1, Pallas kernels, shards(): project_call(dp_count, groups, piece, width, here, padded, 1)  357 us
    pallas_call x1, Pallas kernels, shards(): reduce_call(dp_count, groups, piece, width, here)  255 us
    pallas_call x1, Pallas kernels, shards(): attend_backward(high, start, query, key, value, context_heads, grad_conte...  39.7 us
    pallas_call x1, Pallas kernels, shards(): context_heads, lse = attend_forward(low, start, query, key, value)  25.7 us

profile of v6, /device:TPU:0, one launch (start us, length us, event | category | flops | bytes accessed | tf_op | source)
XLA Modules:
  0.0 1108.4 jit_solution(161178904210127250)
XLA Ops:
  0.7 0.8 fusion.14.gains
  1.5 1.5 fusion.5
  5.6 3.3 compare_select_fusion.7
  8.9 0.0 copy-start.16
  8.9 0.1 slice.22
  9.0 0.5 fusion.15.high_ref
  9.6 0.1 slice.21
  9.6 0.5 and_select_fusion.1.low_ref
  10.2 1.2 pad.18.w_gate
  11.3 1.2 pad.19.w_up
  12.5 0.1 pad.20.w_down
  12.7 356.6 %gather_project.1 = (bf16[512,2048]{1,0:T(8,128)(2,1)S(1)}, f32[8,2048]{1,0:T(8,128)S(1)}, bf16[4,512,512]{2,1,0:T(8,128)(2,1)}, bf16[4,512,512]{2,1,0:T(8,128)(...) custom-call(bf16[512,2048]{1,0:T(8,128)(2,1)} %bitcast.45, ...), custom_call_target="tpu_custom_call" | custom-call | flops 274877906944 | bytes 67108864 | tf_op jit(solution)/shard_map/gather_project/pallas_call | solution.py:1815
  369.3 0.0 copy-start.4
  369.3 1.3 copy-done.4
  370.6 0.6 copy-done.5
  371.2 25.7 %attend_forward.1 = (bf16[2048,512]{1,0:T(8,128)(2,1)}, f32[4,1,2048]{2,1,0:T(1,128)}) custom-call(s32[8]{0:T(128)} %and_select_fusion.1.low_ref, s32[1,2048]{1,0:T(1,128)} %copy-done.16, bf16[2048,512]{1,0:T(8,128)(2,1)} %bitcast.62, bf16[2048,512]{1,0:T(8,128)(2,1)} %bitcast.58, bf16[2048,512]{1,0:T(8,128)(2,1)} %bitcast.60), custom_call_target="tpu_custom_call" | custom-call | flops 34359738368 | bytes 8388608 | tf_op jit(solution)/shard_map/attend_forward/pallas_call | solution.py:1825
  397.0 399.4 %feed_forward.1 = (bf16[512,2048]{1,0:T(8,128)(2,1)}, f32[8,2048]{1,0:T(8,128)}, bf16[512,2048]{1,0:T(8,128)(2,1)}, f32[512,2048]{1,0:T(8,128)}, bf16[512,2048]{...) custom-call(f32[8,2048]{1,0:T(8,128)} %copy-done.5, ...), custom_call_target="tpu_custom_call" | custom-call | flops 274877906944 | bytes 268435456 | tf_op jit(solution)/shard_map/feed_forward/pallas_call | solution.py:1828
  796.4 39.7 %attend_backward.1 = (bf16[2048,512]{1,0:T(8,128)(2,1)}, bf16[2048,512]{1,0:T(8,128)(2,1)}, bf16[2048,512]{1,0:T(8,128)(2,1)}) custom-call(s32[8]{0:T(128)} %fusion.15.high_ref, s32[1,2048]{1,0:T(1,128)} %copy-done.16, bf16[2048,512]{1,0:T(8,128)(2,1)} %bitcast.63, bf16[2048,512]{1,0:T(8,128)(2,1)} %bitcast.59, bf16[2048,512]{1,0:T(8,128)(2,1)} %bitcast.61, ...), custom_call_target="tpu_custom_call" | custom-call | flops 51539607552 | bytes 16777216 | tf_op jit(solution)/shard_map/attend_backward/pallas_call | solution.py:1833
  836.1 255.1 %weight_gradients.1 = (f32[64,2048]{1,0:T(8,128)}, f32[64,2048]{1,0:T(8,128)}, f32[64,2048]{1,0:T(8,128)}, f32[64,2048]{1,0:T(8,128)}, f32[512,2048]{1,0:T(8,128...) custom-call(bf16[512,2048]{1,0:T(8,128)(2,1)} %get-tuple-element.57.context, bf16[512,2048]{1,0:T(8,128)(2,1)} %bitcast.49, ...), custom_call_target="tpu_custom_call" | custom-call | flops 274877906944 | bytes 67108864 | tf_op jit(solution)/shard_map/weight_gradients/pallas_call | solution.py:1835
  1091.2 1.3 slice_bitcast_fusion
  1092.6 3.2 copy.35
  1095.8 2.1 copy.36
  1097.9 1.6 copy-done.6
  1099.5 2.0 copy.37
  1101.5 0.0 copy-done.15
  1101.5 0.8 copy.38
  1102.3 0.8 copy.39
  1103.1 0.8 copy.40
  1103.9 0.8 copy.41
  1104.7 1.1 copy.42
  1105.8 1.1 copy.43
  1106.9 1.1 copy.44
  (28 shorter events, 0.1 us)
Async XLA Ops:
  0.6 11.9 %copy-start.11 = (bf16[172,2048]{1,0:T(8,128)(2,1)S(1)}, bf16[172,2048]{1,0:T(8,128)(2,1)}, u32[]{:S(2)}) copy-start(bf16[172,2048]{1,0:T(8,128)(2,1)} %param.24) | copy-start | bytes 2113540
  0.7 12.0 %copy-start.3 = (bf16[64,2048]{1,0:T(8,128)(2,1)S(1)}, bf16[64,2048]{1,0:T(8,128)(2,1)}, u32[]{:S(2)}) copy-start(bf16[64,2048]{1,0:T(8,128)(2,1)} %w_out.1) | copy-start | bytes 786436
  0.7 12.0 %copy-start.1 = (bf16[64,2048]{1,0:T(8,128)(2,1)S(1)}, bf16[64,2048]{1,0:T(8,128)(2,1)}, u32[]{:S(2)}) copy-start(bf16[64,2048]{1,0:T(8,128)(2,1)} %w_value.1) | copy-start | bytes 786436
  0.7 12.0 %copy-start = (bf16[64,2048]{1,0:T(8,128)(2,1)S(1)}, bf16[64,2048]{1,0:T(8,128)(2,1)}, u32[]{:S(2)}) copy-start(bf16[64,2048]{1,0:T(8,128)(2,1)} %w_key.1) | copy-start | bytes 786436
  0.7 12.0 %copy-start.2 = (bf16[64,2048]{1,0:T(8,128)(2,1)S(1)}, bf16[64,2048]{1,0:T(8,128)(2,1)}, u32[]{:S(2)}) copy-start(bf16[64,2048]{1,0:T(8,128)(2,1)} %w_query.1) | copy-start | bytes 786436
  8.9 360.4 %copy-start.16 = (s32[1,2048]{1,0:T(1,128)}, s32[1,2048]{1,0:T(1,128)S(1)}, u32[]{:S(2)}) copy-start(s32[1,2048]{1,0:T(1,128)S(1)} %get-tuple-element.89.start_ref) | copy-start | bytes 24580
  369.3 1.3 copy-start.4
  370.6 0.6 copy-start.5
  1091.2 4.5 copy-start.7
  1095.8 3.7 copy-start.6
  1099.5 2.0 copy-start.15
  1099.5 2.8 copy-start.14
  1099.5 3.6 copy-start.13
  1101.5 2.4 copy-start.12
  1101.5 3.2 copy-start.10
  1102.3 3.5 copy-start.9
  1104.7 2.2 copy-start.8

commit v7 on v6

--- a/solution.py
+++ b/solution.py
@@ -924,26 +924,20 @@
         sent_parts(job)
         if job + 2 < count:
             send_parts(job + 2)
-        if job == count - 1:
-            for earlier in range(job - 2):
-                send_line(earlier)
         arrived_parts(job)
         to_sibling(job)
         sum_chips(job - 2)
-        if job == count - 1:
-            send_line(job - 2)
+        send_line(job - 2)
         to_chips(job)
+        if job >= 4:
+            relay(job - 4)
         if job == 5:
             memory_gradient()
     sum_chips(6)
     send_line(6)
     query_gradient()
-    relay(0)
-    relay(1)
-    relay(2)
+    relay(4)
     hidden_gradient()
-    relay(3)
-    relay(4)
     relay(5)
     send_gains()
     sum_chips(7)

time: 1120 us -> 1100 us (0.982)
  Pallas kernels: 1080 us -> 1050 us
    pallas_call x1, Pallas kernels: 255 us -> 238 us  [shards(): reduce_call(dp_count, groups, piece, width, here)]
where the time goes in v7:
time: 1100 us; the launch traced here: 1090 us
  Pallas kernels  1050 us (95%)
  local copies, waits for them, and re-layouts  21.3 us (2%)
    pallas_call x1, Pallas kernels, shards(): middle_call(dp_count, groups, piece, width, groups * padded)  402 us
    pallas_call x1, Pallas kernels, shards(): project_call(dp_count, groups, piece, width, here, padded, 1)  357 us
    pallas_call x1, Pallas kernels, shards(): reduce_call(dp_count, groups, piece, width, here)  238 us
    pallas_call x1, Pallas kernels, shards(): attend_backward(high, start, query, key, value, context_heads, grad_conte...  35.5 us
    pallas_call x1, Pallas kernels, shards(): context_heads, lse = attend_forward(low, start, query, key, value)  22.8 us

profile of v7, /device:TPU:0, one launch (start us, length us, event | category | flops | bytes accessed | tf_op | source)
XLA Modules:
  0.0 1086.3 jit_solution(10134624878752824138)
XLA Ops:
  0.7 0.8 fusion.14.gains
  1.5 1.5 fusion.5
  5.6 3.3 compare_select_fusion.7
  8.9 0.0 copy-start.16
  8.9 0.1 slice.22
  9.0 0.5 fusion.15.high_ref
  9.6 0.1 slice.21
  9.6 0.5 and_select_fusion.1.low_ref
  10.2 1.2 pad.18.w_gate
  11.3 1.2 pad.19.w_up
  12.5 0.1 pad.20.w_down
  12.7 356.6 %gather_project.1 = (bf16[512,2048]{1,0:T(8,128)(2,1)S(1)}, f32[8,2048]{1,0:T(8,128)S(1)}, bf16[4,512,512]{2,1,0:T(8,128)(2,1)}, bf16[4,512,512]{2,1,0:T(8,128)(...) custom-call(bf16[512,2048]{1,0:T(8,128)(2,1)} %bitcast.45, ...), custom_call_target="tpu_custom_call" | custom-call | flops 274877906944 | bytes 67108864 | tf_op jit(solution)/shard_map/gather_project/pallas_call | solution.py:1809
  369.3 0.0 copy-done.16
  369.3 0.0 copy-start.4
  369.3 1.3 copy-done.4
  370.6 0.6 copy-done.5
  371.2 22.8 %attend_forward.1 = (bf16[2048,512]{1,0:T(8,128)(2,1)}, f32[4,1,2048]{2,1,0:T(1,128)}) custom-call(s32[8]{0:T(128)} %and_select_fusion.1.low_ref, s32[1,2048]{1,0:T(1,128)} %copy-done.16, bf16[2048,512]{1,0:T(8,128)(2,1)} %bitcast.62, bf16[2048,512]{1,0:T(8,128)(2,1)} %bitcast.58, bf16[2048,512]{1,0:T(8,128)(2,1)} %bitcast.60), custom_call_target="tpu_custom_call" | custom-call | flops 34359738368 | bytes 8388608 | tf_op jit(solution)/shard_map/attend_forward/pallas_call | solution.py:1819
  394.1 401.8 %feed_forward.1 = (bf16[512,2048]{1,0:T(8,128)(2,1)}, f32[8,2048]{1,0:T(8,128)}, bf16[512,2048]{1,0:T(8,128)(2,1)}, f32[512,2048]{1,0:T(8,128)}, bf16[512,2048]{...) custom-call(f32[8,2048]{1,0:T(8,128)} %copy-done.5, ...), custom_call_target="tpu_custom_call" | custom-call | flops 274877906944 | bytes 268435456 | tf_op jit(solution)/shard_map/feed_forward/pallas_call | solution.py:1822
  795.9 35.5 %attend_backward.1 = (bf16[2048,512]{1,0:T(8,128)(2,1)}, bf16[2048,512]{1,0:T(8,128)(2,1)}, bf16[2048,512]{1,0:T(8,128)(2,1)}) custom-call(s32[8]{0:T(128)} %fusion.15.high_ref, s32[1,2048]{1,0:T(1,128)} %copy-done.16, bf16[2048,512]{1,0:T(8,128)(2,1)} %bitcast.63, bf16[2048,512]{1,0:T(8,128)(2,1)} %bitcast.59, bf16[2048,512]{1,0:T(8,128)(2,1)} %bitcast.61, ...), custom_call_target="tpu_custom_call" | custom-call | flops 51539607552 | bytes 16777216 | tf_op jit(solution)/shard_map/attend_backward/pallas_call | solution.py:1827
  831.4 237.7 %weight_gradients.1 = (f32[64,2048]{1,0:T(8,128)}, f32[64,2048]{1,0:T(8,128)}, f32[64,2048]{1,0:T(8,128)}, f32[64,2048]{1,0:T(8,128)}, f32[512,2048]{1,0:T(8,128...) custom-call(bf16[512,2048]{1,0:T(8,128)(2,1)} %get-tuple-element.57.context, bf16[512,2048]{1,0:T(8,128)(2,1)} %bitcast.49, ...), custom_call_target="tpu_custom_call" | custom-call | flops 274877906944 | bytes 67108864 | tf_op jit(solution)/shard_map/weight_gradients/pallas_call | solution.py:1829
  1069.2 1.3 slice_bitcast_fusion
  1070.5 3.2 copy.35
  1073.7 2.1 copy.36
  1075.8 1.6 copy-done.6
  1077.4 2.0 copy.37
  1079.4 0.8 copy.38
  1080.2 0.8 copy.39
  1081.0 0.8 copy.40
  1081.8 0.8 copy.41
  1082.6 1.1 copy.42
  1083.7 1.1 copy.43
  1084.8 1.1 copy.44
  (28 shorter events, 0.1 us)
Async XLA Ops:
  0.6 11.9 %copy-start.11 = (bf16[172,2048]{1,0:T(8,128)(2,1)S(1)}, bf16[172,2048]{1,0:T(8,128)(2,1)}, u32[]{:S(2)}) copy-start(bf16[172,2048]{1,0:T(8,128)(2,1)} %param.24) | copy-start | bytes 2113540
  0.7 12.0 %copy-start.3 = (bf16[64,2048]{1,0:T(8,128)(2,1)S(1)}, bf16[64,2048]{1,0:T(8,128)(2,1)}, u32[]{:S(2)}) copy-start(bf16[64,2048]{1,0:T(8,128)(2,1)} %w_out.1) | copy-start | bytes 786436
  0.7 12.0 %copy-start.1 = (bf16[64,2048]{1,0:T(8,128)(2,1)S(1)}, bf16[64,2048]{1,0:T(8,128)(2,1)}, u32[]{:S(2)}) copy-start(bf16[64,2048]{1,0:T(8,128)(2,1)} %w_value.1) | copy-start | bytes 786436
  0.7 12.0 %copy-start = (bf16[64,2048]{1,0:T(8,128)(2,1)S(1)}, bf16[64,2048]{1,0:T(8,128)(2,1)}, u32[]{:S(2)}) copy-start(bf16[64,2048]{1,0:T(8,128)(2,1)} %w_key.1) | copy-start | bytes 786436
  0.7 12.0 %copy-start.2 = (bf16[64,2048]{1,0:T(8,128)(2,1)S(1)}, bf16[64,2048]{1,0:T(8,128)(2,1)}, u32[]{:S(2)}) copy-start(bf16[64,2048]{1,0:T(8,128)(2,1)} %w_query.1) | copy-start | bytes 786436
  8.9 360.4 %copy-start.16 = (s32[1,2048]{1,0:T(1,128)}, s32[1,2048]{1,0:T(1,128)S(1)}, u32[]{:S(2)}) copy-start(s32[1,2048]{1,0:T(1,128)S(1)} %get-tuple-element.89.start_ref) | copy-start | bytes 24580
  369.3 1.3 copy-start.4
  370.6 0.6 copy-start.5
  1069.1 4.5 copy-start.7
  1073.7 3.7 copy-start.6
  1077.4 2.0 copy-start.15
  1077.4 2.8 copy-start.14
  1077.4 3.6 copy-start.13
  1079.4 2.4 copy-start.12
  1079.4 3.2 copy-start.10
  1080.2 3.5 copy-start.9
  1082.6 2.2 copy-start.8
